TPU v7x, 128 devices: a whole 4x4x4 slice. The times are simulated.
128 devices in a mesh: ctx: 32 (over z, x, core), head: 4 (over y).
Axes of the slice: x: 4, y: 4, z: 4, core: 2. Of those that a mesh axis runs over, the one named last changes fastest.
Arguments:
- queries: bfloat16 [32768, 2048], P('ctx', 'head'), may hold values from -8 to 8
- keys: bfloat16 [32768, 2048], P('ctx', 'head'), may hold values from -8 to 8
- values: bfloat16 [32768, 2048], P('ctx', 'head'), may hold values from -6 to 6
- out_weight: bfloat16 [4096, 2048], P(None, 'head'), may hold values from -0.125 to 0.125
- out_grad: bfloat16 [32768, 4096], P('ctx', 'head'), may hold values from -6 to 6
- long_blocks: int32 [64, 4], replicated, may hold values from 0 to 63, as said below
Outputs:
- layer_out: bfloat16 [32768, 4096], P('ctx', 'head')
- query_grad: bfloat16 [32768, 2048], P('ctx', 'head')
- key_grad: bfloat16 [32768, 2048], P('ctx', 'head')
- value_grad: bfloat16 [32768, 2048], P('ctx', 'head')
Inputs may be any that keep to these rules, and one draw needn't show every extreme that they name: `long_blocks`: row b names 4 different blocks. The 8 blocks named by the rows of the 2 query blocks held by one index of ctx lie on 8 different indices of ctx. A row may name its own block.
All inputs are finite; a program needn't handle non-finite values.
Results may differ from a plain program's by a relative error of at most 0.019.
Values may be sent and summed in bfloat16 or wider, within the bound.
No kernel may reach another device: no remote copies, remote signals or barrier semaphores. Data moves between devices by JAX's collectives and lax.ppermute only.
A program may use at most 192 MiB of HBM per device.

v0:
```python
import math

import jax
import jax.numpy as jnp
from jax import lax
from jax.experimental import pallas as pl
from jax.experimental.pallas import tpu as pltpu
from jax.sharding import PartitionSpec as P

HD = 128
LIN = 3
LISTED = 4
BLOCK = 512
SIDE = 4
CORES = 2
CTX = SIDE * SIDE * CORES
SCALING = 1.0 / math.sqrt(HD)
BF = jnp.bfloat16
F32 = jnp.float32
MIB = 1 << 20
TILE = (BLOCK, HD)


def dot(a, b, ca, cb):
    return lax.dot_general(a, b, (((ca,), (cb,)), ((), ())), preferred_element_type=F32)


def params(mib):
    return pltpu.CompilerParams(vmem_limit_bytes=mib * MIB)


def cost(flops, nbytes):
    return pl.CostEstimate(flops=int(flops), bytes_accessed=int(nbytes), transcendentals=0)


def shift(value, dz=0, dx=0, dc=0):
    pairs = []
    for z in range(SIDE):
        for x in range(SIDE):
            for c in range(CORES):
                to = (((z + dz) % SIDE) * SIDE + (x + dx) % SIDE) * CORES + (c + dc) % CORES
                pairs.append(((z * SIDE + x) * CORES + c, to))
    return lax.ppermute(value, "ctx", pairs)


def along(axis):
    def move(value, step):
        return shift(value, dz=step) if axis == "z" else shift(value, dx=step)

    return move


def swap(value):
    return shift(value, dc=1)


def ring_gather(value, axis):
    move = along(axis)
    half = value.shape[0] // 2
    right = move(value, 1)
    left = move(value, -1)
    far_a = move(right[:half], 1)
    far_b = move(left[half:], -1)
    return [value, right, far_a, far_b, left]


def scan_states(own, backward):
    total = jnp.zeros_like(own)
    step = 1
    while step < CTX:
        if backward:
            pairs = [(i + step, i) for i in range(CTX - step)]
        else:
            pairs = [(i, i + step) for i in range(CTX - step)]
        total = total + lax.ppermute((own + total).astype(BF), "ctx", pairs).astype(F32)
        step *= 2
    return total


def causal_mask():
    s = lax.broadcasted_iota(jnp.int32, (BLOCK, BLOCK), 0)
    u = lax.broadcasted_iota(jnp.int32, (BLOCK, BLOCK), 1)
    return s <= u


def states_kernel(k_ref, v_ref, out_ref):
    out_ref[0, 0] = dot(k_ref[...], v_ref[...], 0, 0)


def adjoint_kernel(q_ref, g_ref, c_ref, out_ref):
    qt = (q_ref[...].astype(F32).T * c_ref[0:1, :]).astype(BF)
    out_ref[0, 0] = dot(qt, g_ref[...], 1, 0)


def tile_spec():
    return pl.BlockSpec(TILE, lambda i, h: (i, h))


def scale_spec():
    return pl.BlockSpec((8, BLOCK), lambda i, h: (0, i))


def state_spec():
    return pl.BlockSpec((1, 1, HD, HD), lambda i, h: (i, h, 0, 0))


def block_states(keys, values):
    return pl.pallas_call(
        states_kernel,
        grid=(2, LIN),
        in_specs=[tile_spec(), tile_spec()],
        out_specs=state_spec(),
        out_shape=jax.ShapeDtypeStruct((2, LIN, HD, HD), F32),
        compiler_params=params(16),
        cost_estimate=cost(1e8, 2 * MIB),
        name="block_states",
    )(keys, values)


def block_adjoints(queries, grads, scale):
    return pl.pallas_call(
        adjoint_kernel,
        grid=(2, LIN),
        in_specs=[tile_spec(), tile_spec(), scale_spec()],
        out_specs=state_spec(),
        out_shape=jax.ShapeDtypeStruct((2, LIN, HD, HD), F32),
        compiler_params=params(16),
        cost_estimate=cost(1e8, 2 * MIB),
        name="block_adjoints",
    )(queries, grads, scale)


def linear_forward_kernel(q_ref, k_ref, v_ref, c_ref, hi_ref, lo_ref, out_ref):
    q, k, v, c = q_ref[...], k_ref[...], v_ref[...], c_ref[0:1, :]
    weights = jnp.where(causal_mask(), dot(k, q, 1, 1) * c, 0.0).astype(BF)
    out = dot(v, weights, 0, 0)
    out = out + c * (dot(hi_ref[0, 0], q, 1, 1) + dot(lo_ref[0, 0], q, 1, 1))
    out_ref[...] = out.T.astype(BF)


def linear_forward(queries, keys, values, scale, hi, lo):
    return pl.pallas_call(
        linear_forward_kernel,
        grid=(2, LIN),
        in_specs=[tile_spec()] * 3 + [scale_spec(), state_spec(), state_spec()],
        out_specs=tile_spec(),
        out_shape=jax.ShapeDtypeStruct(queries.shape, BF),
        compiler_params=params(24),
        cost_estimate=cost(2.4e9, 4 * MIB),
        name="linear_forward",
    )(queries, keys, values, scale, hi, lo)


def linear_backward_kernel(
    q_ref, k_ref, v_ref, g_ref, c_ref, sh_ref, sl_ref, ah_ref, al_ref, base_ref, dq_ref, dk_ref, dv_ref
):
    q, k, v, g, c = q_ref[...], k_ref[...], v_ref[...], g_ref[...], c_ref[0:1, :]
    mask = causal_mask()
    grad_weights = jnp.where(mask, dot(v, g, 1, 1) * c, 0.0).astype(BF)
    dq = dot(k, grad_weights, 0, 0)
    dq = dq + c * (dot(sh_ref[0, 0], g, 1, 1) + dot(sl_ref[0, 0], g, 1, 1))
    dq_ref[...] = dq.T.astype(BF)
    dk = dot(grad_weights, q, 1, 0) + dot(v, ah_ref[0, 0], 1, 1) + dot(v, al_ref[0, 0], 1, 1)
    dk_ref[...] = dk.astype(BF)
    weights = jnp.where(mask, dot(k, q, 1, 1) * c, 0.0).astype(BF)
    dv = dot(weights, g, 1, 0) + dot(k, ah_ref[0, 0], 1, 0) + dot(k, al_ref[0, 0], 1, 0)
    dv_ref[...] = dv.astype(BF)


def linear_backward(queries, keys, values, grads, scale, sh, sl, ah, al, base):
    shape = jax.ShapeDtypeStruct(queries.shape, BF)
    return pl.pallas_call(
        linear_backward_kernel,
        grid=(2, LIN),
        in_specs=[tile_spec()] * 4
        + [scale_spec()]
        + [state_spec()] * 4
        + [pl.BlockSpec(memory_space=pl.ANY)],
        out_specs=[tile_spec()] * 3,
        out_shape=[shape] * 3,
        input_output_aliases={9: 0},
        compiler_params=params(24),
        cost_estimate=cost(5e9, 8 * MIB),
        name="linear_backward",
    )(queries, keys, values, grads, scale, sh, sl, ah, al, base)


def sparse_forward_kernel(table, q_ref, k_ref, v_ref, base_ref, *rest):
    k_pieces, v_pieces = rest[:10], rest[10:20]
    out_ref, p_ref, kf_ref, vf_ref, s_ref, sems = rest[20:]
    step = pl.program_id(0)
    for r in range(LISTED):
        row = step * LISTED + r
        for j in range(10):

            @pl.when(table[row, 0] == j)
            def _():
                pltpu.make_async_copy(
                    k_pieces[j].at[table[row, 1]], kf_ref.at[r], sems.at[0, r]
                ).start()

            @pl.when(table[row, 2] == j)
            def _():
                pltpu.make_async_copy(
                    v_pieces[j].at[table[row, 3]], vf_ref.at[r], sems.at[1, r]
                ).start()

    q = q_ref[...]
    s = jnp.where(causal_mask(), dot(k_ref[...], q, 1, 1) * SCALING, -1e30)
    s_ref[0] = s
    peak = jnp.max(s, axis=0, keepdims=True)
    for r in range(LISTED):
        pltpu.make_async_copy(k_pieces[0].at[0], kf_ref.at[r], sems.at[0, r]).wait()
        bias = jnp.where(table[step * LISTED + r, 4] == 1, 0.0, -1e30).astype(F32)
        s = dot(kf_ref[r], q, 1, 1) * SCALING + bias
        s_ref[r + 1] = s
        peak = jnp.maximum(peak, jnp.max(s, axis=0, keepdims=True))
    total = jnp.zeros((1, BLOCK), F32)
    for r in range(LISTED + 1):
        e = jnp.exp(s_ref[r] - peak)
        s_ref[r] = e
        total = total + jnp.sum(e, axis=0, keepdims=True)
    inverse = 1.0 / total
    out = jnp.zeros((HD, BLOCK), F32)
    for r in range(LISTED + 1):
        p = (s_ref[r] * inverse).astype(BF)
        p_ref[0, r] = p
        if r == 0:
            value = v_ref[...]
        else:
            pltpu.make_async_copy(v_pieces[0].at[0], vf_ref.at[r - 1], sems.at[1, r - 1]).wait()
            value = vf_ref[r - 1]
        out = out + dot(value, p, 0, 0)
    out_ref[...] = out.T.astype(BF)


def sparse_forward(table, queries, keys, values, base, k_pieces, v_pieces):
    column = pl.BlockSpec(TILE, lambda i, t: (i, LIN))
    anywhere = pl.BlockSpec(memory_space=pl.ANY)
    return pl.pallas_call(
        sparse_forward_kernel,
        grid_spec=pltpu.PrefetchScalarGridSpec(
            num_scalar_prefetch=1,
            grid=(2,),
            in_specs=[column] * 3 + [anywhere] * 21,
            out_specs=[
                column,
                pl.BlockSpec((1, LISTED + 1, BLOCK, BLOCK), lambda i, t: (i, 0, 0, 0)),
                pl.BlockSpec((LISTED, BLOCK, HD), lambda i, t: (i, 0, 0)),
                pl.BlockSpec((LISTED, BLOCK, HD), lambda i, t: (i, 0, 0)),
            ],
            scratch_shapes=[
                pltpu.VMEM((LISTED + 1, BLOCK, BLOCK), F32),
                pltpu.SemaphoreType.DMA((2, LISTED)),
            ],
        ),
        out_shape=[
            jax.ShapeDtypeStruct(queries.shape, BF),
            jax.ShapeDtypeStruct((2, LISTED + 1, BLOCK, BLOCK), BF),
            jax.ShapeDtypeStruct((2 * LISTED, BLOCK, HD), BF),
            jax.ShapeDtypeStruct((2 * LISTED, BLOCK, HD), BF),
        ],
        input_output_aliases={4: 0},
        compiler_params=params(32),
        cost_estimate=cost(4e9, 12 * MIB),
        name="sparse_forward",
    )(table, queries, keys, values, base, *k_pieces, *v_pieces)


def sparse_backward_kernel(
    q_ref, k_ref, v_ref, g_ref, o_ref, p_ref, kf_ref, vf_ref, dq_ref, dk_ref, dv_ref, pk_ref, pv_ref
):
    q, g = q_ref[...], g_ref[...]
    row_dot = jnp.sum((g.astype(F32) * o_ref[...].astype(F32)).T, axis=0, keepdims=True)
    dq = jnp.zeros((HD, BLOCK), F32)
    for r in range(LISTED + 1):
        p = p_ref[0, r]
        key = k_ref[...] if r == 0 else kf_ref[r - 1]
        value = v_ref[...] if r == 0 else vf_ref[r - 1]
        dp = dot(value, g, 1, 1)
        ds = (p.astype(F32) * (dp - row_dot)).astype(BF)
        dq = dq + dot(key, ds, 0, 0)
        dk = dot(ds, q, 1, 0) * SCALING
        dv = dot(p, g, 1, 0)
        if r == 0:
            dk_ref[...] = dk
            dv_ref[...] = dv
        else:
            pk_ref[r - 1] = dk.astype(BF)
            pv_ref[r - 1] = dv.astype(BF)
    dq_ref[...] = (dq * SCALING).T.astype(BF)


def sparse_backward(queries, keys, values, grads, outs, probs, far_k, far_v):
    column = pl.BlockSpec(TILE, lambda i: (i, LIN))
    four = pl.BlockSpec((LISTED, BLOCK, HD), lambda i: (i, 0, 0))
    rows = pl.BlockSpec(TILE, lambda i: (i, 0))
    return pl.pallas_call(
        sparse_backward_kernel,
        grid=(2,),
        in_specs=[column] * 5
        + [pl.BlockSpec((1, LISTED + 1, BLOCK, BLOCK), lambda i: (i, 0, 0, 0)), four, four],
        out_specs=[column, rows, rows, four, four],
        out_shape=[
            jax.ShapeDtypeStruct(queries.shape, BF),
            jax.ShapeDtypeStruct((2 * BLOCK, HD), F32),
            jax.ShapeDtypeStruct((2 * BLOCK, HD), F32),
            jax.ShapeDtypeStruct((2 * LISTED, BLOCK, HD), BF),
            jax.ShapeDtypeStruct((2 * LISTED, BLOCK, HD), BF),
        ],
        compiler_params=params(32),
        cost_estimate=cost(8e9, 12 * MIB),
        name="sparse_backward",
    )(queries, keys, values, grads, outs, probs, far_k, far_v)


def placed(table, stream, j, own_ref, peer_ref):
    a, b = table[2 * stream, j], table[2 * stream + 1, j]
    first = own_ref[jnp.maximum(a, 0)].astype(F32) * jnp.where(a >= 0, 1.0, 0.0).astype(F32)
    second = peer_ref[jnp.maximum(b, 0)].astype(F32) * jnp.where(b >= 0, 1.0, 0.0).astype(F32)
    return first + second


def back_call(kernel, table, operands, shapes, name):
    vm = pl.BlockSpec(memory_space=pltpu.VMEM)
    nbytes = sum(math.prod(o.shape) * 2 for o in operands) + sum(math.prod(s) * 2 for s in shapes)
    return pl.pallas_call(
        kernel,
        in_specs=[pl.BlockSpec(memory_space=pltpu.SMEM)] + [vm] * len(operands),
        out_specs=[vm] * len(shapes),
        out_shape=[jax.ShapeDtypeStruct(s, BF) for s in shapes],
        compiler_params=params(32),
        cost_estimate=cost(1e7, nbytes),
        name=name,
    )(table, *operands)


def far_kernel(table, ok, pk, ov, pv, ka, kb, va, vb):
    for stream, own, peer, first, second in ((0, ok, pk, ka, kb), (1, ov, pv, va, vb)):

        @pl.loop(0, 4)
        def _(j):
            first[j] = placed(table, stream, 16 + j, own, peer).astype(BF)
            second[j] = placed(table, stream, 20 + j, own, peer).astype(BF)


def near_kernel(table, ok, pk, ov, pv, rka, rkb, rva, rvb, k1, k3, v1, v3):
    for stream, own, peer, ra, rb, right, left in (
        (0, ok, pk, rka, rkb, k1, k3),
        (1, ov, pv, rva, rvb, v1, v3),
    ):

        @pl.loop(0, 4)
        def _(j):
            right[j] = (placed(table, stream, 8 + j, own, peer) + ra[j].astype(F32)).astype(BF)
            right[j + 4] = placed(table, stream, 12 + j, own, peer).astype(BF)
            left[j] = placed(table, stream, 24 + j, own, peer).astype(BF)
            left[j + 4] = (placed(table, stream, 28 + j, own, peer) + rb[j].astype(F32)).astype(BF)


def turn_kernel(table, ok, pk, ov, pv, rka, rkb, rva, rvb, *outs):
    for stream, own, peer, ra, rb in ((0, ok, pk, rka, rkb), (1, ov, pv, rva, rvb)):
        home, right, far_a, far_b, left = outs[5 * stream : 5 * stream + 5]
        targets = [
            (home, 0), (home, 1), (right, 0), (right, 1), (far_a, 0), (far_b, 0), (left, 0), (left, 1)
        ]
        for j, (ref, w) in enumerate(targets):
            total = placed(table, stream, j, own, peer) + ra[j].astype(F32) + rb[j].astype(F32)
            ref[w] = total.astype(BF)


def last_kernel(kr, kl, vr, vl, rka, rkb, rva, rvb, okr, okl, ovr, ovl):
    for right, left, ra, rb, o_right, o_left in (
        (kr, kl, rka, rkb, okr, okl),
        (vr, vl, rva, rvb, ovr, ovl),
    ):
        o_right[0] = (right[0].astype(F32) + ra[0].astype(F32)).astype(BF)
        o_right[1] = right[1]
        o_left[0] = left[0]
        o_left[1] = (left[1].astype(F32) + rb[0].astype(F32)).astype(BF)


def last_sums(operands):
    vm = pl.BlockSpec(memory_space=pltpu.VMEM)
    return pl.pallas_call(
        last_kernel,
        in_specs=[vm] * 8,
        out_specs=[vm] * 4,
        out_shape=[jax.ShapeDtypeStruct((2, BLOCK, HD), BF)] * 4,
        compiler_params=params(16),
        cost_estimate=cost(1e6, 2 * MIB),
        name="last_sums",
    )(*operands)


def finish_kernel(dk, dv, k0, ka, kb, v0, va, vb, kg_in, vg_in, kg, vg):
    kg[...] = (dk[...] + k0[0].astype(F32) + ka[0].astype(F32) + kb[0].astype(F32)).astype(BF)
    vg[...] = (dv[...] + v0[0].astype(F32) + va[0].astype(F32) + vb[0].astype(F32)).astype(BF)


def finish(dk, dv, pieces, key_grad, value_grad):
    rows = pl.BlockSpec(TILE, lambda i: (i, 0))
    piece = pl.BlockSpec((1, BLOCK, HD), lambda i: (i, 0, 0))
    column = pl.BlockSpec(TILE, lambda i: (i, LIN))
    anywhere = pl.BlockSpec(memory_space=pl.ANY)
    shape = jax.ShapeDtypeStruct(key_grad.shape, BF)
    return pl.pallas_call(
        finish_kernel,
        grid=(2,),
        in_specs=[rows, rows] + [piece] * 6 + [anywhere] * 2,
        out_specs=[column, column],
        out_shape=[shape, shape],
        input_output_aliases={8: 0, 9: 1},
        compiler_params=params(16),
        cost_estimate=cost(1e6, 3 * MIB),
        name="finish",
    )(dk, dv, *pieces, key_grad, value_grad)


def return_sums(pair_k, pair_v, table):
    peer_k, peer_v = swap(pair_k), swap(pair_v)
    base = [pair_k, peer_k, pair_v, peer_v]
    zmove, xmove = along("z"), along("x")
    four, eight = (4, BLOCK, HD), (8, BLOCK, HD)
    ka, kb, va, vb = back_call(far_kernel, table, base, [four] * 4, "back_far")
    got = [zmove(ka, 1), zmove(kb, -1), xmove(va, 1), xmove(vb, -1)]
    k1, k3, v1, v3 = back_call(near_kernel, table, base + got, [eight] * 4, "back_near")
    got = [zmove(k1, 1), zmove(k3, -1), xmove(v1, 1), xmove(v3, -1)]
    two, one = (2, BLOCK, HD), (1, BLOCK, HD)
    outs = back_call(turn_kernel, table, base + got, [two, two, one, one, two] * 2, "back_turn")
    k0, k1, ka, kb, k3, v0, v1, va, vb, v3 = outs
    got = [xmove(ka, 1), xmove(kb, -1), zmove(va, 1), zmove(vb, -1)]
    k1, k3, v1, v3 = last_sums([k1, k3, v1, v3] + got)
    return [k0, xmove(k1, 1), xmove(k3, -1), v0, zmove(v1, 1), zmove(v3, -1)]


def where_is(blocks, place):
    owner, within = blocks // 2, blocks % 2
    pz = (place // (SIDE * CORES) - owner // (SIDE * CORES)) % SIDE
    px = (place // CORES % SIDE - owner // CORES % SIDE) % SIDE
    return pz, px, owner % CORES, within


def piece_of(outer, inner, within, peer):
    second = (outer == 2) & (inner >= 2)
    piece = jnp.where(outer < 2, outer, jnp.where(outer == 3, 4, jnp.where(second, 3, 2)))
    index = inner * 2 + within - jnp.where(second, 4, 0)
    return piece + 5 * peer, index


def fetch_table(lists, place):
    flat = lists.reshape(-1)
    pz, px, core, within = where_is(flat, place)
    peer = (core != place % CORES).astype(jnp.int32)
    k_piece, k_index = piece_of(pz, px, within, peer)
    v_piece, v_index = piece_of(px, pz, within, peer)
    mine = place * 2 + jnp.arange(2 * LISTED, dtype=jnp.int32) // LISTED
    usable = (flat != mine).astype(jnp.int32)
    return jnp.stack([k_piece, k_index, v_piece, v_index, usable], axis=1).astype(jnp.int32)


def back_table(lists, peer_lists, place):
    slots = jnp.arange(2 * LISTED, dtype=jnp.int32)[:, None]
    spots = jnp.arange(32, dtype=jnp.int32)[None, :]
    rows = []
    for outer_z in (True, False):
        for some in (lists, peer_lists):
            pz, px, core, within = where_is(some.reshape(-1), place)
            pz, px = (-pz) % SIDE, (-px) % SIDE
            outer, inner = (pz, px) if outer_z else (px, pz)
            target = jnp.where(core == place % CORES, (outer * SIDE + inner) * 2 + within, -1)
            rows.append(jnp.max(jnp.where(target[:, None] == spots, slots, -1), axis=0))
    return jnp.stack(rows).astype(jnp.int32)


def split(value):
    high = value.astype(BF)
    return high, (value - high.astype(F32)).astype(BF)


def local(queries, keys, values, out_weight, out_grad, long_blocks):
    place = lax.axis_index("ctx")
    row_count = queries.shape[0]
    positions = place * row_count + jnp.arange(row_count, dtype=jnp.int32)
    scale = 1.0 / (math.sqrt(HD) * jnp.sqrt((positions + 1).astype(F32)))
    scale = jnp.broadcast_to(scale[None, :], (8, row_count))
    lists = lax.dynamic_slice_in_dim(long_blocks, place * 2, 2, 0)
    peer_lists = lax.dynamic_slice_in_dim(long_blocks, (place ^ 1) * 2, 2, 0)
    fetch = fetch_table(lists, place)
    back = back_table(lists, peer_lists, place)

    grad_all = lax.all_gather(out_grad, "head", axis=1, tiled=True)

    own_k = keys[:, LIN * HD :].reshape(2, BLOCK, HD)
    own_v = values[:, LIN * HD :].reshape(2, BLOCK, HD)
    line_k = ring_gather(own_k, "x")
    line_v = ring_gather(own_v, "z")
    k_pieces = ring_gather(jnp.concatenate(line_k, axis=0), "z")
    v_pieces = ring_gather(jnp.concatenate(line_v, axis=0), "x")
    k_pieces = k_pieces + [swap(p) for p in k_pieces]
    v_pieces = v_pieces + [swap(p) for p in v_pieces]

    states = block_states(keys, values)
    before = scan_states(states[0] + states[1], False)
    before = jnp.stack([before, before + states[0]])
    flip_hi, flip_lo = split(jnp.swapaxes(before, 2, 3))
    attention = linear_forward(queries, keys, values, scale, flip_hi, flip_lo)
    attention, probs, far_k, far_v = sparse_forward(
        fetch, queries, keys, values, attention, k_pieces, v_pieces
    )
    partial_out = dot(attention, out_weight, 1, 1).astype(BF)
    layer_out = lax.psum_scatter(partial_out, "head", scatter_dimension=1, tiled=True)

    attn_grad = dot(grad_all, out_weight, 1, 0).astype(BF)
    query_grad, own_dk, own_dv, pair_k, pair_v = sparse_backward(
        queries, keys, values, attn_grad, attention, probs, far_k, far_v
    )
    pieces = return_sums(pair_k, pair_v, back)

    adjoints = block_adjoints(queries, attn_grad, scale)
    after = scan_states(adjoints[0] + adjoints[1], True)
    after = jnp.stack([after + adjoints[1], after])
    query_grad, key_grad, value_grad = linear_backward(
        queries, keys, values, attn_grad, scale, *split(before), *split(after), query_grad
    )
    key_grad, value_grad = finish(own_dk, own_dv, pieces, key_grad, value_grad)
    return layer_out, query_grad, key_grad, value_grad


def solution(mesh):
    return jax.shard_map(
        local,
        mesh=mesh,
        in_specs=(
            P("ctx", "head"),
            P("ctx", "head"),
            P("ctx", "head"),
            P(None, "head"),
            P("ctx", "head"),
            P(),
        ),
        out_specs=(P("ctx", "head"), P("ctx", "head"), P("ctx", "head"), P("ctx", "head")),
        check_vma=False,
    )
```

profile of v0, /device:TPU:1, one launch (start us, length us, event | category | flops | bytes accessed | tf_op | source)
XLA Modules:
  0.0 273.7 jit_solution(16308423916943681640)
XLA Ops:
  21.6 3.3 %collective-permute-start = (bf16[3,128,128]{2,1,0:T(8,128)(2,1)S(1)}, bf16[3,128,128]{2,1,0:T(8,128)(2,1)S(1)}, u32[]{:S(2)}, u32[]{:S(2)}) collective-permute-start(bf16[3,128,128]{2,1,0:T(8,128)(2,1)S(1)} %get-tuple-element.86), channel_id=1, source_target_pairs={{0,4},{4,8},{8,12},{12,16},{16,20},{20,24},{24,28},{28,32},{32,36}... | collective-permute-start | bytes 294920 | tf_op jit(solution)/shard_map/ppermute | solution.py:75
  26.6 3.1 %collective-permute-start.1 = (bf16[3,128,128]{2,1,0:T(8,128)(2,1)S(1)}, bf16[3,128,128]{2,1,0:T(8,128)(2,1)S(1)}, u32[]{:S(2)}, u32[]{:S(2)}) collective-permute-start(bf16[3,128,128]{2,1,0:T(8,128)(2,1)S(1)} %fusion.2), channel_id=1, source_target_pairs={{0,8},{4,12},{8,16},{12,20},{16,24},{20,28},{24,32},{28,36},{32,40... | collective-permute-start | bytes 294920 | tf_op jit(solution)/shard_map/ppermute | solution.py:75
  32.7 2.7 collective-permute-start.21
  38.9 2.7 collective-permute-start.11
  43.7 3.5 %collective-permute-start.2 = (bf16[3,128,128]{2,1,0:T(8,128)(2,1)S(1)}, bf16[3,128,128]{2,1,0:T(8,128)(2,1)S(1)}, u32[]{:S(2)}, u32[]{:S(2)}) collective-permute-start(bf16[3,128,128]{2,1,0:T(8,128)(2,1)S(1)} %add_convert_fusion.5), channel_id=1, source_target_pairs={{0,16},{4,20},{8,24},{12,28},{16,32},{20,36},{24,40},{28,44},{32,4... | collective-permute-start | bytes 294920 | tf_op jit(solution)/shard_map/ppermute | solution.py:75
  48.4 15.9 %collective-permute-done.2 = bf16[3,128,128]{2,1,0:T(8,128)(2,1)S(1)} collective-permute-done((bf16[3,128,128]{2,1,0:T(8,128)(2,1)S(1)}, bf16[3,128,128]{2,1,0:T(8,128)(2,1)S(1)}, u32[]{:S(2)}, u32[]{:S(2)}) %collective-permute-start.2) | collective-permute-done | bytes 98336 | tf_op jit(solution)/shard_map/ppermute | solution.py:75
  64.4 3.9 %collective-permute-start.3 = (bf16[3,128,128]{2,1,0:T(8,128)(2,1)S(1)}, bf16[3,128,128]{2,1,0:T(8,128)(2,1)S(1)}, u32[]{:S(2)}, u32[]{:S(2)}) collective-permute-start(bf16[3,128,128]{2,1,0:T(8,128)(2,1)S(1)} %add_convert_fusion.4), channel_id=1, source_target_pairs={{0,32},{4,36},{8,40},{12,44},{16,48},{20,52},{24,56},{28,60},{32,6... | collective-permute-start | bytes 294920 | tf_op jit(solution)/shard_map/ppermute | solution.py:75
  70.9 6.9 %collective-permute-start.13 = (bf16[8,512,128]{2,1,0:T(8,128)(2,1)}, bf16[8,512,128]{2,1,0:T(8,128)(2,1)}, u32[]{:S(2)}, u32[]{:S(2)}) collective-permute-start(bf16[8,512,128]{2,1,0:T(8,128)(2,1)} %constant_dynamic-update-slice_fusion.rest_0_), channel_id=1, source_target_pairs={{0,4},{4,0},{8,12},{12,8},{16,20},{20,16},{24,28},{28,24},{32,36},... | collective-permute-start | bytes 3145736 | tf_op jit(solution)/shard_map/ppermute | solution.py:43
  78.0 4.1 %collective-permute-start.4 = (bf16[3,128,128]{2,1,0:T(8,128)(2,1)S(1)}, bf16[3,128,128]{2,1,0:T(8,128)(2,1)S(1)}, u32[]{:S(2)}, u32[]{:S(2)}) collective-permute-start(bf16[3,128,128]{2,1,0:T(8,128)(2,1)S(1)} %add_convert_fusion.3), channel_id=1, source_target_pairs={{0,64},{4,68},{8,72},{12,76},{16,80},{20,84},{24,88},{28,92},{32,9... | collective-permute-start | bytes 294920 | tf_op jit(solution)/shard_map/ppermute | solution.py:75
  84.7 2.9 %collective-permute-start.12 = (bf16[4,512,128]{2,1,0:T(8,128)(2,1)}, bf16[4,512,128]{2,1,0:T(8,128)(2,1)}, u32[]{:S(2)}, u32[]{:S(2)}) collective-permute-start(bf16[4,512,128]{2,1,0:T(8,128)(2,1)} %slice.63), channel_id=1, source_target_pairs={{0,96},{4,100},{8,104},{12,108},{16,112},{20,116},{24,120},{28,124... | collective-permute-start | bytes 1572872 | tf_op jit(solution)/shard_map/ppermute | solution.py:43
  92.0 2.6 collective-permute-start.25
  100.9 3.1 %collective-permute-done.23.rest_12_ = bf16[4,512,128]{2,1,0:T(8,128)(2,1)} collective-permute-done((bf16[4,512,128]{2,1,0:T(8,128)(2,1)}, bf16[4,512,128]{2,1,0:T(8,128)(2,1)}, u32[]{:S(2)}, u32[]{:S(2)}) %collective-permute-start.23) | collective-permute-done | bytes 524320 | tf_op jit(solution)/shard_map/ppermute | solution.py:43
  114.5 3.8 %linear_forward.1.base_ref = bf16[1024,512]{1,0:T(8,128)(2,1)S(1)} custom-call(bf16[1024,512]{1,0:T(8,128)(2,1)S(1)} %copy-done.7, bf16[1024,512]{1,0:T(8,128)(2,1)S(1)} %copy-done.1, bf16[1024,512]{1,0:T(8,128)(2,1)S(1)} %copy-done.4, f32[8,1024]{1,0:T(8,128)S(1)} %broadcast_in_dim.60.c_ref, bf16[2,3,128,128]{3,2,1,0:T(8,128)(2,1)S(1)} %copy.30.hi_ref, ...), custom_call_target="tpu_custom_call" | custom-call | flops 2400000000 | bytes 4194304 | tf_op jit(solution)/shard_map/linear_forward/pallas_call | solution.py:142
  118.4 11.4 %sparse_forward.1 = (bf16[1024,512]{1,0:T(8,128)(2,1)S(1)}, bf16[2,5,512,512]{3,2,1,0:T(8,128)(2,1)}, bf16[8,512,128]{2,1,0:T(8,128)(2,1)S(1)}, bf16[8,512,128]{2,1,0:T(8,128)(2,1)S(1)}) custom-call(s32[8,5]{1,0:T(8,128)S(1)} %stack.41.table, bf16[1024,512]{1,0:T(8,128)(2,1)S(1)} %copy-done.7, ...), custom_call_target="tpu_custom_call", output_to_operand_aliasing={{0}: (4, {})} | custom-call | flops 4000000000 | bytes 12582912 | tf_op jit(solution)/shard_map/sparse_forward/pallas_call | solution.py:240
  131.7 9.2 %convolution_convert_fusion = bf16[1024,4096]{1,0:T(8,128)(2,1)} fusion(bf16[1024,512]{1,0:T(8,128)(2,1)S(1)} %get-tuple-element.40.o_ref, bf16[4096,512]{1,0:T(8,128)(2,1)} %param.9), kind=kOutput, calls=%fused_computation | convolution fusion | flops 4299161600 | bytes 13631488 | tf_op jit(solution)/shard_map/dot_general | solution.py:25
  142.6 9.2 %convolution_convert_fusion.1.g_ref = bf16[1024,512]{1,0:T(8,128)(2,1)S(1)} fusion(bf16[1024,4096]{1,0:T(8,128)(2,1)} %all-gather.2.cloned.1.call-done, bf16[4096,512]{1,0:T(8,128)(2,1)} %param.9), kind=kOutput, calls=%fused_computation.1 | convolution fusion | flops 4295491584 | bytes 13631488 | tf_op jit(solution)/shard_map/dot_general | solution.py:25
  151.9 2.8 %copy-done.30 = bf16[2,5,512,512]{3,2,1,0:T(8,128)(2,1)S(1)} copy-done((bf16[2,5,512,512]{3,2,1,0:T(8,128)(2,1)S(1)}, bf16[2,5,512,512]{3,2,1,0:T(8,128)(2,1)}, u32[]{:S(2)}) %copy-start.30) | copy-done | bytes 5242904
  154.7 7.0 %sparse_backward.1 = (bf16[1024,512]{1,0:T(8,128)(2,1)}, f32[1024,128]{1,0:T(8,128)S(1)}, f32[1024,128]{1,0:T(8,128)S(1)}, bf16[8,512,128]{2,1,0:T(8,128)(2,1)S(1)}, bf16[8,512,128]{2,1,0:T(8,128)(2,1)S(1)}) custom-call(bf16[1024,512]{1,0:T(8,128)(2,1)S(1)} %copy-done.8, bf16[1024,512]{1,0:T(8,128)(2,1)S(1)} %copy-done.1, bf16[1024,512]{1,0:T(8,128)(2,1)S(1)} %copy-done.5, ...), custom_call_target="tpu_custom_call" | custom-call | flops 8000000000 | bytes 12582912 | tf_op jit(solution)/shard_map/sparse_backward/pallas_call | solution.py:298
  171.8 2.7 collective-permute-start.39
  174.4 3.8 %collective-permute-start.41 = (bf16[4,512,128]{2,1,0:T(8,128)(2,1)S(1)}, bf16[4,512,128]{2,1,0:T(8,128)(2,1)S(1)}, u32[]{:S(2)}, u32[]{:S(2)}) collective-permute-start(bf16[4,512,128]{2,1,0:T(8,128)(2,1)S(1)} %get-tuple-element.53), channel_id=1, source_target_pairs={{0,24},{4,28},{8,0},{12,4},{16,8},{20,12},{24,16},{28,20},{32,56},... | collective-permute-start | bytes 1572872 | tf_op jit(solution)/shard_map/ppermute | solution.py:43
  178.2 3.0 %collective-permute-start.31 = (bf16[3,128,128]{2,1,0:T(8,128)(2,1)S(1)}, bf16[3,128,128]{2,1,0:T(8,128)(2,1)S(1)}, u32[]{:S(2)}, u32[]{:S(2)}) collective-permute-start(bf16[3,128,128]{2,1,0:T(8,128)(2,1)S(1)} %get-tuple-element.84), channel_id=1, source_target_pairs={{4,0},{8,4},{12,8},{16,12},{20,16},{24,20},{28,24},{32,28},{36,32}... | collective-permute-start | bytes 294920 | tf_op jit(solution)/shard_map/ppermute | solution.py:75
  181.3 8.4 %collective-permute-done.31 = bf16[3,128,128]{2,1,0:T(8,128)(2,1)S(1)} collective-permute-done((bf16[3,128,128]{2,1,0:T(8,128)(2,1)S(1)}, bf16[3,128,128]{2,1,0:T(8,128)(2,1)S(1)}, u32[]{:S(2)}, u32[]{:S(2)}) %collective-permute-start.31) | collective-permute-done | bytes 98336 | tf_op jit(solution)/shard_map/ppermute | solution.py:75
  191.2 3.1 %back_near.1 = (bf16[8,512,128]{2,1,0:T(8,128)(2,1)S(1)}, bf16[8,512,128]{2,1,0:T(8,128)(2,1)S(1)}, bf16[8,512,128]{2,1,0:T(8,128)(2,1)S(1)}, bf16[8,512,128]{2,1,0:T(8,128)(2,1)S(1)}) custom-call(s32[4,32]{1,0:T(4,128)S(1)} %pad_add_fusion.table, bf16[8,512,128]{2,1,0:T(8,128)(2,1)S(1)} %get-tuple-element.48.ok, ...), custom_call_target="tpu_custom_call" | custom-call | flops 10000000 | bytes 10485760 | tf_op jit(solution)/shard_map/back_near/pallas_call | solution.py:327
  194.3 4.9 %collective-permute-start.42 = (bf16[8,512,128]{2,1,0:T(8,128)(2,1)S(1)}, bf16[8,512,128]{2,1,0:T(8,128)(2,1)S(1)}, u32[]{:S(2)}, u32[]{:S(2)}) collective-permute-start(bf16[8,512,128]{2,1,0:T(8,128)(2,1)S(1)} %get-tuple-element.54), channel_id=1, source_target_pairs={{0,32},{4,36},{8,40},{12,44},{16,48},{20,52},{24,56},{28,60},{32,6... | collective-permute-start | bytes 3145736 | tf_op jit(solution)/shard_map/ppermute | solution.py:43
  204.4 24.4 %collective-permute-done.33 = bf16[3,128,128]{2,1,0:T(8,128)(2,1)S(1)} collective-permute-done((bf16[3,128,128]{2,1,0:T(8,128)(2,1)S(1)}, bf16[3,128,128]{2,1,0:T(8,128)(2,1)S(1)}, u32[]{:S(2)}, u32[]{:S(2)}) %collective-permute-start.33) | collective-permute-done | bytes 98336 | tf_op jit(solution)/shard_map/ppermute | solution.py:75
  230.2 4.9 %collective-permute-done.34 = bf16[3,128,128]{2,1,0:T(8,128)(2,1)S(1)} collective-permute-done((bf16[3,128,128]{2,1,0:T(8,128)(2,1)S(1)}, bf16[3,128,128]{2,1,0:T(8,128)(2,1)S(1)}, u32[]{:S(2)}, u32[]{:S(2)}) %collective-permute-start.34) | collective-permute-done | bytes 98336 | tf_op jit(solution)/shard_map/ppermute | solution.py:75
  236.5 5.5 %collective-permute-done.35 = bf16[3,128,128]{2,1,0:T(8,128)(2,1)S(1)} collective-permute-done((bf16[3,128,128]{2,1,0:T(8,128)(2,1)S(1)}, bf16[3,128,128]{2,1,0:T(8,128)(2,1)S(1)}, u32[]{:S(2)}, u32[]{:S(2)}) %collective-permute-start.35) | collective-permute-done | bytes 98336 | tf_op jit(solution)/shard_map/ppermute | solution.py:75
  242.1 2.7 back_turn.1
  247.6 2.7 collective-permute-start.49
  253.0 2.7 collective-permute-start.51
  255.7 2.7 collective-permute-start.53
  258.4 7.5 %linear_backward.1 = (bf16[1024,512]{1,0:T(8,128)(2,1)}, bf16[1024,512]{1,0:T(8,128)(2,1)}, bf16[1024,512]{1,0:T(8,128)(2,1)}) custom-call(bf16[1024,512]{1,0:T(8,128)(2,1)S(1)} %copy-done.10, bf16[1024,512]{1,0:T(8,128)(2,1)S(1)} %copy-done.2, bf16[1024,512]{1,0:T(8,128)(2,1)S(1)} %copy-done.6, ...), custom_call_target="tpu_custom_call", output_to_operand_aliasing={{0}: (9, {})} | custom-call | flops 5000000000 | bytes 8388608 | tf_op jit(solution)/shard_map/linear_backward/pallas_call | solution.py:172
  (250 shorter events, 81.6 us)
Async XLA Ops:
  7.2 135.4 %all-gather.2.cloned.1.call-start = ((), (), s32[]{:S(2)}) async-start(), calls=%async_computation.2 | async-start | bytes 10485760 | tf_op jit(solution)/shard_map/all_gather | solution.py:492
  7.9 259.0 %reduce-scatter.2.cloned.1.call-start = ((), (), s32[]{:S(2)}) async-start(), calls=%async_computation.1 | async-start | bytes 10485760 | tf_op jit(solution)/shard_map/reduce_scatter | solution.py:512
  8.9 20.8 %collective-permute-start.5 = (bf16[2,512,128]{2,1,0:T(8,128)(2,1)S(1)}, bf16[2,512,128]{2,1,0:T(8,128)(2,1)S(1)}, u32[]{:S(2)}, u32[]{:S(2)}) collective-permute-start(bf16[2,512,128]{2,1,0:T(8,128)(2,1)S(1)} %bitcast.52), channel_id=1, source_target_pairs={{0,8},{4,12},{8,16},{12,20},{16,24},{20,28},{24,0},{28,4},{32,40},... | collective-permute-start | bytes 786440 | tf_op jit(solution)/shard_map/ppermute | solution.py:43
  11.0 19.7 %collective-permute-start.7 = (bf16[2,512,128]{2,1,0:T(8,128)(2,1)S(1)}, bf16[2,512,128]{2,1,0:T(8,128)(2,1)S(1)}, u32[]{:S(2)}, u32[]{:S(2)}) collective-permute-start(bf16[2,512,128]{2,1,0:T(8,128)(2,1)S(1)} %bitcast.53), channel_id=1, source_target_pairs={{0,24},{4,28},{8,0},{12,4},{16,8},{20,12},{24,16},{28,20},{32,56},... | collective-permute-start | bytes 786440 | tf_op jit(solution)/shard_map/ppermute | solution.py:43
  13.3 19.2 %collective-permute-start.18 = (bf16[2,512,128]{2,1,0:T(8,128)(2,1)S(1)}, bf16[2,512,128]{2,1,0:T(8,128)(2,1)S(1)}, u32[]{:S(2)}, u32[]{:S(2)}) collective-permute-start(bf16[2,512,128]{2,1,0:T(8,128)(2,1)S(1)} %bitcast.49), channel_id=1, source_target_pairs={{0,32},{4,36},{8,40},{12,44},{16,48},{20,52},{24,56},{28,60},{32,6... | collective-permute-start | bytes 786440 | tf_op jit(solution)/shard_map/ppermute | solution.py:43
  15.2 17.5 %collective-permute-start.20 = (bf16[2,512,128]{2,1,0:T(8,128)(2,1)S(1)}, bf16[2,512,128]{2,1,0:T(8,128)(2,1)S(1)}, u32[]{:S(2)}, u32[]{:S(2)}) collective-permute-start(bf16[2,512,128]{2,1,0:T(8,128)(2,1)S(1)} %bitcast.50), channel_id=1, source_target_pairs={{0,96},{4,100},{8,104},{12,108},{16,112},{20,116},{24,120},{28,124... | collective-permute-start | bytes 786440 | tf_op jit(solution)/shard_map/ppermute | solution.py:43
  26.6 17.1 %collective-permute-start.1 = (bf16[3,128,128]{2,1,0:T(8,128)(2,1)S(1)}, bf16[3,128,128]{2,1,0:T(8,128)(2,1)S(1)}, u32[]{:S(2)}, u32[]{:S(2)}) collective-permute-start(bf16[3,128,128]{2,1,0:T(8,128)(2,1)S(1)} %fusion.2), channel_id=1, source_target_pairs={{0,8},{4,12},{8,16},{12,20},{16,24},{20,28},{24,32},{28,36},{32,40... | collective-permute-start | bytes 294920 | tf_op jit(solution)/shard_map/ppermute | solution.py:75
  38.9 39.0 %collective-permute-start.9 = (bf16[8,512,128]{2,1,0:T(8,128)(2,1)}, bf16[8,512,128]{2,1,0:T(8,128)(2,1)S(1)}, u32[]{:S(2)}, u32[]{:S(2)}) collective-permute-start(bf16[8,512,128]{2,1,0:T(8,128)(2,1)} %constant_dynamic-update-slice_fusion.rest_0_), channel_id=1, source_target_pairs={{0,32},{4,36},{8,40},{12,44},{16,48},{20,52},{24,56},{28,60},{32,6... | collective-permute-start | bytes 3145736 | tf_op jit(solution)/shard_map/ppermute | solution.py:43
  38.9 44.0 %collective-permute-start.11 = (bf16[8,512,128]{2,1,0:T(8,128)(2,1)}, bf16[8,512,128]{2,1,0:T(8,128)(2,1)S(1)}, u32[]{:S(2)}, u32[]{:S(2)}) collective-permute-start(bf16[8,512,128]{2,1,0:T(8,128)(2,1)} %constant_dynamic-update-slice_fusion.rest_0_), channel_id=1, source_target_pairs={{0,96},{4,100},{8,104},{12,108},{16,112},{20,116},{24,120},{28,124... | collective-permute-start | bytes 3145736 | tf_op jit(solution)/shard_map/ppermute | solution.py:43
  43.7 43.9 %collective-permute-start.22 = (bf16[8,512,128]{2,1,0:T(8,128)(2,1)}, bf16[8,512,128]{2,1,0:T(8,128)(2,1)S(1)}, u32[]{:S(2)}, u32[]{:S(2)}) collective-permute-start(bf16[8,512,128]{2,1,0:T(8,128)(2,1)} %constant_dynamic-update-slice_fusion.5.rest_10_), channel_id=1, source_target_pairs={{0,8},{4,12},{8,16},{12,20},{16,24},{20,28},{24,0},{28,4},{32,40},... | collective-permute-start | bytes 3145736 | tf_op jit(solution)/shard_map/ppermute | solution.py:43
  43.7 20.6 %collective-permute-start.2 = (bf16[3,128,128]{2,1,0:T(8,128)(2,1)S(1)}, bf16[3,128,128]{2,1,0:T(8,128)(2,1)S(1)}, u32[]{:S(2)}, u32[]{:S(2)}) collective-permute-start(bf16[3,128,128]{2,1,0:T(8,128)(2,1)S(1)} %add_convert_fusion.5), channel_id=1, source_target_pairs={{0,16},{4,20},{8,24},{12,28},{16,32},{20,36},{24,40},{28,44},{32,4... | collective-permute-start | bytes 294920 | tf_op jit(solution)/shard_map/ppermute | solution.py:75
  47.3 42.8 %collective-permute-start.24 = (bf16[8,512,128]{2,1,0:T(8,128)(2,1)}, bf16[8,512,128]{2,1,0:T(8,128)(2,1)}, u32[]{:S(2)}, u32[]{:S(2)}) collective-permute-start(bf16[8,512,128]{2,1,0:T(8,128)(2,1)} %constant_dynamic-update-slice_fusion.5.rest_10_), channel_id=1, source_target_pairs={{0,24},{4,28},{8,0},{12,4},{16,8},{20,12},{24,16},{28,20},{32,56},... | collective-permute-start | bytes 3145736 | tf_op jit(solution)/shard_map/ppermute | solution.py:43
  70.9 21.1 %collective-permute-start.13 = (bf16[8,512,128]{2,1,0:T(8,128)(2,1)}, bf16[8,512,128]{2,1,0:T(8,128)(2,1)}, u32[]{:S(2)}, u32[]{:S(2)}) collective-permute-start(bf16[8,512,128]{2,1,0:T(8,128)(2,1)} %constant_dynamic-update-slice_fusion.rest_0_), channel_id=1, source_target_pairs={{0,4},{4,0},{8,12},{12,8},{16,20},{20,16},{24,28},{28,24},{32,36},... | collective-permute-start | bytes 3145736 | tf_op jit(solution)/shard_map/ppermute | solution.py:43
  82.9 14.2 %collective-permute-start.10 = (bf16[4,512,128]{2,1,0:T(8,128)(2,1)}, bf16[4,512,128]{2,1,0:T(8,128)(2,1)}, u32[]{:S(2)}, u32[]{:S(2)}) collective-permute-start(bf16[4,512,128]{2,1,0:T(8,128)(2,1)} %slice.62), channel_id=1, source_target_pairs={{0,32},{4,36},{8,40},{12,44},{16,48},{20,52},{24,56},{28,60},{32,6... | collective-permute-start | bytes 1572872 | tf_op jit(solution)/shard_map/ppermute | solution.py:43
  84.7 14.1 %collective-permute-start.12 = (bf16[4,512,128]{2,1,0:T(8,128)(2,1)}, bf16[4,512,128]{2,1,0:T(8,128)(2,1)}, u32[]{:S(2)}, u32[]{:S(2)}) collective-permute-start(bf16[4,512,128]{2,1,0:T(8,128)(2,1)} %slice.63), channel_id=1, source_target_pairs={{0,96},{4,100},{8,104},{12,108},{16,112},{20,116},{24,120},{28,124... | collective-permute-start | bytes 1572872 | tf_op jit(solution)/shard_map/ppermute | solution.py:43
  87.6 19.0 %collective-permute-start.26 = (bf16[8,512,128]{2,1,0:T(8,128)(2,1)}, bf16[8,512,128]{2,1,0:T(8,128)(2,1)}, u32[]{:S(2)}, u32[]{:S(2)}) collective-permute-start(bf16[8,512,128]{2,1,0:T(8,128)(2,1)} %constant_dynamic-update-slice_fusion.5.rest_10_), channel_id=1, source_target_pairs={{0,4},{4,0},{8,12},{12,8},{16,20},{20,16},{24,28},{28,24},{32,36},... | collective-permute-start | bytes 3145736 | tf_op jit(solution)/shard_map/ppermute | solution.py:43
  90.1 14.0 %collective-permute-start.23 = (bf16[4,512,128]{2,1,0:T(8,128)(2,1)}, bf16[4,512,128]{2,1,0:T(8,128)(2,1)}, u32[]{:S(2)}, u32[]{:S(2)}) collective-permute-start(bf16[4,512,128]{2,1,0:T(8,128)(2,1)} %slice.66), channel_id=1, source_target_pairs={{0,8},{4,12},{8,16},{12,20},{16,24},{20,28},{24,0},{28,4},{32,40},... | collective-permute-start | bytes 1572872 | tf_op jit(solution)/shard_map/ppermute | solution.py:43
  92.0 14.5 %collective-permute-start.25 = (bf16[4,512,128]{2,1,0:T(8,128)(2,1)}, bf16[4,512,128]{2,1,0:T(8,128)(2,1)}, u32[]{:S(2)}, u32[]{:S(2)}) collective-permute-start(bf16[4,512,128]{2,1,0:T(8,128)(2,1)} %slice.67), channel_id=1, source_target_pairs={{0,24},{4,28},{8,0},{12,4},{16,8},{20,12},{24,16},{28,20},{32,56},... | collective-permute-start | bytes 1572872 | tf_op jit(solution)/shard_map/ppermute | solution.py:43
  106.6 11.7 %collective-permute-start.14 = (bf16[8,512,128]{2,1,0:T(8,128)(2,1)}, bf16[8,512,128]{2,1,0:T(8,128)(2,1)}, u32[]{:S(2)}, u32[]{:S(2)}) collective-permute-start(bf16[8,512,128]{2,1,0:T(8,128)(2,1)} %copy-done.11), channel_id=1, source_target_pairs={{0,4},{4,0},{8,12},{12,8},{16,20},{20,16},{24,28},{28,24},{32,36},... | collective-permute-start | bytes 3145736 | tf_op jit(solution)/shard_map/ppermute | solution.py:43
  106.6 11.7 %collective-permute-start.17 = (bf16[8,512,128]{2,1,0:T(8,128)(2,1)}, bf16[8,512,128]{2,1,0:T(8,128)(2,1)}, u32[]{:S(2)}, u32[]{:S(2)}) collective-permute-start(bf16[8,512,128]{2,1,0:T(8,128)(2,1)} %copy-done.13), channel_id=1, source_target_pairs={{0,4},{4,0},{8,12},{12,8},{16,20},{20,16},{24,28},{28,24},{32,36},... | collective-permute-start | bytes 3145736 | tf_op jit(solution)/shard_map/ppermute | solution.py:43
  171.7 19.5 %collective-permute-start.38 = (bf16[4,512,128]{2,1,0:T(8,128)(2,1)S(1)}, bf16[4,512,128]{2,1,0:T(8,128)(2,1)S(1)}, u32[]{:S(2)}, u32[]{:S(2)}) collective-permute-start(bf16[4,512,128]{2,1,0:T(8,128)(2,1)S(1)} %get-tuple-element.50), channel_id=1, source_target_pairs={{0,32},{4,36},{8,40},{12,44},{16,48},{20,52},{24,56},{28,60},{32,6... | collective-permute-start | bytes 1572872 | tf_op jit(solution)/shard_map/ppermute | solution.py:43
  171.8 19.4 %collective-permute-start.39 = (bf16[4,512,128]{2,1,0:T(8,128)(2,1)S(1)}, bf16[4,512,128]{2,1,0:T(8,128)(2,1)S(1)}, u32[]{:S(2)}, u32[]{:S(2)}) collective-permute-start(bf16[4,512,128]{2,1,0:T(8,128)(2,1)S(1)} %get-tuple-element.51), channel_id=1, source_target_pairs={{0,96},{4,100},{8,104},{12,108},{16,112},{20,116},{24,120},{28,124... | collective-permute-start | bytes 1572872 | tf_op jit(solution)/shard_map/ppermute | solution.py:43
  174.4 16.7 %collective-permute-start.40 = (bf16[4,512,128]{2,1,0:T(8,128)(2,1)S(1)}, bf16[4,512,128]{2,1,0:T(8,128)(2,1)S(1)}, u32[]{:S(2)}, u32[]{:S(2)}) collective-permute-start(bf16[4,512,128]{2,1,0:T(8,128)(2,1)S(1)} %get-tuple-element.52), channel_id=1, source_target_pairs={{0,8},{4,12},{8,16},{12,20},{16,24},{20,28},{24,0},{28,4},{32,40},... | collective-permute-start | bytes 1572872 | tf_op jit(solution)/shard_map/ppermute | solution.py:43
  174.4 16.7 %collective-permute-start.41 = (bf16[4,512,128]{2,1,0:T(8,128)(2,1)S(1)}, bf16[4,512,128]{2,1,0:T(8,128)(2,1)S(1)}, u32[]{:S(2)}, u32[]{:S(2)}) collective-permute-start(bf16[4,512,128]{2,1,0:T(8,128)(2,1)S(1)} %get-tuple-element.53), channel_id=1, source_target_pairs={{0,24},{4,28},{8,0},{12,4},{16,8},{20,12},{24,16},{28,20},{32,56},... | collective-permute-start | bytes 1572872 | tf_op jit(solution)/shard_map/ppermute | solution.py:43
  189.7 13.4 %collective-permute-start.32 = (bf16[3,128,128]{2,1,0:T(8,128)(2,1)S(1)}, bf16[3,128,128]{2,1,0:T(8,128)(2,1)S(1)}, u32[]{:S(2)}, u32[]{:S(2)}) collective-permute-start(bf16[3,128,128]{2,1,0:T(8,128)(2,1)S(1)} %fusion.3), channel_id=1, source_target_pairs={{8,0},{12,4},{16,8},{20,12},{24,16},{28,20},{32,24},{36,28},{40,32... | collective-permute-start | bytes 294920 | tf_op jit(solution)/shard_map/ppermute | solution.py:75
  194.3 47.8 %collective-permute-start.42 = (bf16[8,512,128]{2,1,0:T(8,128)(2,1)S(1)}, bf16[8,512,128]{2,1,0:T(8,128)(2,1)S(1)}, u32[]{:S(2)}, u32[]{:S(2)}) collective-permute-start(bf16[8,512,128]{2,1,0:T(8,128)(2,1)S(1)} %get-tuple-element.54), channel_id=1, source_target_pairs={{0,32},{4,36},{8,40},{12,44},{16,48},{20,52},{24,56},{28,60},{32,6... | collective-permute-start | bytes 3145736 | tf_op jit(solution)/shard_map/ppermute | solution.py:43
  199.2 42.9 %collective-permute-start.43 = (bf16[8,512,128]{2,1,0:T(8,128)(2,1)S(1)}, bf16[8,512,128]{2,1,0:T(8,128)(2,1)S(1)}, u32[]{:S(2)}, u32[]{:S(2)}) collective-permute-start(bf16[8,512,128]{2,1,0:T(8,128)(2,1)S(1)} %get-tuple-element.55), channel_id=1, source_target_pairs={{0,96},{4,100},{8,104},{12,108},{16,112},{20,116},{24,120},{28,124... | collective-permute-start | bytes 3145736 | tf_op jit(solution)/shard_map/ppermute | solution.py:43
  200.4 41.7 %collective-permute-start.44 = (bf16[8,512,128]{2,1,0:T(8,128)(2,1)S(1)}, bf16[8,512,128]{2,1,0:T(8,128)(2,1)S(1)}, u32[]{:S(2)}, u32[]{:S(2)}) collective-permute-start(bf16[8,512,128]{2,1,0:T(8,128)(2,1)S(1)} %get-tuple-element.56), channel_id=1, source_target_pairs={{0,8},{4,12},{8,16},{12,20},{16,24},{20,28},{24,0},{28,4},{32,40},... | collective-permute-start | bytes 3145736 | tf_op jit(solution)/shard_map/ppermute | solution.py:43
  200.7 41.5 %collective-permute-start.45 = (bf16[8,512,128]{2,1,0:T(8,128)(2,1)S(1)}, bf16[8,512,128]{2,1,0:T(8,128)(2,1)S(1)}, u32[]{:S(2)}, u32[]{:S(2)}) collective-permute-start(bf16[8,512,128]{2,1,0:T(8,128)(2,1)S(1)} %get-tuple-element.57), channel_id=1, source_target_pairs={{0,24},{4,28},{8,0},{12,4},{16,8},{20,12},{24,16},{28,20},{32,56},... | collective-permute-start | bytes 3145736 | tf_op jit(solution)/shard_map/ppermute | solution.py:43
  203.1 25.7 %collective-permute-start.33 = (bf16[3,128,128]{2,1,0:T(8,128)(2,1)S(1)}, bf16[3,128,128]{2,1,0:T(8,128)(2,1)S(1)}, u32[]{:S(2)}, u32[]{:S(2)}) collective-permute-start(bf16[3,128,128]{2,1,0:T(8,128)(2,1)S(1)} %add_convert_fusion.2), channel_id=1, source_target_pairs={{16,0},{20,4},{24,8},{28,12},{32,16},{36,20},{40,24},{44,28},{48,3... | collective-permute-start | bytes 294920 | tf_op jit(solution)/shard_map/ppermute | solution.py:75
  252.9 13.0 %collective-permute-start.50 = (bf16[2,512,128]{2,1,0:T(8,128)(2,1)S(1)}, bf16[2,512,128]{2,1,0:T(8,128)(2,1)S(1)}, u32[]{:S(2)}, u32[]{:S(2)}) collective-permute-start(bf16[2,512,128]{2,1,0:T(8,128)(2,1)S(1)} %get-tuple-element.67), channel_id=1, source_target_pairs={{0,8},{4,12},{8,16},{12,20},{16,24},{20,28},{24,0},{28,4},{32,40},... | collective-permute-start | bytes 786440 | tf_op jit(solution)/shard_map/ppermute | solution.py:43
  253.0 12.9 %collective-permute-start.51 = (bf16[2,512,128]{2,1,0:T(8,128)(2,1)S(1)}, bf16[2,512,128]{2,1,0:T(8,128)(2,1)S(1)}, u32[]{:S(2)}, u32[]{:S(2)}) collective-permute-start(bf16[2,512,128]{2,1,0:T(8,128)(2,1)S(1)} %get-tuple-element.68), channel_id=1, source_target_pairs={{0,24},{4,28},{8,0},{12,4},{16,8},{20,12},{24,16},{28,20},{32,56},... | collective-permute-start | bytes 786440 | tf_op jit(solution)/shard_map/ppermute | solution.py:43
  (72 other events, 822.3 us)
Sparse Core Ops, SparseCore 0:
  9.7 86.5 all-gather.1
  142.0 80.5 reduce-scatter.1
where the time goes:
time: 278 us; the launch traced here: 274 us
  starting transfers between devices  90.9 us (33%)
  waiting for transfers between devices  70.7 us (25%)
  Pallas kernels  42.2 us (15%)
  local copies, waits for them, and re-layouts  31.3 us (11%)
  matrix products  18.4 us (7%)
  between operations  15 us (5%)
  other arithmetic  5.31 us (2%)
    ppermute x44, starting transfers between devices, shift(): return lax.ppermute(value, 'ctx', pairs)  64.5 us
    ppermute x10, waiting for transfers between devices, scan_states(): lax.ppermute((own + total).astype(BF), 'ctx', pairs).astype(F32)  61.9 us
    ppermute x10, starting transfers between devices, scan_states(): lax.ppermute((own + total).astype(BF), 'ctx', pairs).astype(F32)  26.3 us
    unnamed x104, local copies, waits for them, and re-layouts  20.3 us
    dot_general x2, matrix products, dot(): lax.dot_general(a, b, (((ca,), (cb,)), ((), ())), preferred_element_type=...  18.4 us
    pallas_call x1, Pallas kernels, sparse_forward(): pl.pallas_call(sparse_forward_kernel, grid_spec=pltpu.PrefetchScalarGridS...  11.4 us
    ppermute x44, waiting for transfers between devices, shift(): return lax.ppermute(value, 'ctx', pairs)  8.15 us
    pallas_call x3, Pallas kernels, back_call(): pl.pallas_call(kernel, in_specs=[pl.BlockSpec(memory_space=pltpu.SMEM)] +...  7.88 us
  transfers between devices with their start and end apart: 56, of which 10 were waited for; matrix products, arithmetic and copies ran while one was open for 15% of the time, Pallas kernels for 15%

commit v1 on v0

v1 whole, which is shorter than its diff:
```python
import functools
import math

import jax
import jax.numpy as jnp
from jax import lax
from jax.experimental import pallas as pl
from jax.experimental.pallas import tpu as pltpu
from jax.sharding import PartitionSpec as P

HD = 128
LIN = 3
LISTED = 4
BLOCK = 512
SIDE = 4
CORES = 2
CTX = SIDE * SIDE * CORES
SCALING = 1.0 / math.sqrt(HD)
BF = jnp.bfloat16
F32 = jnp.float32
MIB = 1 << 20
TILE = (BLOCK, HD)


def dot(a, b, ca, cb):
    return lax.dot_general(a, b, (((ca,), (cb,)), ((), ())), preferred_element_type=F32)


def params(mib):
    return pltpu.CompilerParams(vmem_limit_bytes=mib * MIB)


def cost(flops, nbytes):
    return pl.CostEstimate(flops=int(flops), bytes_accessed=int(nbytes), transcendentals=0)


def ring_move(value, axis, step):
    pairs = []
    for z in range(SIDE):
        for x in range(SIDE):
            for c in range(CORES):
                dx, dz = (step, 0) if axis == c else (0, step)
                to = (((z + dz) % SIDE) * SIDE + (x + dx) % SIDE) * CORES + c
                pairs.append(((z * SIDE + x) * CORES + c, to))
    return lax.ppermute(value, "ctx", pairs)


def swap(value):
    return lax.ppermute(value, "ctx", [(i, i ^ 1) for i in range(CTX)])


def head_move(value, step):
    return lax.ppermute(value, "head", [(i, (i + step) % SIDE) for i in range(SIDE)])


def after(value, *others):
    return lax.optimization_barrier((value, *others))[0]


def scan_step(own, total, step, backward):
    if backward:
        pairs = [(i + step, i) for i in range(CTX - step)]
    else:
        pairs = [(i, i + step) for i in range(CTX - step)]
    return lax.ppermute((own + total).astype(BF), "ctx", pairs)


def copies_kernel(moves, n_in, *refs):
    ins, outs, sems = refs[:n_in], refs[n_in:-1], refs[-1]
    copies = [
        pltpu.make_async_copy(
            ins[i].at[pl.ds(i0, n)], outs[o].at[pl.ds(o0, n)], sems.at[m]
        )
        for m, (i, i0, o, o0, n) in enumerate(moves)
    ]
    for copy in copies:
        copy.start()
    for copy in copies:
        copy.wait()


def copies(inputs, sizes, moves):
    anywhere = pl.BlockSpec(memory_space=pl.ANY)
    return pl.pallas_call(
        functools.partial(copies_kernel, moves, len(inputs)),
        in_specs=[anywhere] * len(inputs),
        out_specs=[anywhere] * len(sizes),
        out_shape=[jax.ShapeDtypeStruct((n,) + inputs[0].shape[1:], BF) for n in sizes],
        scratch_shapes=[pltpu.SemaphoreType.DMA((len(moves),))],
        compiler_params=params(4),
        cost_estimate=cost(0, sum(m[4] for m in moves) * math.prod(inputs[0].shape[1:]) * 4),
        name="copies",
    )(*inputs)


def joined(pieces):
    moves, spot = [], 0
    for i, piece in enumerate(pieces):
        moves.append((i, 0, 0, spot, piece.shape[0]))
        spot += piece.shape[0]
    return copies(pieces, [spot], moves)[0]


def halves(right, left):
    n = right.shape[0] // 2
    return copies([right, left], [n, n], [(0, 0, 0, 0, n), (1, n, 1, 0, n)])


def causal_mask():
    s = lax.broadcasted_iota(jnp.int32, (BLOCK, BLOCK), 0)
    u = lax.broadcasted_iota(jnp.int32, (BLOCK, BLOCK), 1)
    return s <= u


def states_kernel(k_ref, v_ref, out_ref):
    out_ref[0, 0] = dot(k_ref[...], v_ref[...], 0, 0)


def adjoint_kernel(q_ref, g_ref, c_ref, out_ref):
    qt = (q_ref[...].astype(F32).T * c_ref[0:1, :]).astype(BF)
    out_ref[0, 0] = dot(qt, g_ref[...], 1, 0)


def tile_spec():
    return pl.BlockSpec(TILE, lambda i, h: (i, h))


def scale_spec():
    return pl.BlockSpec((8, BLOCK), lambda i, h: (0, i))


def state_spec():
    return pl.BlockSpec((1, 1, HD, HD), lambda i, h: (i, h, 0, 0))


def block_states(keys, values):
    return pl.pallas_call(
        states_kernel,
        grid=(2, LIN),
        in_specs=[tile_spec(), tile_spec()],
        out_specs=state_spec(),
        out_shape=jax.ShapeDtypeStruct((2, LIN, HD, HD), F32),
        compiler_params=params(16),
        cost_estimate=cost(1e8, 2 * MIB),
        name="block_states",
    )(keys, values)


def block_adjoints(queries, grads, scale):
    return pl.pallas_call(
        adjoint_kernel,
        grid=(2, LIN),
        in_specs=[tile_spec(), tile_spec(), scale_spec()],
        out_specs=state_spec(),
        out_shape=jax.ShapeDtypeStruct((2, LIN, HD, HD), F32),
        compiler_params=params(16),
        cost_estimate=cost(1e8, 2 * MIB),
        name="block_adjoints",
    )(queries, grads, scale)


def linear_forward_kernel(q_ref, k_ref, v_ref, c_ref, hi_ref, lo_ref, out_ref):
    q, k, v, c = q_ref[...], k_ref[...], v_ref[...], c_ref[0:1, :]
    weights = jnp.where(causal_mask(), dot(k, q, 1, 1) * c, 0.0).astype(BF)
    out = dot(v, weights, 0, 0)
    out = out + c * (dot(hi_ref[0, 0], q, 1, 1) + dot(lo_ref[0, 0], q, 1, 1))
    out_ref[...] = out.T.astype(BF)


def linear_forward(queries, keys, values, scale, hi, lo):
    return pl.pallas_call(
        linear_forward_kernel,
        grid=(2, LIN),
        in_specs=[tile_spec()] * 3 + [scale_spec(), state_spec(), state_spec()],
        out_specs=tile_spec(),
        out_shape=jax.ShapeDtypeStruct(queries.shape, BF),
        compiler_params=params(24),
        cost_estimate=cost(2.4e9, 4 * MIB),
        name="linear_forward",
    )(queries, keys, values, scale, hi, lo)


def linear_backward_kernel(
    q_ref, k_ref, v_ref, g_ref, c_ref, sh_ref, sl_ref, ah_ref, al_ref, base_ref, dq_ref, dk_ref, dv_ref
):
    q, k, v, g, c = q_ref[...], k_ref[...], v_ref[...], g_ref[...], c_ref[0:1, :]
    mask = causal_mask()
    grad_weights = jnp.where(mask, dot(v, g, 1, 1) * c, 0.0).astype(BF)
    dq = dot(k, grad_weights, 0, 0)
    dq = dq + c * (dot(sh_ref[0, 0], g, 1, 1) + dot(sl_ref[0, 0], g, 1, 1))
    dq_ref[...] = dq.T.astype(BF)
    dk = dot(grad_weights, q, 1, 0) + dot(v, ah_ref[0, 0], 1, 1) + dot(v, al_ref[0, 0], 1, 1)
    dk_ref[...] = dk.astype(BF)
    weights = jnp.where(mask, dot(k, q, 1, 1) * c, 0.0).astype(BF)
    dv = dot(weights, g, 1, 0) + dot(k, ah_ref[0, 0], 1, 0) + dot(k, al_ref[0, 0], 1, 0)
    dv_ref[...] = dv.astype(BF)


def linear_backward(queries, keys, values, grads, scale, sh, sl, ah, al, base):
    shape = jax.ShapeDtypeStruct(queries.shape, BF)
    return pl.pallas_call(
        linear_backward_kernel,
        grid=(2, LIN),
        in_specs=[tile_spec()] * 4
        + [scale_spec()]
        + [state_spec()] * 4
        + [pl.BlockSpec(memory_space=pl.ANY)],
        out_specs=[tile_spec()] * 3,
        out_shape=[shape] * 3,
        input_output_aliases={9: 0},
        compiler_params=params(24),
        cost_estimate=cost(5e9, 8 * MIB),
        name="linear_backward",
    )(queries, keys, values, grads, scale, sh, sl, ah, al, base)


def sparse_forward_kernel(table, q_ref, k_ref, v_ref, base_ref, *rest):
    pieces = rest[:10]
    out_ref, p_ref, kf_ref, vf_ref, s_ref, sems = rest[10:]
    step = pl.program_id(0)
    for r in range(LISTED):
        row = step * LISTED + r
        for j in range(10):

            @pl.when(table[row, 0] == j)
            def _():
                pltpu.make_async_copy(pieces[j].at[table[row, 1]], kf_ref.at[r], sems.at[0, r]).start()

            @pl.when(table[row, 2] == j)
            def _():
                pltpu.make_async_copy(pieces[j].at[table[row, 3]], vf_ref.at[r], sems.at[1, r]).start()

    q = q_ref[...]
    s = jnp.where(causal_mask(), dot(k_ref[...], q, 1, 1) * SCALING, -1e30)
    s_ref[0] = s
    peak = jnp.max(s, axis=0, keepdims=True)
    for r in range(LISTED):
        pltpu.make_async_copy(pieces[0].at[0], kf_ref.at[r], sems.at[0, r]).wait()
        bias = jnp.where(table[step * LISTED + r, 4] == 1, 0.0, -1e30).astype(F32)
        s = dot(kf_ref[r], q, 1, 1) * SCALING + bias
        s_ref[r + 1] = s
        peak = jnp.maximum(peak, jnp.max(s, axis=0, keepdims=True))
    total = jnp.zeros((1, BLOCK), F32)
    for r in range(LISTED + 1):
        e = jnp.exp(s_ref[r] - peak)
        s_ref[r] = e
        total = total + jnp.sum(e, axis=0, keepdims=True)
    inverse = 1.0 / total
    out = jnp.zeros((HD, BLOCK), F32)
    for r in range(LISTED + 1):
        p = (s_ref[r] * inverse).astype(BF)
        p_ref[0, r] = p
        if r == 0:
            value = v_ref[...]
        else:
            pltpu.make_async_copy(pieces[0].at[0], vf_ref.at[r - 1], sems.at[1, r - 1]).wait()
            value = vf_ref[r - 1]
        out = out + dot(value, p, 0, 0)
    out_ref[...] = out.T.astype(BF)


def sparse_forward(table, queries, keys, values, base, pieces):
    column = pl.BlockSpec(TILE, lambda i, t: (i, LIN))
    anywhere = pl.BlockSpec(memory_space=pl.ANY)
    return pl.pallas_call(
        sparse_forward_kernel,
        grid_spec=pltpu.PrefetchScalarGridSpec(
            num_scalar_prefetch=1,
            grid=(2,),
            in_specs=[column] * 3 + [anywhere] * 11,
            out_specs=[
                column,
                pl.BlockSpec((1, LISTED + 1, BLOCK, BLOCK), lambda i, t: (i, 0, 0, 0)),
                pl.BlockSpec((LISTED, BLOCK, HD), lambda i, t: (i, 0, 0)),
                pl.BlockSpec((LISTED, BLOCK, HD), lambda i, t: (i, 0, 0)),
            ],
            scratch_shapes=[
                pltpu.VMEM((LISTED + 1, BLOCK, BLOCK), F32),
                pltpu.SemaphoreType.DMA((2, LISTED)),
            ],
        ),
        out_shape=[
            jax.ShapeDtypeStruct(queries.shape, BF),
            jax.ShapeDtypeStruct((2, LISTED + 1, BLOCK, BLOCK), BF),
            jax.ShapeDtypeStruct((2 * LISTED, BLOCK, HD), BF),
            jax.ShapeDtypeStruct((2 * LISTED, BLOCK, HD), BF),
        ],
        input_output_aliases={4: 0},
        compiler_params=params(32),
        cost_estimate=cost(4e9, 12 * MIB),
        name="sparse_forward",
    )(table, queries, keys, values, base, *pieces)


def sparse_backward_kernel(
    core, q_ref, k_ref, v_ref, g_ref, o_ref, p_ref, kf_ref, vf_ref, dq_ref, dk_ref, dv_ref, mine_ref, sent_ref
):
    first = core[0] == 0
    q, g = q_ref[...], g_ref[...]
    row_dot = jnp.sum((g.astype(F32) * o_ref[...].astype(F32)).T, axis=0, keepdims=True)
    dq = jnp.zeros((HD, BLOCK), F32)
    for r in range(LISTED + 1):
        p = p_ref[0, r]
        key = k_ref[...] if r == 0 else kf_ref[r - 1]
        value = v_ref[...] if r == 0 else vf_ref[r - 1]
        dp = dot(value, g, 1, 1)
        ds = (p.astype(F32) * (dp - row_dot)).astype(BF)
        dq = dq + dot(key, ds, 0, 0)
        dk = dot(ds, q, 1, 0) * SCALING
        dv = dot(p, g, 1, 0)
        if r == 0:
            dk_ref[...] = dk
            dv_ref[...] = dv
        else:
            mine_ref[r - 1] = jnp.where(first, dk, dv).astype(BF)
            sent_ref[r - 1] = jnp.where(first, dv, dk).astype(BF)
    dq_ref[...] = (dq * SCALING).T.astype(BF)


def sparse_backward(core, queries, keys, values, grads, outs, probs, far_k, far_v):
    column = pl.BlockSpec(TILE, lambda i, c: (i, LIN))
    four = pl.BlockSpec((LISTED, BLOCK, HD), lambda i, c: (i, 0, 0))
    rows = pl.BlockSpec(TILE, lambda i, c: (i, 0))
    five = pl.BlockSpec((1, LISTED + 1, BLOCK, BLOCK), lambda i, c: (i, 0, 0, 0))
    return pl.pallas_call(
        sparse_backward_kernel,
        grid_spec=pltpu.PrefetchScalarGridSpec(
            num_scalar_prefetch=1,
            grid=(2,),
            in_specs=[column] * 5 + [five, four, four],
            out_specs=[column, rows, rows, four, four],
        ),
        out_shape=[
            jax.ShapeDtypeStruct(queries.shape, BF),
            jax.ShapeDtypeStruct((2 * BLOCK, HD), F32),
            jax.ShapeDtypeStruct((2 * BLOCK, HD), F32),
            jax.ShapeDtypeStruct((2 * LISTED, BLOCK, HD), BF),
            jax.ShapeDtypeStruct((2 * LISTED, BLOCK, HD), BF),
        ],
        compiler_params=params(32),
        cost_estimate=cost(8e9, 12 * MIB),
        name="sparse_backward",
    )(core, queries, keys, values, grads, outs, probs, far_k, far_v)


def choose_kernel(core, k_ref, v_ref, mine_ref, sent_ref):
    first = core[0] == 0
    k, v = k_ref[...], v_ref[...]
    mine_ref[0] = jnp.where(first, k, v)
    sent_ref[0] = jnp.where(first, v, k)


def choose(core, keys, values):
    column = pl.BlockSpec(TILE, lambda i, c: (i, LIN))
    block = pl.BlockSpec((1, BLOCK, HD), lambda i, c: (i, 0, 0))
    return pl.pallas_call(
        choose_kernel,
        grid_spec=pltpu.PrefetchScalarGridSpec(
            num_scalar_prefetch=1, grid=(2,), in_specs=[column] * 2, out_specs=[block] * 2
        ),
        out_shape=[jax.ShapeDtypeStruct((2, BLOCK, HD), BF)] * 2,
        compiler_params=params(4),
        cost_estimate=cost(1e6, MIB),
        name="choose",
    )(core, keys, values)


ROWS = 256


def grad_near_kernel(order, own, right, left, w0, w3, w1, out):
    out[...] = (
        dot(own[...], w0[...], 1, 0) + dot(right[...], w3[...], 1, 0) + dot(left[...], w1[...], 1, 0)
    )


def weight_spec(shape, nth):
    return pl.BlockSpec(shape, lambda i, o: (o[nth], 0))


def grad_near(order, own, right, left, weight):
    rows, width = own.shape
    cols = weight.shape[1]
    part = pl.BlockSpec((ROWS, width), lambda i, o: (i, 0))
    return pl.pallas_call(
        grad_near_kernel,
        grid_spec=pltpu.PrefetchScalarGridSpec(
            num_scalar_prefetch=1,
            grid=(rows // ROWS,),
            in_specs=[part] * 3 + [weight_spec((width, cols), n) for n in (0, 3, 1)],
            out_specs=pl.BlockSpec((ROWS, cols), lambda i, o: (i, 0)),
        ),
        out_shape=jax.ShapeDtypeStruct((rows, cols), F32),
        compiler_params=params(32),
        cost_estimate=cost(6 * rows * width * cols, 11 * MIB),
        name="grad_near",
    )(order, own, right, left, weight, weight, weight)


def low(i):
    return jnp.minimum(i, 1)


def high(i):
    return jnp.maximum(i - 2, 0)


def grad_far_kernel(order, part, far_a, far_b, w2, out):
    far = jnp.where(pl.program_id(0) < 2, far_a[...], far_b[...])
    out[...] = (part[...] + dot(far, w2[...], 1, 0)).astype(BF)


def grad_far(order, part, far_a, far_b, weight):
    rows, cols = part.shape
    width = far_a.shape[1]
    tile = pl.BlockSpec((ROWS, cols), lambda i, o: (i, 0))
    return pl.pallas_call(
        grad_far_kernel,
        grid_spec=pltpu.PrefetchScalarGridSpec(
            num_scalar_prefetch=1,
            grid=(rows // ROWS,),
            in_specs=[
                tile,
                pl.BlockSpec((ROWS, width), lambda i, o: (low(i), 0)),
                pl.BlockSpec((ROWS, width), lambda i, o: (high(i), 0)),
                weight_spec((width, cols), 2),
            ],
            out_specs=tile,
        ),
        out_shape=jax.ShapeDtypeStruct((rows, cols), BF),
        compiler_params=params(32),
        cost_estimate=cost(2 * rows * width * cols, 6 * MIB),
        name="grad_far",
    )(order, part, far_a, far_b, weight)


def out_far_kernel(order, a, w, far_a, far_b):
    value = dot(a[...], w[...], 1, 1).astype(BF)

    @pl.when(pl.program_id(0) < 2)
    def _():
        far_a[...] = value

    @pl.when(pl.program_id(0) >= 2)
    def _():
        far_b[...] = value


def out_near_kernel(order, a, w1, w3, ra, rb, n1, n3):
    first = pl.program_id(0) < 2
    more = jnp.where(first, ra[...], 0).astype(F32)
    n1[...] = (dot(a[...], w1[...], 1, 1) + more).astype(BF)
    more = jnp.where(first, 0, rb[...]).astype(F32)
    n3[...] = (dot(a[...], w3[...], 1, 1) + more).astype(BF)


def out_home_kernel(order, a, w0, r1, r3, out):
    out[...] = (dot(a[...], w0[...], 1, 1) + r1[...].astype(F32) + r3[...].astype(F32)).astype(BF)


def out_call(kernel, order, attention, weight, nths, others, other_maps, out_rows, out_maps, name):
    rows, cols = attention.shape
    width = weight.shape[0] // SIDE

    def spec(index):
        return pl.BlockSpec((ROWS, width), lambda i, o: (index(i), 0))

    return pl.pallas_call(
        kernel,
        grid_spec=pltpu.PrefetchScalarGridSpec(
            num_scalar_prefetch=1,
            grid=(rows // ROWS,),
            in_specs=[pl.BlockSpec((ROWS, cols), lambda i, o: (i, 0))]
            + [weight_spec((width, cols), n) for n in nths]
            + [spec(m) for m in other_maps],
            out_specs=[spec(m) for m in out_maps],
        ),
        out_shape=[jax.ShapeDtypeStruct((r, width), BF) for r in out_rows],
        compiler_params=params(32),
        cost_estimate=cost(2 * len(nths) * rows * width * cols, (3 + 2 * len(out_rows)) * MIB),
        name=name,
    )(order, attention, *([weight] * len(nths)), *others)


def same(i):
    return i


def placed(table, j, own_ref, peer_ref):
    a, b = table[0, j], table[1, j]
    first = own_ref[jnp.maximum(a, 0)].astype(F32) * jnp.where(a >= 0, 1.0, 0.0).astype(F32)
    second = peer_ref[jnp.maximum(b, 0)].astype(F32) * jnp.where(b >= 0, 1.0, 0.0).astype(F32)
    return first + second


def back_call(kernel, table, operands, sizes, name):
    vm = pl.BlockSpec(memory_space=pltpu.VMEM)
    shapes = [(n, BLOCK, HD) for n in sizes]
    nbytes = sum(math.prod(o.shape) * 2 for o in operands) + sum(math.prod(s) * 2 for s in shapes)
    return pl.pallas_call(
        kernel,
        in_specs=[pl.BlockSpec(memory_space=pltpu.SMEM)] + [vm] * len(operands),
        out_specs=[vm] * len(shapes),
        out_shape=[jax.ShapeDtypeStruct(s, BF) for s in shapes],
        compiler_params=params(32),
        cost_estimate=cost(1e7, nbytes),
        name=name,
    )(table, *operands)


def far_kernel(table, own, peer, far_a, far_b):
    @pl.loop(0, 8)
    def _(j):
        far_a[j] = placed(table, 32 + j, own, peer).astype(BF)
        far_b[j] = placed(table, 40 + j, own, peer).astype(BF)


def near_kernel(table, own, peer, ra, rb, right, left):
    @pl.loop(0, 8)
    def _(j):
        right[j] = (placed(table, 16 + j, own, peer) + ra[j].astype(F32)).astype(BF)
        right[j + 8] = placed(table, 24 + j, own, peer).astype(BF)
        left[j] = placed(table, 48 + j, own, peer).astype(BF)
        left[j + 8] = (placed(table, 56 + j, own, peer) + rb[j].astype(F32)).astype(BF)


def turn_kernel(table, own, peer, r1, r3, home, right, far_a, far_b, left):
    def total(j):
        return (placed(table, j, own, peer) + r1[j].astype(F32) + r3[j].astype(F32)).astype(BF)

    @pl.loop(0, 4)
    def _(j):
        home[j] = total(j)
        right[j] = total(4 + j)
        left[j] = total(12 + j)

    @pl.loop(0, 2)
    def _(j):
        far_a[j] = total(8 + j)
        far_b[j] = total(10 + j)


def last_kernel(table, right, left, ra, rb, o_right, o_left):
    for j in range(2):
        o_right[j] = (right[j].astype(F32) + ra[j].astype(F32)).astype(BF)
        o_right[j + 2] = right[j + 2]
        o_left[j] = left[j]
        o_left[j + 2] = (left[j + 2].astype(F32) + rb[j].astype(F32)).astype(BF)


def tail_kernel(table, home, r1, r3, mine, sent):
    for j in range(2):
        mine[j] = (home[j].astype(F32) + r1[j].astype(F32) + r3[j].astype(F32)).astype(BF)
        sent[j] = (home[j + 2].astype(F32) + r1[j + 2].astype(F32) + r3[j + 2].astype(F32)).astype(BF)


def finish_kernel(core, dk, dv, mine_ref, got_ref, kg_in, vg_in, kg, vg):
    first = core[0] == 0
    mine, got = mine_ref[0].astype(F32), got_ref[0].astype(F32)
    kg[...] = (dk[...] + jnp.where(first, mine, got)).astype(BF)
    vg[...] = (dv[...] + jnp.where(first, got, mine)).astype(BF)


def finish(core, dk, dv, mine, got, key_grad, value_grad):
    rows = pl.BlockSpec(TILE, lambda i, c: (i, 0))
    piece = pl.BlockSpec((1, BLOCK, HD), lambda i, c: (i, 0, 0))
    column = pl.BlockSpec(TILE, lambda i, c: (i, LIN))
    anywhere = pl.BlockSpec(memory_space=pl.ANY)
    shape = jax.ShapeDtypeStruct(key_grad.shape, BF)
    return pl.pallas_call(
        finish_kernel,
        grid_spec=pltpu.PrefetchScalarGridSpec(
            num_scalar_prefetch=1,
            grid=(2,),
            in_specs=[rows, rows, piece, piece, anywhere, anywhere],
            out_specs=[column, column],
        ),
        out_shape=[shape, shape],
        input_output_aliases={5: 0, 6: 1},
        compiler_params=params(16),
        cost_estimate=cost(1e6, 3 * MIB),
        name="finish",
    )(core, dk, dv, mine, got, key_grad, value_grad)


def where_is(blocks, place):
    owner, within = blocks // 2, blocks % 2
    pz = (place // (SIDE * CORES) - owner // (SIDE * CORES)) % SIDE
    px = (place // CORES % SIDE - owner // CORES % SIDE) % SIDE
    return pz, px, owner % CORES, within


def spot_of(blocks, place, stream):
    pz, px, core, within = where_is(blocks, place)
    rel = (core != stream).astype(jnp.int32)
    outer = jnp.where(stream == 0, pz, px)
    first = jnp.where(stream == 0, px, pz)
    return outer, first, rel * 2 + within


def piece_of(blocks, place, stream):
    outer, first, rest = spot_of(blocks, place, stream)
    second = (outer == 2) & (first >= 2)
    piece = jnp.where(outer < 2, outer, jnp.where(outer == 3, 4, jnp.where(second, 3, 2)))
    index = first * 4 + rest - jnp.where(second, 8, 0)
    return piece + 5 * (place % CORES != stream).astype(jnp.int32), index


def fetch_table(lists, place):
    flat = lists.reshape(-1)
    mine = place * 2 + jnp.arange(2 * LISTED, dtype=jnp.int32) // LISTED
    usable = (flat != mine).astype(jnp.int32)
    columns = [*piece_of(flat, place, 0), *piece_of(flat, place, 1), usable]
    return jnp.stack(columns, axis=1).astype(jnp.int32)


def back_table(lists, peer_lists, place):
    slots = jnp.arange(2 * LISTED, dtype=jnp.int32)[:, None]
    spots = jnp.arange(64, dtype=jnp.int32)[None, :]
    rows = []
    for some in (lists, peer_lists):
        outer, first, rest = spot_of(some.reshape(-1), place, place % CORES)
        target = (-outer) % SIDE * 16 + (-first) % SIDE * 4 + rest
        rows.append(jnp.max(jnp.where(target[:, None] == spots, slots, -1), axis=0))
    return jnp.stack(rows).astype(jnp.int32)


def split(value):
    high = value.astype(BF)
    return high, (value - high.astype(F32)).astype(BF)


def local(queries, keys, values, out_weight, out_grad, long_blocks):
    place = lax.axis_index("ctx")
    core = (place % CORES).astype(jnp.int32).reshape(1)
    order = (lax.axis_index("head") + jnp.arange(SIDE, dtype=jnp.int32)) % SIDE
    row_count = queries.shape[0]
    positions = place * row_count + jnp.arange(row_count, dtype=jnp.int32)
    scale = 1.0 / (math.sqrt(HD) * jnp.sqrt((positions + 1).astype(F32)))
    scale = jnp.broadcast_to(scale[None, :], (8, row_count))
    lists = lax.dynamic_slice_in_dim(long_blocks, place * 2, 2, 0)
    peer_lists = lax.dynamic_slice_in_dim(long_blocks, (place ^ 1) * 2, 2, 0)
    fetch = fetch_table(lists, place)
    back = back_table(lists, peer_lists, place)

    og_right, og_left = head_move(out_grad, 1), head_move(out_grad, -1)
    mine, sent = choose(core, keys, values)
    start = joined([mine, swap(sent)])
    a_right, a_left = ring_move(start, 0, 1), ring_move(start, 0, -1)
    cut = halves(a_right, a_left)
    a_far = ring_move(cut[0], 0, 1), ring_move(cut[1], 0, -1)
    line = joined([start, a_right, a_far[0], a_far[1], a_left])
    b_right, b_left = ring_move(line, 1, 1), ring_move(line, 1, -1)
    line_swapped = swap(line)
    cut = halves(b_right, b_left)
    b_far = ring_move(cut[0], 1, 1), ring_move(cut[1], 1, -1)
    pieces = [line, b_right, b_far[0], b_far[1], b_left]
    pieces = pieces + [line_swapped] + [swap(p) for p in pieces[1:]]

    grad_part = grad_near(order, out_grad, og_right, og_left, out_weight)
    rows = row_count // 2
    og_far = head_move(og_right[:rows], 1), head_move(og_left[rows:], -1)

    states = block_states(keys, values)
    own = states[0] + states[1]
    total = jnp.zeros_like(own)
    total = total + scan_step(own, total, 1, False).astype(F32)
    total = total + scan_step(own, total, 2, False).astype(F32)
    total = after(total, a_right, a_left)
    total = total + after(scan_step(own, total, 4, False), line).astype(F32)
    total = after(total, line_swapped)
    total = total + after(scan_step(own, total, 8, False), b_right, b_left).astype(F32)
    total = total + after(scan_step(own, total, 16, False), *b_far).astype(F32)
    before = jnp.stack([total, total + states[0]])
    flip_hi, flip_lo = split(jnp.swapaxes(before, 2, 3))

    attention = linear_forward(queries, keys, values, scale, flip_hi, flip_lo)
    attention, probs, far_k, far_v = sparse_forward(
        fetch, queries, keys, values, attention, pieces
    )
    attn_grad = grad_far(order, grad_part, *og_far, out_weight)
    query_grad, own_dk, own_dv, pair_mine, pair_sent = sparse_backward(
        core, queries, keys, values, attn_grad, attention, probs, far_k, far_v
    )

    base = [pair_mine, swap(pair_sent)]
    far = back_call(far_kernel, back, base, [8, 8], "back_far")
    r1, r3 = ring_move(far[0], 1, 1), ring_move(far[1], 1, -1)
    near = back_call(near_kernel, back, base + [r1, r3], [16, 16], "back_near")
    n1, n3 = ring_move(near[0], 1, 1), ring_move(near[1], 1, -1)

    of = out_call(out_far_kernel, order, attention, out_weight, (2,), [], [], [rows] * 2, [low, high], "out_far")
    o1, o3 = head_move(of[0], 1), head_move(of[1], -1)
    on = out_call(
        out_near_kernel, order, attention, out_weight, (1, 3), [o1, o3], [low, high], [row_count] * 2, [same] * 2, "out_near"
    )
    o1, o3 = head_move(on[0], 1), head_move(on[1], -1)
    (layer_out,) = out_call(
        out_home_kernel, order, attention, out_weight, (0,), [o1, o3], [same] * 2, [row_count], [same], "out_home"
    )

    adjoints = block_adjoints(queries, attn_grad, scale)
    own = adjoints[0] + adjoints[1]
    total = jnp.zeros_like(own)
    for step in (1, 2, 4):
        total = total + scan_step(own, total, step, True).astype(F32)
    total = after(total, pair_sent)
    total = total + scan_step(own, total, 8, True).astype(F32)
    total = total + after(scan_step(own, total, 16, True), r1, r3).astype(F32)
    later = jnp.stack([total + adjoints[1], total])
    query_grad, key_grad, value_grad = linear_backward(
        queries, keys, values, attn_grad, scale, *split(before), *split(later), query_grad
    )

    turn = back_call(turn_kernel, back, base + [after(n1, key_grad), n3], [4, 4, 2, 2, 4], "back_turn")
    home, right, far_a, far_b, left = turn
    r1, r3 = ring_move(far_a, 0, 1), ring_move(far_b, 0, -1)
    right, left = back_call(last_kernel, back, [right, left, r1, r3], [4, 4], "back_last")
    r1, r3 = ring_move(right, 0, 1), ring_move(left, 0, -1)
    mine, sent = back_call(tail_kernel, back, [home, r1, r3], [2, 2], "back_tail")
    key_grad, value_grad = finish(core, own_dk, own_dv, mine, swap(sent), key_grad, value_grad)
    return layer_out, query_grad, key_grad, value_grad


def solution(mesh):
    return jax.shard_map(
        local,
        mesh=mesh,
        in_specs=(
            P("ctx", "head"),
            P("ctx", "head"),
            P("ctx", "head"),
            P(None, "head"),
            P("ctx", "head"),
            P(),
        ),
        out_specs=(P("ctx", "head"), P("ctx", "head"), P("ctx", "head"), P("ctx", "head")),
        check_vma=False,
    )
```

time: 278 us -> 316 us (1.14); the launches traced: 274 us -> 315 us
  Pallas kernels: 42.2 us -> 131 us
  matrix products: 18.4 us -> 0 us
  between operations: 15 us -> 1.41 us
  starting transfers between devices: 90.9 us -> 81.4 us
  local copies, waits for them, and re-layouts: 31.3 us -> 22.8 us
  waiting for transfers between devices: 70.7 us -> 77.3 us
  other arithmetic: 5.31 us -> 1.62 us
    pallas_call x3 -> x12, Pallas kernels: 8.09 us -> 94.8 us  [the longest x4 66.1 us: copies(): pl.pallas_call(functools.partial(copies_kernel, moves, len(inputs)), in_s...]
    dot_general x2 -> x0, matrix products: 18.4 us -> none  [dot(): lax.dot_general(a, b, (((ca,), (cb,)), ((), ())), preferred_element_type=...]
    ppermute x54 -> x42, starting transfers between devices: 90.8 us -> 81.4 us  [the longest x10 27.2 us: scan_step(): return lax.ppermute((own + total).astype(BF), 'ctx', pairs)]
    ppermute x54 -> x42, waiting for transfers between devices: 70 us -> 77.3 us  [the longest x10 51.1 us: scan_step(): return lax.ppermute((own + total).astype(BF), 'ctx', pairs)]
    slice x10 -> x2, local copies, waits for them, and re-layouts: 6.38 us -> 3.3 us  [local(): og_far = (head_move(og_right[:rows], 1), head_move(og_left[rows:], -1))]
    unnamed x104 -> x62, local copies, waits for them, and re-layouts: 20.3 us -> 18.6 us
    pallas_call x3 -> x5, Pallas kernels: 7.88 us -> 9.29 us  [back_call(): pl.pallas_call(kernel, in_specs=[pl.BlockSpec(memory_space=pltpu.SMEM)] +...]
  transfers between devices with their start and end apart: 56 -> 42, of which waited for: 10 -> 13; matrix products, arithmetic and copies ran while one was open for 15% -> 2% of each run, Pallas kernels for 15% -> 34%
where the time goes in v1:
time: 316 us; the launch traced here: 315 us
  Pallas kernels  131 us (41%)
  starting transfers between devices  81.4 us (26%)
  waiting for transfers between devices  77.3 us (24%)
  local copies, waits for them, and re-layouts  22.8 us (7%)
    pallas_call x4, Pallas kernels, copies(): pl.pallas_call(functools.partial(copies_kernel, moves, len(inputs)), in_s...  66.1 us
    ppermute x10, waiting for transfers between devices, scan_step(): return lax.ppermute((own + total).astype(BF), 'ctx', pairs)  51.1 us
    ppermute x10, starting transfers between devices, scan_step(): return lax.ppermute((own + total).astype(BF), 'ctx', pairs)  27.2 us
    ppermute x16, starting transfers between devices, ring_move(): return lax.ppermute(value, 'ctx', pairs)  24 us
    ppermute x16, waiting for transfers between devices, ring_move(): return lax.ppermute(value, 'ctx', pairs)  20.1 us
    unnamed x62, local copies, waits for them, and re-layouts  18.6 us
    ppermute x8, starting transfers between devices, swap(): return lax.ppermute(value, 'ctx', [(i, i ^ 1) for i in range(CTX)])  16.2 us
    ppermute x8, starting transfers between devices, head_move(): lax.ppermute(value, 'head', [(i, (i + step) % SIDE) for i in range(SIDE)])  14.1 us
  transfers between devices with their start and end apart: 42, of which 13 were waited for; matrix products, arithmetic and copies ran while one was open for 2% of the time, Pallas kernels for 34%

profile of v1, /device:TPU:1, one launch (start us, length us, event | category | flops | bytes accessed | tf_op | source)
XLA Modules:
  0.0 315.2 jit_solution(8306219600469794984)
XLA Ops:
  6.1 3.9 %collective-permute-start.4 = (bf16[4,512,128]{2,1,0:T(8,128)(2,1)S(1)}, bf16[4,512,128]{2,1,0:T(8,128)(2,1)S(1)}, u32[]{:S(2)}, u32[]{:S(2)}) collective-permute-start(bf16[4,512,128]{2,1,0:T(8,128)(2,1)S(1)} %copies.4.refs_0_), channel_id=1, source_target_pairs={{0,24},{4,100},{8,0},{12,108},{16,8},{20,116},{24,16},{28,124},{32... | collective-permute-start | bytes 1572872 | tf_op jit(solution)/shard_map/ppermute | solution.py:45
  13.1 3.0 collective-permute-done.4.refs_1_.refs_4_
  16.1 3.4 %collective-permute-done.3.refs_0_.refs_1_ = bf16[4,512,128]{2,1,0:T(8,128)(2,1)S(1)} collective-permute-done((bf16[4,512,128]{2,1,0:T(8,128)(2,1)S(1)}, bf16[4,512,128]{2,1,0:T(8,128)(2,1)S(1)}, u32[]{:S(2)}, u32[]{:S(2)}) %collective-permute-start.3) | collective-permute-done | bytes 524320 | tf_op jit(solution)/shard_map/ppermute | solution.py:45
  19.7 2.7 collective-permute-start.7
  27.8 2.7 collective-permute-start.11
  34.3 21.5 %collective-permute-done.1 = bf16[3,128,128]{2,1,0:T(8,128)(2,1)S(1)} collective-permute-done((bf16[3,128,128]{2,1,0:T(8,128)(2,1)S(1)}, bf16[3,128,128]{2,1,0:T(8,128)(2,1)S(1)}, u32[]{:S(2)}, u32[]{:S(2)}) %collective-permute-start.1) | collective-permute-done | bytes 98336 | tf_op jit(solution)/shard_map/ppermute | solution.py:65
  55.8 2.7 collective-permute-start.24
  59.0 3.9 %collective-permute-start.5 = (bf16[3,128,128]{2,1,0:T(8,128)(2,1)S(1)}, bf16[3,128,128]{2,1,0:T(8,128)(2,1)S(1)}, u32[]{:S(2)}, u32[]{:S(2)}) collective-permute-start(bf16[3,128,128]{2,1,0:T(8,128)(2,1)S(1)} %add_convert_fusion.5), channel_id=1, source_target_pairs={{0,16},{4,20},{8,24},{12,28},{16,32},{20,36},{24,40},{28,44},{32,4... | collective-permute-start | bytes 294920 | tf_op jit(solution)/shard_map/ppermute | solution.py:65
  65.8 64.6 %copies.7 = (bf16[8,512,128]{2,1,0:T(8,128)(2,1)}, bf16[8,512,128]{2,1,0:T(8,128)(2,1)}) custom-call(bf16[16,512,128]{2,1,0:T(8,128)(2,1)} %collective-permute-done.10.refs_0_.rest_1_, bf16[16,512,128]{2,1,0:T(8,128)(2,1)} %collective-permute-done.11.refs_1_.rest_4_), custom_call_target="tpu_custom_call" | custom-call | bytes 4194304 | tf_op jit(solution)/shard_map/copies/pallas_call | solution.py:84
  131.4 2.7 collective-permute-start.14
  134.1 6.3 %collective-permute-start.9 = (bf16[3,128,128]{2,1,0:T(8,128)(2,1)S(1)}, bf16[3,128,128]{2,1,0:T(8,128)(2,1)S(1)}, u32[]{:S(2)}, u32[]{:S(2)}) collective-permute-start(bf16[3,128,128]{2,1,0:T(8,128)(2,1)S(1)} %add_convert_fusion.4), channel_id=1, source_target_pairs={{0,32},{4,36},{8,40},{12,44},{16,48},{20,52},{24,56},{28,60},{32,6... | collective-permute-start | bytes 294920 | tf_op jit(solution)/shard_map/ppermute | solution.py:65
  143.3 2.7 collective-permute-start.26
  149.9 6.0 %grad_near.1.part = f32[1024,512]{1,0:T(8,128)S(1)} custom-call(s32[4]{0:T(128)S(1)} %and_select_fusion.20.order, bf16[1024,1024]{1,0:T(8,128)(2,1)} %own.1, bf16[1024,1024]{1,0:T(8,128)(2,1)S(1)} %copy-done.9, bf16[1024,1024]{1,0:T(8,128)(2,1)} %collective-permute-done.24.left, bf16[4096,512]{1,0:T(8,128)(2,1)S(1)} %copy-done, ...), custom_call_target="tpu_custom_call" | custom-call | flops 3221225472 | bytes 11534336 | tf_op jit(solution)/shard_map/grad_near/pallas_call | solution.py:385
  155.9 5.3 %collective-permute-start.16 = (bf16[8,512,128]{2,1,0:T(8,128)(2,1)}, bf16[8,512,128]{2,1,0:T(8,128)(2,1)}, u32[]{:S(2)}, u32[]{:S(2)}) collective-permute-start(bf16[8,512,128]{2,1,0:T(8,128)(2,1)} %collective-permute-done.13.rest_2_), channel_id=1, source_target_pairs={{0,4},{4,0},{8,12},{12,8},{16,20},{20,16},{24,28},{28,24},{32,36},... | collective-permute-start | bytes 3145736 | tf_op jit(solution)/shard_map/ppermute | solution.py:49
  163.8 5.6 %collective-permute-start.12 = (bf16[3,128,128]{2,1,0:T(8,128)(2,1)S(1)}, bf16[3,128,128]{2,1,0:T(8,128)(2,1)S(1)}, u32[]{:S(2)}, u32[]{:S(2)}) collective-permute-start(bf16[3,128,128]{2,1,0:T(8,128)(2,1)S(1)} %add_convert_fusion.3), channel_id=1, source_target_pairs={{0,64},{4,68},{8,72},{12,76},{16,80},{20,84},{24,88},{28,92},{32,9... | collective-permute-start | bytes 294920 | tf_op jit(solution)/shard_map/ppermute | solution.py:65
  169.4 4.3 %grad_far.1.g_ref = bf16[1024,512]{1,0:T(8,128)(2,1)S(1)} custom-call(s32[4]{0:T(128)S(1)} %and_select_fusion.20.order, f32[1024,512]{1,0:T(8,128)S(1)} %grad_near.1.part, bf16[512,1024]{1,0:T(8,128)(2,1)} %collective-permute-done.25.far_a, bf16[512,1024]{1,0:T(8,128)(2,1)} %collective-permute-done.26.far_b, bf16[4096,512]{1,0:T(8,128)(2,1)S(1)} %copy-done), custom_call_target="tpu_custom_call" | custom-call | flops 1073741824 | bytes 6291456 | tf_op jit(solution)/shard_map/grad_far/pallas_call | solution.py:417
  177.1 3.7 %linear_forward.1.base_ref = bf16[1024,512]{1,0:T(8,128)(2,1)S(1)} custom-call(bf16[1024,512]{1,0:T(8,128)(2,1)S(1)} %copy-done.10, bf16[1024,512]{1,0:T(8,128)(2,1)S(1)} %copy-done.3, bf16[1024,512]{1,0:T(8,128)(2,1)S(1)} %copy-done.5, f32[8,1024]{1,0:T(8,128)S(1)} %broadcast_in_dim.41.c_ref, bf16[2,3,128,128]{3,2,1,0:T(8,128)(2,1)S(1)} %copy.30.hi_ref, ...), custom_call_target="tpu_custom_call" | custom-call | flops 2400000000 | bytes 4194304 | tf_op jit(solution)/shard_map/linear_forward/pallas_call | solution.py:171
  180.9 11.7 %sparse_forward.1 = (bf16[1024,512]{1,0:T(8,128)(2,1)S(1)}, bf16[2,5,512,512]{3,2,1,0:T(8,128)(2,1)}, bf16[8,512,128]{2,1,0:T(8,128)(2,1)S(1)}, bf16[8,512,128]{2,1,0:T(8,128)(2,1)S(1)}) custom-call(s32[8,5]{1,0:T(8,128)S(1)} %stack.35.table, bf16[1024,512]{1,0:T(8,128)(2,1)S(1)} %copy-done.11, ...), custom_call_target="tpu_custom_call", output_to_operand_aliasing={{0}: (4, {})} | custom-call | flops 4000000000 | bytes 12582912 | tf_op jit(solution)/shard_map/sparse_forward/pallas_call | solution.py:265
  195.1 7.2 %sparse_backward.1 = (bf16[1024,512]{1,0:T(8,128)(2,1)}, f32[1024,128]{1,0:T(8,128)S(1)}, f32[1024,128]{1,0:T(8,128)S(1)}, bf16[8,512,128]{2,1,0:T(8,128)(2,1)S(1)}, bf16[8,512,128]{2,1,0:T(8,128)(2,1)}) custom-call(s32[1]{0:T(128)} %bitcast.2.core, bf16[1024,512]{1,0:T(8,128)(2,1)S(1)} %copy-done.11, bf16[1024,512]{1,0:T(8,128)(2,1)S(1)} %copy-done.3, ...), custom_call_target="tpu_custom_call" | custom-call | flops 8000000000 | bytes 12582912 | tf_op jit(solution)/shard_map/sparse_backward/pallas_call | solution.py:325
  205.0 6.1 %collective-permute-start.32 = (bf16[8,512,128]{2,1,0:T(8,128)(2,1)}, bf16[8,512,128]{2,1,0:T(8,128)(2,1)}, u32[]{:S(2)}, u32[]{:S(2)}) collective-permute-start(bf16[8,512,128]{2,1,0:T(8,128)(2,1)} %get-tuple-element.68), channel_id=1, source_target_pairs={{0,4},{4,0},{8,12},{12,8},{16,20},{20,16},{24,28},{28,24},{32,36},... | collective-permute-start | bytes 3145736 | tf_op jit(solution)/shard_map/ppermute | solution.py:49
  224.2 2.8 collective-permute-start.27
  227.1 2.7 out_far.1
  229.9 3.5 %collective-permute-start.20 = (bf16[512,1024]{1,0:T(8,128)(2,1)S(1)}, bf16[512,1024]{1,0:T(8,128)(2,1)S(1)}, u32[]{:S(2)}, u32[]{:S(2)}) collective-permute-start(bf16[512,1024]{1,0:T(8,128)(2,1)S(1)} %get-tuple-element.62), channel_id=1, source_target_pairs={{0,3},{1,0},{2,1},{3,2},{4,7},{5,4},{6,5},{7,6},{8,11},{9,8},{10,9... | collective-permute-start | bytes 3145736 | tf_op jit(solution)/shard_map/ppermute | solution.py:53
  234.7 3.1 back_near.1
  241.9 23.5 %collective-permute-done.29 = bf16[3,128,128]{2,1,0:T(8,128)(2,1)S(1)} collective-permute-done((bf16[3,128,128]{2,1,0:T(8,128)(2,1)S(1)}, bf16[3,128,128]{2,1,0:T(8,128)(2,1)S(1)}, u32[]{:S(2)}, u32[]{:S(2)}) %collective-permute-start.29) | collective-permute-done | bytes 98336 | tf_op jit(solution)/shard_map/ppermute | solution.py:65
  266.9 3.7 %out_near.1 = (bf16[1024,1024]{1,0:T(8,128)(2,1)S(1)}, bf16[1024,1024]{1,0:T(8,128)(2,1)S(1)}) custom-call(s32[4]{0:T(128)S(1)} %and_select_fusion.20.order, bf16[1024,512]{1,0:T(8,128)(2,1)S(1)} %get-tuple-element.60.a.o_ref, bf16[4096,512]{1,0:T(8,128)(2,1)S(1)} %copy-done.1, bf16[4096,512]{1,0:T(8,128)(2,1)S(1)} %copy-done.1, ...), custom_call_target="tpu_custom_call" | custom-call | flops 2147483648 | bytes 7340032 | tf_op jit(solution)/shard_map/out_near/pallas_call | solution.py:468
  271.0 3.4 %collective-permute-start.22 = (bf16[1024,1024]{1,0:T(8,128)(2,1)S(1)}, bf16[1024,1024]{1,0:T(8,128)(2,1)S(1)}, u32[]{:S(2)}, u32[]{:S(2)}) collective-permute-start(bf16[1024,1024]{1,0:T(8,128)(2,1)S(1)} %get-tuple-element.64), channel_id=1, source_target_pairs={{0,3},{1,0},{2,1},{3,2},{4,7},{5,4},{6,5},{7,6},{8,11},{9,8},{10,9... | collective-permute-start | bytes 6291464 | tf_op jit(solution)/shard_map/ppermute | solution.py:53
  275.7 6.1 %collective-permute-done.31 = bf16[3,128,128]{2,1,0:T(8,128)(2,1)S(1)} collective-permute-done((bf16[3,128,128]{2,1,0:T(8,128)(2,1)S(1)}, bf16[3,128,128]{2,1,0:T(8,128)(2,1)S(1)}, u32[]{:S(2)}, u32[]{:S(2)}) %collective-permute-start.31) | collective-permute-done | bytes 98336 | tf_op jit(solution)/shard_map/ppermute | solution.py:65
  282.0 7.5 %linear_backward.1 = (bf16[1024,512]{1,0:T(8,128)(2,1)}, bf16[1024,512]{1,0:T(8,128)(2,1)}, bf16[1024,512]{1,0:T(8,128)(2,1)}) custom-call(bf16[1024,512]{1,0:T(8,128)(2,1)S(1)} %copy-done.13, bf16[1024,512]{1,0:T(8,128)(2,1)S(1)} %copy-done.3, bf16[1024,512]{1,0:T(8,128)(2,1)S(1)} %copy-done.5, ...), custom_call_target="tpu_custom_call", output_to_operand_aliasing={{0}: (9, {})} | custom-call | flops 5000000000 | bytes 8388608 | tf_op jit(solution)/shard_map/linear_backward/pallas_call | solution.py:201
  294.8 4.1 %collective-permute-done.37.ra = bf16[2,512,128]{2,1,0:T(8,128)(2,1)S(1)} collective-permute-done((bf16[2,512,128]{2,1,0:T(8,128)(2,1)S(1)}, bf16[2,512,128]{2,1,0:T(8,128)(2,1)S(1)}, u32[]{:S(2)}, u32[]{:S(2)}) %collective-permute-start.37) | collective-permute-done | bytes 262176 | tf_op jit(solution)/shard_map/ppermute | solution.py:45
  303.2 6.6 %collective-permute-done.39.r1 = bf16[4,512,128]{2,1,0:T(8,128)(2,1)S(1)} collective-permute-done((bf16[4,512,128]{2,1,0:T(8,128)(2,1)S(1)}, bf16[4,512,128]{2,1,0:T(8,128)(2,1)S(1)}, u32[]{:S(2)}, u32[]{:S(2)}) %collective-permute-start.39) | collective-permute-done | bytes 524320 | tf_op jit(solution)/shard_map/ppermute | solution.py:45
  310.6 3.6 %out_home.1 = bf16[1024,1024]{1,0:T(8,128)(2,1)} custom-call(s32[4]{0:T(128)S(1)} %and_select_fusion.20.order, bf16[1024,512]{1,0:T(8,128)(2,1)S(1)} %get-tuple-element.60.a.o_ref, bf16[4096,512]{1,0:T(8,128)(2,1)S(1)} %copy-done.1, bf16[1024,1024]{1,0:T(8,128)(2,1)S(1)} %collective-permute-done.21.r1, bf16[1024,1024]{1,0:T(8,128)(2,1)S(1)} %collective-permute-done.22.r3), custom_call_target="tpu_custom_call" | custom-call | flops 1073741824 | bytes 5242880 | tf_op jit(solution)/shard_map/out_home/pallas_call | solution.py:468
  (177 shorter events, 73.1 us)
Async XLA Ops:
  6.1 10.0 %collective-permute-start.4 = (bf16[4,512,128]{2,1,0:T(8,128)(2,1)S(1)}, bf16[4,512,128]{2,1,0:T(8,128)(2,1)S(1)}, u32[]{:S(2)}, u32[]{:S(2)}) collective-permute-start(bf16[4,512,128]{2,1,0:T(8,128)(2,1)S(1)} %copies.4.refs_0_), channel_id=1, source_target_pairs={{0,24},{4,100},{8,0},{12,108},{16,8},{20,116},{24,16},{28,124},{32... | collective-permute-start | bytes 1572872 | tf_op jit(solution)/shard_map/ppermute | solution.py:45
  10.0 9.5 %collective-permute-start.3 = (bf16[4,512,128]{2,1,0:T(8,128)(2,1)S(1)}, bf16[4,512,128]{2,1,0:T(8,128)(2,1)S(1)}, u32[]{:S(2)}, u32[]{:S(2)}) collective-permute-start(bf16[4,512,128]{2,1,0:T(8,128)(2,1)S(1)} %copies.4.refs_0_), channel_id=1, source_target_pairs={{0,8},{4,36},{8,16},{12,44},{16,24},{20,52},{24,0},{28,60},{32,40}... | collective-permute-start | bytes 1572872 | tf_op jit(solution)/shard_map/ppermute | solution.py:45
  10.0 49.0 %collective-permute-start.23 = (bf16[1024,1024]{1,0:T(8,128)(2,1)}, bf16[1024,1024]{1,0:T(8,128)(2,1)S(1)}, u32[]{:S(2)}, u32[]{:S(2)}) collective-permute-start(bf16[1024,1024]{1,0:T(8,128)(2,1)} %own.1), channel_id=1, source_target_pairs={{0,1},{1,2},{2,3},{3,0},{4,5},{5,6},{6,7},{7,4},{8,9},{9,10},{10,1... | collective-permute-start | bytes 6291464 | tf_op jit(solution)/shard_map/ppermute | solution.py:53
  22.4 10.6 %collective-permute-start = (bf16[3,128,128]{2,1,0:T(8,128)(2,1)S(1)}, bf16[3,128,128]{2,1,0:T(8,128)(2,1)S(1)}, u32[]{:S(2)}, u32[]{:S(2)}) collective-permute-start(bf16[3,128,128]{2,1,0:T(8,128)(2,1)S(1)} %get-tuple-element.96), channel_id=1, source_target_pairs={{0,4},{4,8},{8,12},{12,16},{16,20},{20,24},{24,28},{28,32},{32,36}... | collective-permute-start | bytes 294920 | tf_op jit(solution)/shard_map/ppermute | solution.py:65
  27.8 38.0 %collective-permute-start.11 = (bf16[16,512,128]{2,1,0:T(8,128)(2,1)}, bf16[16,512,128]{2,1,0:T(8,128)(2,1)}, u32[]{:S(2)}, u32[]{:S(2)}) collective-permute-start(bf16[16,512,128]{2,1,0:T(8,128)(2,1)} %copies.6.rest_0_), channel_id=1, source_target_pairs={{0,96},{4,28},{8,104},{12,4},{16,112},{20,12},{24,120},{28,20},{32... | collective-permute-start | bytes 6291464 | tf_op jit(solution)/shard_map/ppermute | solution.py:45
  30.5 35.3 %collective-permute-start.10 = (bf16[16,512,128]{2,1,0:T(8,128)(2,1)}, bf16[16,512,128]{2,1,0:T(8,128)(2,1)}, u32[]{:S(2)}, u32[]{:S(2)}) collective-permute-start(bf16[16,512,128]{2,1,0:T(8,128)(2,1)} %copies.6.rest_0_), channel_id=1, source_target_pairs={{0,32},{4,12},{8,40},{12,20},{16,48},{20,28},{24,56},{28,4},{32,64... | collective-permute-start | bytes 6291464 | tf_op jit(solution)/shard_map/ppermute | solution.py:45
  30.5 103.6 %collective-permute-start.8 = (bf16[16,512,128]{2,1,0:T(8,128)(2,1)}, bf16[16,512,128]{2,1,0:T(8,128)(2,1)}, u32[]{:S(2)}, u32[]{:S(2)}) collective-permute-start(bf16[16,512,128]{2,1,0:T(8,128)(2,1)} %copies.6.rest_0_), channel_id=1, source_target_pairs={{0,4},{4,0},{8,12},{12,8},{16,20},{20,16},{24,28},{28,24},{32,36},... | collective-permute-start | bytes 6291464 | tf_op jit(solution)/shard_map/ppermute | solution.py:49
  33.0 22.8 %collective-permute-start.1 = (bf16[3,128,128]{2,1,0:T(8,128)(2,1)S(1)}, bf16[3,128,128]{2,1,0:T(8,128)(2,1)S(1)}, u32[]{:S(2)}, u32[]{:S(2)}) collective-permute-start(bf16[3,128,128]{2,1,0:T(8,128)(2,1)S(1)} %fusion.2), channel_id=1, source_target_pairs={{0,8},{4,12},{8,16},{12,20},{16,24},{20,28},{24,32},{28,36},{32,40... | collective-permute-start | bytes 294920 | tf_op jit(solution)/shard_map/ppermute | solution.py:65
  55.8 84.6 %collective-permute-start.24 = (bf16[1024,1024]{1,0:T(8,128)(2,1)}, bf16[1024,1024]{1,0:T(8,128)(2,1)}, u32[]{:S(2)}, u32[]{:S(2)}) collective-permute-start(bf16[1024,1024]{1,0:T(8,128)(2,1)} %own.1), channel_id=1, source_target_pairs={{0,3},{1,0},{2,1},{3,2},{4,7},{5,4},{6,5},{7,6},{8,11},{9,8},{10,9... | collective-permute-start | bytes 6291464 | tf_op jit(solution)/shard_map/ppermute | solution.py:53
  65.3 75.2 %collective-permute-start.25 = (bf16[512,1024]{1,0:T(8,128)(2,1)}, bf16[512,1024]{1,0:T(8,128)(2,1)}, u32[]{:S(2)}, u32[]{:S(2)}) collective-permute-start(bf16[512,1024]{1,0:T(8,128)(2,1)} %slice.28), channel_id=1, source_target_pairs={{0,1},{1,2},{2,3},{3,0},{4,5},{5,6},{6,7},{7,4},{8,9},{9,10},{10,1... | collective-permute-start | bytes 3145736 | tf_op jit(solution)/shard_map/ppermute | solution.py:53
  130.4 25.5 %collective-permute-start.13 = (bf16[8,512,128]{2,1,0:T(8,128)(2,1)}, bf16[8,512,128]{2,1,0:T(8,128)(2,1)}, u32[]{:S(2)}, u32[]{:S(2)}) collective-permute-start(bf16[8,512,128]{2,1,0:T(8,128)(2,1)} %get-tuple-element.57), channel_id=1, source_target_pairs={{0,32},{4,12},{8,40},{12,20},{16,48},{20,28},{24,56},{28,4},{32,64... | collective-permute-start | bytes 3145736 | tf_op jit(solution)/shard_map/ppermute | solution.py:45
  131.4 29.9 %collective-permute-start.14 = (bf16[8,512,128]{2,1,0:T(8,128)(2,1)}, bf16[8,512,128]{2,1,0:T(8,128)(2,1)}, u32[]{:S(2)}, u32[]{:S(2)}) collective-permute-start(bf16[8,512,128]{2,1,0:T(8,128)(2,1)} %get-tuple-element.58), channel_id=1, source_target_pairs={{0,96},{4,28},{8,104},{12,4},{16,112},{20,12},{24,120},{28,20},{32... | collective-permute-start | bytes 3145736 | tf_op jit(solution)/shard_map/ppermute | solution.py:45
  134.1 9.2 %collective-permute-start.9 = (bf16[3,128,128]{2,1,0:T(8,128)(2,1)S(1)}, bf16[3,128,128]{2,1,0:T(8,128)(2,1)S(1)}, u32[]{:S(2)}, u32[]{:S(2)}) collective-permute-start(bf16[3,128,128]{2,1,0:T(8,128)(2,1)S(1)} %add_convert_fusion.4), channel_id=1, source_target_pairs={{0,32},{4,36},{8,40},{12,44},{16,48},{20,52},{24,56},{28,60},{32,6... | collective-permute-start | bytes 294920 | tf_op jit(solution)/shard_map/ppermute | solution.py:65
  140.4 40.5 %collective-permute-start.18 = (bf16[16,512,128]{2,1,0:T(8,128)(2,1)}, bf16[16,512,128]{2,1,0:T(8,128)(2,1)}, u32[]{:S(2)}, u32[]{:S(2)}) collective-permute-start(bf16[16,512,128]{2,1,0:T(8,128)(2,1)} %collective-permute-done.11.refs_1_.rest_4_), channel_id=1, source_target_pairs={{0,4},{4,0},{8,12},{12,8},{16,20},{20,16},{24,28},{28,24},{32,36},... | collective-permute-start | bytes 6291464 | tf_op jit(solution)/shard_map/ppermute | solution.py:49
  140.5 40.4 %collective-permute-start.15 = (bf16[16,512,128]{2,1,0:T(8,128)(2,1)}, bf16[16,512,128]{2,1,0:T(8,128)(2,1)}, u32[]{:S(2)}, u32[]{:S(2)}) collective-permute-start(bf16[16,512,128]{2,1,0:T(8,128)(2,1)} %collective-permute-done.10.refs_0_.rest_1_), channel_id=1, source_target_pairs={{0,4},{4,0},{8,12},{12,8},{16,20},{20,16},{24,28},{28,24},{32,36},... | collective-permute-start | bytes 6291464 | tf_op jit(solution)/shard_map/ppermute | solution.py:49
  143.3 20.5 %collective-permute-start.26 = (bf16[512,1024]{1,0:T(8,128)(2,1)}, bf16[512,1024]{1,0:T(8,128)(2,1)}, u32[]{:S(2)}, u32[]{:S(2)}) collective-permute-start(bf16[512,1024]{1,0:T(8,128)(2,1)} %slice.29), channel_id=1, source_target_pairs={{0,3},{1,0},{2,1},{3,2},{4,7},{5,4},{6,5},{7,6},{8,11},{9,8},{10,9... | collective-permute-start | bytes 3145736 | tf_op jit(solution)/shard_map/ppermute | solution.py:53
  155.9 24.9 %collective-permute-start.16 = (bf16[8,512,128]{2,1,0:T(8,128)(2,1)}, bf16[8,512,128]{2,1,0:T(8,128)(2,1)}, u32[]{:S(2)}, u32[]{:S(2)}) collective-permute-start(bf16[8,512,128]{2,1,0:T(8,128)(2,1)} %collective-permute-done.13.rest_2_), channel_id=1, source_target_pairs={{0,4},{4,0},{8,12},{12,8},{16,20},{20,16},{24,28},{28,24},{32,36},... | collective-permute-start | bytes 3145736 | tf_op jit(solution)/shard_map/ppermute | solution.py:49
  161.2 19.6 %collective-permute-start.17 = (bf16[8,512,128]{2,1,0:T(8,128)(2,1)}, bf16[8,512,128]{2,1,0:T(8,128)(2,1)}, u32[]{:S(2)}, u32[]{:S(2)}) collective-permute-start(bf16[8,512,128]{2,1,0:T(8,128)(2,1)} %collective-permute-done.14.rest_3_), channel_id=1, source_target_pairs={{0,4},{4,0},{8,12},{12,8},{16,20},{20,16},{24,28},{28,24},{32,36},... | collective-permute-start | bytes 3145736 | tf_op jit(solution)/shard_map/ppermute | solution.py:49
  163.8 10.9 %collective-permute-start.12 = (bf16[3,128,128]{2,1,0:T(8,128)(2,1)S(1)}, bf16[3,128,128]{2,1,0:T(8,128)(2,1)S(1)}, u32[]{:S(2)}, u32[]{:S(2)}) collective-permute-start(bf16[3,128,128]{2,1,0:T(8,128)(2,1)S(1)} %add_convert_fusion.3), channel_id=1, source_target_pairs={{0,64},{4,68},{8,72},{12,76},{16,80},{20,84},{24,88},{28,92},{32,9... | collective-permute-start | bytes 294920 | tf_op jit(solution)/shard_map/ppermute | solution.py:65
  217.2 17.5 %collective-permute-start.33 = (bf16[8,512,128]{2,1,0:T(8,128)(2,1)S(1)}, bf16[8,512,128]{2,1,0:T(8,128)(2,1)S(1)}, u32[]{:S(2)}, u32[]{:S(2)}) collective-permute-start(bf16[8,512,128]{2,1,0:T(8,128)(2,1)S(1)} %get-tuple-element.71), channel_id=1, source_target_pairs={{0,32},{4,12},{8,40},{12,20},{16,48},{20,28},{24,56},{28,4},{32,64... | collective-permute-start | bytes 3145736 | tf_op jit(solution)/shard_map/ppermute | solution.py:45
  217.3 17.4 %collective-permute-start.34 = (bf16[8,512,128]{2,1,0:T(8,128)(2,1)S(1)}, bf16[8,512,128]{2,1,0:T(8,128)(2,1)S(1)}, u32[]{:S(2)}, u32[]{:S(2)}) collective-permute-start(bf16[8,512,128]{2,1,0:T(8,128)(2,1)S(1)} %get-tuple-element.72), channel_id=1, source_target_pairs={{0,96},{4,28},{8,104},{12,4},{16,112},{20,12},{24,120},{28,20},{32... | collective-permute-start | bytes 3145736 | tf_op jit(solution)/shard_map/ppermute | solution.py:45
  224.2 9.1 %collective-permute-start.27 = (bf16[3,128,128]{2,1,0:T(8,128)(2,1)S(1)}, bf16[3,128,128]{2,1,0:T(8,128)(2,1)S(1)}, u32[]{:S(2)}, u32[]{:S(2)}) collective-permute-start(bf16[3,128,128]{2,1,0:T(8,128)(2,1)S(1)} %get-tuple-element.94), channel_id=1, source_target_pairs={{4,0},{8,4},{12,8},{16,12},{20,16},{24,20},{28,24},{32,28},{36,32}... | collective-permute-start | bytes 294920 | tf_op jit(solution)/shard_map/ppermute | solution.py:65
  229.8 37.1 %collective-permute-start.19 = (bf16[512,1024]{1,0:T(8,128)(2,1)S(1)}, bf16[512,1024]{1,0:T(8,128)(2,1)S(1)}, u32[]{:S(2)}, u32[]{:S(2)}) collective-permute-start(bf16[512,1024]{1,0:T(8,128)(2,1)S(1)} %get-tuple-element.61), channel_id=1, source_target_pairs={{0,1},{1,2},{2,3},{3,0},{4,5},{5,6},{6,7},{7,4},{8,9},{9,10},{10,1... | collective-permute-start | bytes 3145736 | tf_op jit(solution)/shard_map/ppermute | solution.py:53
  229.9 37.0 %collective-permute-start.20 = (bf16[512,1024]{1,0:T(8,128)(2,1)S(1)}, bf16[512,1024]{1,0:T(8,128)(2,1)S(1)}, u32[]{:S(2)}, u32[]{:S(2)}) collective-permute-start(bf16[512,1024]{1,0:T(8,128)(2,1)S(1)} %get-tuple-element.62), channel_id=1, source_target_pairs={{0,3},{1,0},{2,1},{3,2},{4,7},{5,4},{6,5},{7,6},{8,11},{9,8},{10,9... | collective-permute-start | bytes 3145736 | tf_op jit(solution)/shard_map/ppermute | solution.py:53
  237.8 51.7 %collective-permute-start.35 = (bf16[16,512,128]{2,1,0:T(8,128)(2,1)S(1)}, bf16[16,512,128]{2,1,0:T(8,128)(2,1)S(1)}, u32[]{:S(2)}, u32[]{:S(2)}) collective-permute-start(bf16[16,512,128]{2,1,0:T(8,128)(2,1)S(1)} %get-tuple-element.78), channel_id=1, source_target_pairs={{0,32},{4,12},{8,40},{12,20},{16,48},{20,28},{24,56},{28,4},{32,64... | collective-permute-start | bytes 6291464 | tf_op jit(solution)/shard_map/ppermute | solution.py:45
  239.9 49.5 %collective-permute-start.36 = (bf16[16,512,128]{2,1,0:T(8,128)(2,1)S(1)}, bf16[16,512,128]{2,1,0:T(8,128)(2,1)S(1)}, u32[]{:S(2)}, u32[]{:S(2)}) collective-permute-start(bf16[16,512,128]{2,1,0:T(8,128)(2,1)S(1)} %get-tuple-element.81), channel_id=1, source_target_pairs={{0,96},{4,28},{8,104},{12,4},{16,112},{20,12},{24,120},{28,20},{32... | collective-permute-start | bytes 6291464 | tf_op jit(solution)/shard_map/ppermute | solution.py:45
  240.6 24.8 %collective-permute-start.29 = (bf16[3,128,128]{2,1,0:T(8,128)(2,1)S(1)}, bf16[3,128,128]{2,1,0:T(8,128)(2,1)S(1)}, u32[]{:S(2)}, u32[]{:S(2)}) collective-permute-start(bf16[3,128,128]{2,1,0:T(8,128)(2,1)S(1)} %add_convert_fusion.2), channel_id=1, source_target_pairs={{16,0},{20,4},{24,8},{28,12},{32,16},{36,20},{40,24},{44,28},{48,3... | collective-permute-start | bytes 294920 | tf_op jit(solution)/shard_map/ppermute | solution.py:65
  265.4 8.9 %collective-permute-start.30 = (bf16[3,128,128]{2,1,0:T(8,128)(2,1)S(1)}, bf16[3,128,128]{2,1,0:T(8,128)(2,1)S(1)}, u32[]{:S(2)}, u32[]{:S(2)}) collective-permute-start(bf16[3,128,128]{2,1,0:T(8,128)(2,1)S(1)} %add_convert_fusion.1), channel_id=1, source_target_pairs={{32,0},{36,4},{40,8},{44,12},{48,16},{52,20},{56,24},{60,28},{64,3... | collective-permute-start | bytes 294920 | tf_op jit(solution)/shard_map/ppermute | solution.py:65
  270.6 40.0 %collective-permute-start.21 = (bf16[1024,1024]{1,0:T(8,128)(2,1)S(1)}, bf16[1024,1024]{1,0:T(8,128)(2,1)S(1)}, u32[]{:S(2)}, u32[]{:S(2)}) collective-permute-start(bf16[1024,1024]{1,0:T(8,128)(2,1)S(1)} %get-tuple-element.63), channel_id=1, source_target_pairs={{0,1},{1,2},{2,3},{3,0},{4,5},{5,6},{6,7},{7,4},{8,9},{9,10},{10,1... | collective-permute-start | bytes 6291464 | tf_op jit(solution)/shard_map/ppermute | solution.py:53
  271.0 39.7 %collective-permute-start.22 = (bf16[1024,1024]{1,0:T(8,128)(2,1)S(1)}, bf16[1024,1024]{1,0:T(8,128)(2,1)S(1)}, u32[]{:S(2)}, u32[]{:S(2)}) collective-permute-start(bf16[1024,1024]{1,0:T(8,128)(2,1)S(1)} %get-tuple-element.64), channel_id=1, source_target_pairs={{0,3},{1,0},{2,1},{3,2},{4,7},{5,4},{6,5},{7,6},{8,11},{9,8},{10,9... | collective-permute-start | bytes 6291464 | tf_op jit(solution)/shard_map/ppermute | solution.py:53
  300.4 9.3 %collective-permute-start.39 = (bf16[4,512,128]{2,1,0:T(8,128)(2,1)S(1)}, bf16[4,512,128]{2,1,0:T(8,128)(2,1)S(1)}, u32[]{:S(2)}, u32[]{:S(2)}) collective-permute-start(bf16[4,512,128]{2,1,0:T(8,128)(2,1)S(1)} %get-tuple-element.87), channel_id=1, source_target_pairs={{0,8},{4,36},{8,16},{12,44},{16,24},{20,52},{24,0},{28,60},{32,40}... | collective-permute-start | bytes 1572872 | tf_op jit(solution)/shard_map/ppermute | solution.py:45
  300.6 9.2 %collective-permute-start.40 = (bf16[4,512,128]{2,1,0:T(8,128)(2,1)S(1)}, bf16[4,512,128]{2,1,0:T(8,128)(2,1)S(1)}, u32[]{:S(2)}, u32[]{:S(2)}) collective-permute-start(bf16[4,512,128]{2,1,0:T(8,128)(2,1)S(1)} %get-tuple-element.88), channel_id=1, source_target_pairs={{0,24},{4,100},{8,0},{12,108},{16,8},{20,116},{24,16},{28,124},{32... | collective-permute-start | bytes 1572872 | tf_op jit(solution)/shard_map/ppermute | solution.py:45
  (41 other events, 255.0 us)

commit v2 on v0

v2 whole, which is shorter than its diff:
```python
import functools
import math

import jax
import jax.numpy as jnp
from jax import lax
from jax.experimental import pallas as pl
from jax.experimental.pallas import tpu as pltpu
from jax.sharding import PartitionSpec as P

HD = 128
LIN = 3
LISTED = 4
BLOCK = 512
SIDE = 4
CORES = 2
CTX = SIDE * SIDE * CORES
SCALING = 1.0 / math.sqrt(HD)
BF = jnp.bfloat16
F32 = jnp.float32
MIB = 1 << 20
COSTS = 1.0
HALF = LIN * HD // CORES
UNIT = 4 * BLOCK + HALF
FRONT = 2 * BLOCK + HALF
LINE = 4 * 4 * BLOCK + 2 * HALF
MID = 8 * BLOCK
TILE = (BLOCK, HD)


def dot(a, b, ca, cb):
    return lax.dot_general(a, b, (((ca,), (cb,)), ((), ())), preferred_element_type=F32)


def params(mib):
    return pltpu.CompilerParams(vmem_limit_bytes=mib * MIB)


def cost(flops, nbytes):
    return pl.CostEstimate(flops=int(flops * COSTS), bytes_accessed=int(nbytes * COSTS), transcendentals=0)


def ring_move(value, axis, step):
    pairs = []
    for z in range(SIDE):
        for x in range(SIDE):
            for c in range(CORES):
                dx, dz = (step, 0) if axis == c else (0, step)
                to = (((z + dz) % SIDE) * SIDE + (x + dx) % SIDE) * CORES + c
                pairs.append(((z * SIDE + x) * CORES + c, to))
    return lax.ppermute(value, "ctx", pairs)


def swap(value):
    return lax.ppermute(value, "ctx", [(i, i ^ 1) for i in range(CTX)])


def copies_kernel(moves, n_in, n_deps, *refs):
    ins, outs, sems = refs[:n_in], refs[n_in + n_deps : -1], refs[-1]
    copies = [
        pltpu.make_async_copy(
            ins[i].at[pl.ds(i0, n)], outs[o].at[pl.ds(o0, n)], sems.at[m]
        )
        for m, (i, i0, o, o0, n) in enumerate(moves)
    ]
    for copy in copies:
        copy.start()
    for copy in copies:
        copy.wait()


def copies(inputs, sizes, moves, deps=()):
    anywhere = pl.BlockSpec(memory_space=pl.ANY)
    return pl.pallas_call(
        functools.partial(copies_kernel, moves, len(inputs), len(deps)),
        in_specs=[anywhere] * (len(inputs) + len(deps)),
        out_specs=[pl.BlockSpec(memory_space=pltpu.VMEM)] * len(sizes),
        out_shape=[jax.ShapeDtypeStruct((n,) + inputs[0].shape[1:], BF) for n in sizes],
        scratch_shapes=[pltpu.SemaphoreType.DMA((len(moves),))],
        compiler_params=params(16),
        cost_estimate=cost(0, sum(m[4] for m in moves) * math.prod(inputs[0].shape[1:]) * 4),
        name="copies",
    )(*inputs, *deps)


def halves(right, left, n, deps=()):
    m = left.shape[0] - n
    return copies([right, left], [n, m], [(0, 0, 0, 0, n), (1, n, 1, 0, m)], deps)


def drop(kernel, n_in, n_deps, *refs):
    kernel(*refs[:n_in], *refs[n_in + n_deps :])


ANY = pl.BlockSpec(memory_space=pl.ANY)
VM = pl.BlockSpec(memory_space=pltpu.VMEM)
SM = pl.BlockSpec(memory_space=pltpu.SMEM)


def whole_call(kernel, scalars, operands, outs, name, deps=(), scratch=(), flops=1e6):
    outs = [jax.ShapeDtypeStruct(*o) for o in outs]
    nbytes = sum(math.prod(o.shape) * o.dtype.itemsize for o in [*operands, *outs])
    n_in = len(scalars) + len(operands)
    return pl.pallas_call(
        functools.partial(drop, kernel, n_in, len(deps)),
        in_specs=[SM] * len(scalars) + [VM] * len(operands) + [ANY] * len(deps),
        out_specs=[VM] * len(outs),
        out_shape=outs,
        scratch_shapes=list(scratch),
        compiler_params=params(32),
        cost_estimate=cost(flops, nbytes),
        name=name,
    )(*scalars, *operands, *deps)


def causal_mask():
    s = lax.broadcasted_iota(jnp.int32, (BLOCK, BLOCK), 0)
    u = lax.broadcasted_iota(jnp.int32, (BLOCK, BLOCK), 1)
    return s <= u


def adjoint_kernel(q_ref, g_ref, c_ref, out_ref):
    qt = (q_ref[...].astype(F32).T * c_ref[0:1, :]).astype(BF)
    out_ref[0, 0] = dot(qt, g_ref[...], 1, 0)


def tile_spec():
    return pl.BlockSpec(TILE, lambda i, h: (i, h))


def scale_spec():
    return pl.BlockSpec((8, BLOCK), lambda i, h: (0, i))


def state_spec():
    return pl.BlockSpec((1, 1, HD, HD), lambda i, h: (i, h, 0, 0))


def block_adjoints(queries, grads, scale):
    return pl.pallas_call(
        adjoint_kernel,
        grid=(2, LIN),
        in_specs=[tile_spec(), tile_spec(), scale_spec()],
        out_specs=state_spec(),
        out_shape=jax.ShapeDtypeStruct((2, LIN, HD, HD), F32),
        compiler_params=params(16),
        cost_estimate=cost(1e8, 2 * MIB),
        name="block_adjoints",
    )(queries, grads, scale)


def split(value):
    high = value.astype(BF)
    return high, (value - high.astype(F32)).astype(BF)


def linear_forward_kernel(q_ref, k_ref, v_ref, c_ref, s_ref, out_ref):
    q, k, v, c = q_ref[...], k_ref[...], v_ref[...], c_ref[0:1, :]
    weights = jnp.where(causal_mask(), dot(k, q, 1, 1) * c, 0.0).astype(BF)
    hi, lo = split(s_ref[0, 0].T)
    out = dot(v, weights, 0, 0) + c * (dot(hi, q, 1, 1) + dot(lo, q, 1, 1))
    out_ref[...] = out.T.astype(BF)


def linear_forward(queries, keys, values, scale, before):
    return pl.pallas_call(
        linear_forward_kernel,
        grid=(2, LIN),
        in_specs=[tile_spec()] * 3 + [scale_spec(), state_spec()],
        out_specs=tile_spec(),
        out_shape=jax.ShapeDtypeStruct(queries.shape, BF),
        compiler_params=params(24),
        cost_estimate=cost(2.4e9, 4 * MIB),
        name="linear_forward",
    )(queries, keys, values, scale, before)


def linear_backward_kernel(
    q_ref, k_ref, v_ref, g_ref, c_ref, s_ref, b0, b1, b2, dep, dq_ref, dk_ref, dv_ref
):
    q, k, v, g, c = q_ref[...], k_ref[...], v_ref[...], g_ref[...], c_ref[0:1, :]
    mask = causal_mask()
    grad_weights = jnp.where(mask, dot(v, g, 1, 1) * c, 0.0).astype(BF)
    hi, lo = split(s_ref[0, 0])
    dq = dot(k, grad_weights, 0, 0) + c * (dot(hi, g, 1, 1) + dot(lo, g, 1, 1))
    dq_ref[...] = dq.T.astype(BF)
    dk_ref[...] = dot(grad_weights, q, 1, 0)
    weights = jnp.where(mask, dot(k, q, 1, 1) * c, 0.0).astype(BF)
    dv_ref[...] = dot(weights, g, 1, 0)


def linear_backward(queries, keys, values, grads, scale, before, bases, dep):
    shape = queries.shape
    return pl.pallas_call(
        linear_backward_kernel,
        grid=(2, LIN),
        in_specs=[tile_spec()] * 4 + [scale_spec(), state_spec()] + [ANY] * 4,
        out_specs=[tile_spec()] * 3,
        out_shape=[jax.ShapeDtypeStruct(shape, t) for t in (BF, F32, F32)],
        input_output_aliases={6: 0, 7: 1, 8: 2},
        compiler_params=params(24),
        cost_estimate=cost(5e9, 9 * MIB),
        name="linear_backward",
    )(queries, keys, values, grads, scale, before, *bases, dep)


def sparse_forward_kernel(table, q_ref, k_ref, v_ref, base_ref, dep, *rest):
    pieces = rest[:10]
    out_ref, p_ref, kf_ref, vf_ref, s_ref, sems = rest[10:]
    step = pl.program_id(0)
    for r in range(LISTED):
        row = step * LISTED + r
        for j in range(10):

            @pl.when(table[row, 0] == j)
            def _():
                pltpu.make_async_copy(pieces[j].at[pl.ds(pl.multiple_of(table[row, 1] * HD, HD), BLOCK)], kf_ref.at[r], sems.at[0, r]).start()

            @pl.when(table[row, 2] == j)
            def _():
                pltpu.make_async_copy(pieces[j].at[pl.ds(pl.multiple_of(table[row, 3] * HD, HD), BLOCK)], vf_ref.at[r], sems.at[1, r]).start()

    q = q_ref[...]
    s = jnp.where(causal_mask(), dot(k_ref[...], q, 1, 1) * SCALING, -1e30)
    s_ref[0] = s
    peak = jnp.max(s, axis=0, keepdims=True)
    for r in range(LISTED):
        pltpu.make_async_copy(pieces[0].at[pl.ds(0, BLOCK)], kf_ref.at[r], sems.at[0, r]).wait()
        bias = jnp.where(table[step * LISTED + r, 4] == 1, 0.0, -1e30).astype(F32)
        s = dot(kf_ref[r], q, 1, 1) * SCALING + bias
        s_ref[r + 1] = s
        peak = jnp.maximum(peak, jnp.max(s, axis=0, keepdims=True))
    total = jnp.zeros((1, BLOCK), F32)
    for r in range(LISTED + 1):
        e = jnp.exp(s_ref[r] - peak)
        s_ref[r] = e
        total = total + jnp.sum(e, axis=0, keepdims=True)
    inverse = 1.0 / total
    out = jnp.zeros((HD, BLOCK), F32)
    for r in range(LISTED + 1):
        p = (s_ref[r] * inverse).astype(BF)
        p_ref[0, r] = p
        if r == 0:
            value = v_ref[...]
        else:
            pltpu.make_async_copy(pieces[0].at[pl.ds(0, BLOCK)], vf_ref.at[r - 1], sems.at[1, r - 1]).wait()
            value = vf_ref[r - 1]
        out = out + dot(value, p, 0, 0)
    out_ref[...] = out.T.astype(BF)


def sparse_forward(table, queries, keys, values, base, dep, pieces):
    column = pl.BlockSpec(TILE, lambda i, t: (i, LIN))
    anywhere = pl.BlockSpec(memory_space=pl.ANY)
    return pl.pallas_call(
        sparse_forward_kernel,
        grid_spec=pltpu.PrefetchScalarGridSpec(
            num_scalar_prefetch=1,
            grid=(2,),
            in_specs=[column] * 3 + [anywhere] * 12,
            out_specs=[
                column,
                pl.BlockSpec((1, LISTED + 1, BLOCK, BLOCK), lambda i, t: (i, 0, 0, 0)),
                pl.BlockSpec((LISTED, BLOCK, HD), lambda i, t: (i, 0, 0)),
                pl.BlockSpec((LISTED, BLOCK, HD), lambda i, t: (i, 0, 0)),
            ],
            scratch_shapes=[
                pltpu.VMEM((LISTED + 1, BLOCK, BLOCK), F32),
                pltpu.SemaphoreType.DMA((2, LISTED)),
            ],
        ),
        out_shape=[
            jax.ShapeDtypeStruct(queries.shape, BF),
            jax.ShapeDtypeStruct((2, LISTED + 1, BLOCK, BLOCK), BF),
            jax.ShapeDtypeStruct((2 * LISTED, BLOCK, HD), BF),
            jax.ShapeDtypeStruct((2 * LISTED, BLOCK, HD), BF),
        ],
        input_output_aliases={4: 0},
        compiler_params=params(32),
        cost_estimate=cost(4e9, 12 * MIB),
        name="sparse_forward",
    )(table, queries, keys, values, base, dep, *pieces)


def sparse_backward_kernel(
    core, q_ref, k_ref, v_ref, g_ref, o_ref, p_ref, kf_ref, vf_ref, dep, dq_ref, dk_ref, dv_ref, mine_ref, sent_ref
):
    first = core[0] == 0
    q, g = q_ref[...], g_ref[...]
    row_dot = jnp.sum((g.astype(F32) * o_ref[...].astype(F32)).T, axis=0, keepdims=True)
    dq = jnp.zeros((HD, BLOCK), F32)
    for r in range(LISTED + 1):
        p = p_ref[0, r]
        key = k_ref[...] if r == 0 else kf_ref[r - 1]
        value = v_ref[...] if r == 0 else vf_ref[r - 1]
        dp = dot(value, g, 1, 1)
        ds = (p.astype(F32) * (dp - row_dot)).astype(BF)
        dq = dq + dot(key, ds, 0, 0)
        dk = dot(ds, q, 1, 0) * SCALING
        dv = dot(p, g, 1, 0)
        if r == 0:
            dk_ref[...] = dk
            dv_ref[...] = dv
        else:
            mine_ref[r - 1] = jnp.where(first, dk, dv).astype(BF)
            sent_ref[r - 1] = jnp.where(first, dv, dk).astype(BF)
    dq_ref[...] = (dq * SCALING).T.astype(BF)


def sparse_backward(core, queries, keys, values, grads, outs, probs, far_k, far_v, dep):
    column = pl.BlockSpec(TILE, lambda i, c: (i, LIN))
    four = pl.BlockSpec((LISTED, BLOCK, HD), lambda i, c: (i, 0, 0))
    five = pl.BlockSpec((1, LISTED + 1, BLOCK, BLOCK), lambda i, c: (i, 0, 0, 0))
    return pl.pallas_call(
        sparse_backward_kernel,
        grid_spec=pltpu.PrefetchScalarGridSpec(
            num_scalar_prefetch=1,
            grid=(2,),
            in_specs=[column] * 3
            + [pl.BlockSpec(TILE, lambda i, c: (i, 0)), column, five, four, four, ANY],
            out_specs=[column, column, column, four, four],
        ),
        out_shape=[
            jax.ShapeDtypeStruct(queries.shape, BF),
            jax.ShapeDtypeStruct(queries.shape, F32),
            jax.ShapeDtypeStruct(queries.shape, F32),
            jax.ShapeDtypeStruct((2 * LISTED, BLOCK, HD), BF),
            jax.ShapeDtypeStruct((2 * LISTED, BLOCK, HD), BF),
        ],
        compiler_params=params(32),
        cost_estimate=cost(8e9, 12 * MIB),
        name="sparse_backward",
    )(core, queries, keys, values, grads, outs, probs, far_k, far_v, dep)


def begin_kernel(core, k_ref, v_ref, states, mine, sent):
    first = core[0] == 0
    for h in range(LIN):
        at = pl.ds(h * HD, HD)
        s0 = dot(k_ref[0:BLOCK, at], v_ref[0:BLOCK, at], 0, 0)
        s1 = dot(k_ref[BLOCK:, at], v_ref[BLOCK:, at], 0, 0)
        states[0, h] = s0
        states[1, h] = s1
        sent[2 * BLOCK + h * HD : 2 * BLOCK + (h + 1) * HD] = (s0 + s1).astype(BF)
    at = pl.ds(LIN * HD, HD)
    k, v = k_ref[:, at], v_ref[:, at]
    mine[...] = jnp.where(first, k, v)
    sent[0 : 2 * BLOCK] = jnp.where(first, v, k)


def start_kernel(core, mine, got, states, out, scratch):
    out[0 : 2 * BLOCK] = mine[...]
    out[FRONT:] = got[0 : 2 * BLOCK]
    for h in range(LIN):
        other = got[2 * BLOCK + h * HD : 2 * BLOCK + (h + 1) * HD].astype(F32)
        scratch[h * HD : (h + 1) * HD] = states[0, h] + states[1, h] + other
    out[2 * BLOCK : FRONT] = scratch[pl.ds(pl.multiple_of(core[0] * HALF, HALF), HALF)].astype(BF)


def line_kernel(core, earlier, start, right, far_a, far_b, left, line, local):
    for spot, piece in ((0, start), (4 * BLOCK, right), (MID + 2 * HALF + 4 * BLOCK, left)):
        line[spot : spot + 2 * BLOCK] = piece[0 : 2 * BLOCK]
        line[spot + 2 * BLOCK : spot + 4 * BLOCK] = piece[FRONT:]
    spot = MID + 2 * HALF
    line[spot : spot + 2 * BLOCK] = far_a[0 : 2 * BLOCK]
    line[spot + 2 * BLOCK : spot + 4 * BLOCK] = far_b[...]
    first = core[0] == 0
    s = [p[2 * BLOCK : FRONT].astype(F32) for p in (start, right, far_a, left)]
    m = [earlier[0, p].astype(F32) for p in range(SIDE)]
    before = s[1] * m[1] + s[2] * m[2] + s[3] * m[3]
    total = s[0] + s[1] + s[2] + s[3]
    line[MID : MID + HALF] = jnp.where(first, total, s[0]).astype(BF)
    line[MID + HALF : MID + 2 * HALF] = jnp.where(first, 0.0, before).astype(BF)
    local[...] = before


def prefix_kernel(earlier, local, right, far, left, out, scratch, sems):
    got = [
        pltpu.make_async_copy(piece.at[pl.ds(MID, 2 * HALF)], scratch.at[n], sems.at[n])
        for n, piece in enumerate((right, far, left))
    ]
    for copy in got:
        copy.start()
    for copy in got:
        copy.wait()
    total = local[...]
    for n in range(3):
        total = total + scratch[n, 0:HALF].astype(F32) * earlier[1, n + 1].astype(F32)
        total = total + scratch[n, HALF:].astype(F32)
    out[...] = total


def prefix(earlier, local, right, far, left):
    return pl.pallas_call(
        prefix_kernel,
        in_specs=[SM, VM, ANY, ANY, ANY],
        out_specs=VM,
        out_shape=jax.ShapeDtypeStruct((HALF, HD), F32),
        scratch_shapes=[pltpu.VMEM((3, 2 * HALF, HD), BF), pltpu.SemaphoreType.DMA((3,))],
        compiler_params=params(4),
        cost_estimate=cost(1e5, MIB // 2),
        name="prefix",
    )(earlier, local, right, far, left)


SPOTS = (0, BLOCK, FRONT, FRONT + BLOCK)


def placed(table, j, own_ref, peer_ref):
    a, b = table[0, j], table[1, j]
    first = own_ref[jnp.maximum(a, 0)].astype(F32) * jnp.where(a >= 0, 1.0, 0.0).astype(F32)
    second = peer_ref[jnp.maximum(b, 0)].astype(F32) * jnp.where(b >= 0, 1.0, 0.0).astype(F32)
    return first + second


def fill(table, own, peer, half, j, out, u, more=(), m=0):
    for q, spot in enumerate(SPOTS):
        at = pl.ds(spot, BLOCK)
        value = placed(table, 4 * j + q, own, peer)
        for ref in more:
            value = value + ref[m, at].astype(F32)
        out[u, at] = value.astype(BF)
    at = pl.ds(2 * BLOCK, HALF)
    value = half[...] * table[2, j].astype(F32)
    for ref in more:
        value = value + ref[m, at].astype(F32)
    out[u, at] = value.astype(BF)


def far_kernel(table, own, peer, half, far_a, far_b):
    @pl.loop(0, 2)
    def _(u):
        fill(table, own, peer, half, 8 + u, far_a, u)
        fill(table, own, peer, half, 10 + u, far_b, u)


def near_kernel(table, own, peer, half, ra, rb, right, left):
    @pl.loop(0, 2)
    def _(u):
        fill(table, own, peer, half, 4 + u, right, u, [ra], u)
        fill(table, own, peer, half, 6 + u, right, u + 2)
        fill(table, own, peer, half, 12 + u, left, u)
        fill(table, own, peer, half, 14 + u, left, u + 2, [rb], u)


def turn_kernel(table, own, peer, half, r1, r3, home, right, far_a, far_b, left, unit):
    @pl.loop(0, SIDE)
    def _(u):
        fill(table, own, peer, half, u, unit, u, [r1, r3], u)

    home[...] = unit[0]
    right[...] = unit[1]
    far_a[...] = unit[2, 0:FRONT]
    far_b[...] = unit[2, FRONT:]
    left[...] = unit[3]


def last_kernel(right, left, ra, rb, o_right, o_left):
    o_right[0:FRONT] = (right[0:FRONT].astype(F32) + ra[...].astype(F32)).astype(BF)
    o_right[FRONT:] = right[FRONT:]
    o_left[0:FRONT] = left[0:FRONT]
    o_left[FRONT:] = (left[FRONT:].astype(F32) + rb[...].astype(F32)).astype(BF)


def tail_kernel(home, r1, r3, mine, sent, extra):
    def total(a, b):
        return home[a:b].astype(F32) + r1[a:b].astype(F32) + r3[a:b].astype(F32)

    mine[...] = total(0, 2 * BLOCK).astype(BF)
    more = total(2 * BLOCK, FRONT)
    extra[...] = more
    sent[0 : 2 * BLOCK] = total(FRONT, UNIT).astype(BF)
    sent[2 * BLOCK :] = more.astype(BF)


def finish_kernel(core, k_ref, v_ref, dk, dv, mine_ref, got_ref, tail_ref, extra, adj, peer, kg, vg, scratch):
    first = core[0] == 0
    mine, got = mine_ref[...].astype(F32), got_ref[...].astype(F32)
    at = pl.ds(LIN * HD, HD)
    kg[:, at] = (dk[:, at] + jnp.where(first, mine, got)).astype(BF)
    vg[:, at] = (dv[:, at] + jnp.where(first, got, mine)).astype(BF)
    tail = tail_ref[...].astype(F32)
    scratch[0:HALF] = jnp.where(first, extra[...], tail)
    scratch[HALF:] = jnp.where(first, tail, extra[...])
    inner = jnp.where(pl.program_id(0) == 0, 1.0, 0.0).astype(F32)
    chip = jnp.where(first, 1.0, 0.0).astype(F32)
    for h in range(LIN):
        at = pl.ds(h * HD, HD)
        state = scratch[at, :] + peer[at, :].astype(F32) * chip + adj[1, h] * inner
        hi, lo = split(state)
        k, v = k_ref[:, at], v_ref[:, at]
        kg[:, at] = (dk[:, at] + dot(v, hi, 1, 1) + dot(v, lo, 1, 1)).astype(BF)
        vg[:, at] = (dv[:, at] + dot(k, hi, 1, 0) + dot(k, lo, 1, 0)).astype(BF)


def finish(core, keys, values, dk, dv, mine, got, extra, adjoints, peer):
    rows = pl.BlockSpec((BLOCK, keys.shape[1]), lambda i, c: (i, 0))
    piece = pl.BlockSpec((BLOCK, HD), lambda i, c: (i, 0))
    fixed = [
        pl.BlockSpec((HALF, HD), lambda i, c: (0, 0)),
        pl.BlockSpec(adjoints.shape, lambda i, c: (0, 0, 0, 0)),
        pl.BlockSpec((LIN * HD, HD), lambda i, c: (0, 0)),
    ]
    shape = jax.ShapeDtypeStruct(keys.shape, BF)
    return pl.pallas_call(
        finish_kernel,
        grid_spec=pltpu.PrefetchScalarGridSpec(
            num_scalar_prefetch=1,
            grid=(2,),
            in_specs=[rows] * 4 + [piece, piece, fixed[0]] + fixed,
            out_specs=[rows, rows],
            scratch_shapes=[pltpu.VMEM((LIN * HD, HD), F32)],
        ),
        out_shape=[shape, shape],
        compiler_params=params(32),
        cost_estimate=cost(5e8, 9 * MIB),
        name="finish",
    )(core, keys, values, dk, dv, mine, got, got[2 * BLOCK :], extra, adjoints, peer)


def where_is(blocks, place):
    owner, within = blocks // 2, blocks % 2
    pz = (place // (SIDE * CORES) - owner // (SIDE * CORES)) % SIDE
    px = (place // CORES % SIDE - owner // CORES % SIDE) % SIDE
    return pz, px, owner % CORES, within


def spot_of(blocks, place, stream):
    pz, px, core, within = where_is(blocks, place)
    rel = (core != stream).astype(jnp.int32)
    outer = jnp.where(stream == 0, pz, px)
    first = jnp.where(stream == 0, px, pz)
    return outer, first, rel * 2 + within


def spot_of(blocks, place, stream):
    pz, px, core, within = where_is(blocks, place)
    rel = (core != stream).astype(jnp.int32)
    outer = jnp.where(stream == 0, pz, px)
    first = jnp.where(stream == 0, px, pz)
    return outer, first, rel * 2 + within


def piece_of(blocks, place, stream):
    outer, first, rest = spot_of(blocks, place, stream)
    late = first >= 2
    second = (outer == 2) & late
    piece = jnp.where(outer < 2, outer, jnp.where(outer == 3, 4, jnp.where(second, 3, 2)))
    index = first * 16 + rest * 4 + jnp.where(late, 3, 0) - jnp.where(second, 35, 0)
    return piece + 5 * (place % CORES != stream).astype(jnp.int32), index


def fetch_table(lists, place):
    flat = lists.reshape(-1)
    mine = place * 2 + jnp.arange(2 * LISTED, dtype=jnp.int32) // LISTED
    usable = (flat != mine).astype(jnp.int32)
    columns = [*piece_of(flat, place, 0), *piece_of(flat, place, 1), usable]
    return jnp.stack(columns, axis=1).astype(jnp.int32)


def back_table(lists, peer_lists, place):
    slots = jnp.arange(2 * LISTED, dtype=jnp.int32)[:, None]
    spots = jnp.arange(64, dtype=jnp.int32)[None, :]
    rows = []
    for some in (lists, peer_lists):
        outer, first, rest = spot_of(some.reshape(-1), place, place % CORES)
        target = (-outer) % SIDE * 16 + (-first) % SIDE * 4 + rest
        rows.append(jnp.max(jnp.where(target[:, None] == spots, slots, -1), axis=0))
    z, x = place // (SIDE * CORES), place // CORES % SIDE
    step = jnp.arange(64, dtype=jnp.int32)
    outer, inner = step // SIDE, step % SIDE
    on_keys = place % CORES == 0
    to_z = (z + jnp.where(on_keys, outer, inner)) % SIDE
    to_x = (x + jnp.where(on_keys, inner, outer)) % SIDE
    rows.append((to_z * SIDE + to_x < z * SIDE + x).astype(jnp.int32))
    return jnp.stack(rows).astype(jnp.int32)


def earlier_table(place):
    z, x = place // (SIDE * CORES), place // CORES % SIDE
    on_keys = place % CORES == 0
    first, second = jnp.where(on_keys, x, z), jnp.where(on_keys, z, x)
    step = jnp.arange(SIDE, dtype=jnp.int32)
    rows = [(c - step) % SIDE < c for c in (first, second)]
    return jnp.stack(rows).astype(jnp.int32)


def local(queries, keys, values, out_weight, out_grad, long_blocks):
    place = lax.axis_index("ctx").astype(jnp.int32)
    core = (place % CORES).reshape(1)
    row_count = queries.shape[0]
    positions = place * row_count + jnp.arange(row_count, dtype=jnp.int32)
    scale = 1.0 / (math.sqrt(HD) * jnp.sqrt((positions + 1).astype(F32)))
    scale = jnp.broadcast_to(scale[None, :], (8, row_count))
    lists = lax.dynamic_slice_in_dim(long_blocks, place * 2, 2, 0)
    peer_lists = lax.dynamic_slice_in_dim(long_blocks, (place ^ 1) * 2, 2, 0)
    fetch = fetch_table(lists, place)
    back = back_table(lists, peer_lists, place)
    earlier = earlier_table(place)

    grad_all = lax.all_gather(out_grad, "head", axis=1, tiled=True)

    states, mine, sent = whole_call(
        begin_kernel,
        [core],
        [keys, values],
        [((2, LIN, HD, HD), F32), ((2 * BLOCK, HD), BF), ((2 * BLOCK + LIN * HD, HD), BF)],
        "begin",
    )
    got = swap(sent)
    (start,) = whole_call(
        start_kernel, [core], [mine, got, states], [((UNIT, HD), BF)], "start",
        scratch=[pltpu.VMEM((LIN * HD, HD), F32)],
    )
    a_right, a_left = ring_move(start, 0, 1), ring_move(start, 0, -1)
    cut = halves(a_right, a_left, FRONT)
    a_far = ring_move(cut[0], 0, 1), ring_move(cut[1], 0, -1)
    line, inside = whole_call(
        line_kernel, [core, earlier], [start, a_right, *a_far, a_left],
        [((LINE, HD), BF), ((HALF, HD), F32)], "line",
    )
    b_right, b_left = ring_move(line, 1, 1), ring_move(line, 1, -1)
    line_swapped = swap(line)
    cut = halves(b_right, b_left, MID + 2 * HALF, [line_swapped])
    b_far = ring_move(cut[0], 1, 1), ring_move(cut[1], 1, -1)
    pieces = [line, b_right, *b_far, b_left]
    pieces = pieces + [line_swapped] + [swap(p) for p in pieces[1:]]
    part = prefix(earlier, inside, b_right, b_far[0], b_left)
    other = swap(part)
    on_keys = place % CORES == 0
    chip = jnp.where(on_keys, jnp.concatenate([part, other]), jnp.concatenate([other, part]))
    chip = chip + jnp.where(on_keys, 0.0, got[2 * BLOCK :].astype(F32))
    chip = chip.reshape(LIN, HD, HD)
    before = jnp.stack([chip, chip + states[0]])

    attention = linear_forward(queries, keys, values, scale, before)
    attention, probs, far_k, far_v = sparse_forward(
        fetch, queries, keys, values, attention, inside, pieces
    )
    partial_out = dot(attention, out_weight, 1, 1).astype(BF)
    layer_out = lax.psum_scatter(partial_out, "head", scatter_dimension=1, tiled=True)
    sparse_grad = dot(grad_all, out_weight[:, LIN * HD :], 1, 0).astype(BF)
    linear_grad = dot(grad_all, out_weight[:, : LIN * HD], 1, 0).astype(BF)
    query_grad, own_dk, own_dv, pair_mine, pair_sent = sparse_backward(
        core, queries, keys, values, sparse_grad, attention, probs, far_k, far_v, inside
    )

    adjoints = block_adjoints(queries, linear_grad, scale)
    adjoint = (adjoints[0] + adjoints[1]).reshape(LIN * HD, HD)
    adjoint_peer = swap(adjoint.astype(BF))
    half = lax.dynamic_slice_in_dim(
        adjoint + adjoint_peer.astype(F32), place % CORES * HALF, HALF, 0
    )
    base = [pair_mine, swap(pair_sent), half]
    far_a, far_b = whole_call(
        far_kernel, [back], base, [((2, UNIT, HD), BF)] * 2, "back_far"
    )
    r1, r3 = ring_move(far_a, 1, 1), ring_move(far_b, 1, -1)
    near = whole_call(
        near_kernel, [back], base + [r1, r3], [((SIDE, UNIT, HD), BF)] * 2, "back_near"
    )
    r1, r3 = ring_move(near[0], 1, 1), ring_move(near[1], 1, -1)

    query_grad, own_dk, own_dv = linear_backward(
        queries, keys, values, linear_grad, scale, before, (query_grad, own_dk, own_dv), inside
    )

    home, right, far_a, far_b, left = whole_call(
        turn_kernel, [back], base + [r1, r3],
        [((UNIT, HD), BF), ((UNIT, HD), BF), ((FRONT, HD), BF), ((2 * BLOCK, HD), BF), ((UNIT, HD), BF)],
        "back_turn", deps=[query_grad], scratch=[pltpu.VMEM((SIDE, UNIT, HD), BF)],
    )
    r1, r3 = ring_move(far_a, 0, 1), ring_move(far_b, 0, -1)
    right, left = whole_call(
        last_kernel, [], [right, left, r1, r3], [((UNIT, HD), BF)] * 2, "back_last"
    )
    r1, r3 = ring_move(right, 0, 1), ring_move(left, 0, -1)
    mine, sent, extra = whole_call(
        tail_kernel, [], [home, r1, r3],
        [((2 * BLOCK, HD), BF), ((FRONT, HD), BF), ((HALF, HD), F32)], "back_tail",
    )
    key_grad, value_grad = finish(
        core, keys, values, own_dk, own_dv, mine, swap(sent), extra, adjoints, adjoint_peer
    )
    return layer_out, query_grad, key_grad, value_grad


def solution(mesh):
    return jax.shard_map(
        local,
        mesh=mesh,
        in_specs=(
            P("ctx", "head"),
            P("ctx", "head"),
            P("ctx", "head"),
            P(None, "head"),
            P("ctx", "head"),
            P(),
        ),
        out_specs=(P("ctx", "head"), P("ctx", "head"), P("ctx", "head"), P("ctx", "head")),
        check_vma=False,
    )
```

time: 278 us -> 229 us (0.82); the launches traced: 274 us -> 228 us
  starting transfers between devices: 90.9 us -> 41.5 us
  waiting for transfers between devices: 70.7 us -> 92.4 us
  local copies, waits for them, and re-layouts: 31.3 us -> 10.3 us
  Pallas kernels: 42.2 us -> 48.2 us
  other arithmetic: 5.31 us -> 1.42 us
    ppermute x54 -> x26, starting transfers between devices: 90.8 us -> 41.4 us  [the longest x16 24.3 us: ring_move(): return lax.ppermute(value, 'ctx', pairs)]
    ppermute x54 -> x26, waiting for transfers between devices: 70 us -> 91.6 us  [the longest x16 86.7 us: ring_move(): return lax.ppermute(value, 'ctx', pairs)]
    unnamed x104 -> x60, local copies, waits for them, and re-layouts: 20.3 us -> 9.71 us
    slice x10 -> x1, local copies, waits for them, and re-layouts: 6.38 us -> 0.01 us  [finish(): got[2 * BLOCK:]]
    pallas_call x7 -> x13, Pallas kernels: 17.7 us -> 23.5 us  [the longest x8 8.04 us: whole_call(): pl.pallas_call(functools.partial(drop, kernel, n_in, len(deps)), in_specs...]
    dot_general x2 -> x3, matrix products: 18.4 us -> 19.7 us  [dot(): lax.dot_general(a, b, (((ca,), (cb,)), ((), ())), preferred_element_type=...]
  transfers between devices with their start and end apart: 56 -> 28, of which waited for: 10 -> 14; matrix products, arithmetic and copies ran while one was open for 15% -> 10% of each run, Pallas kernels for 15% -> 21%
where the time goes in v2:
time: 229 us; the launch traced here: 228 us
  waiting for transfers between devices  92.4 us (40%)
  Pallas kernels  48.2 us (21%)
  starting transfers between devices  41.5 us (18%)
  matrix products  19.7 us (9%)
  between operations  14.5 us (6%)
  local copies, waits for them, and re-layouts  10.3 us (4%)
    ppermute x16, waiting for transfers between devices, ring_move(): return lax.ppermute(value, 'ctx', pairs)  86.7 us
    ppermute x16, starting transfers between devices, ring_move(): return lax.ppermute(value, 'ctx', pairs)  24.3 us
    dot_general x3, matrix products, dot(): lax.dot_general(a, b, (((ca,), (cb,)), ((), ())), preferred_element_type=...  19.7 us
    ppermute x10, starting transfers between devices, swap(): return lax.ppermute(value, 'ctx', [(i, i ^ 1) for i in range(CTX)])  17.2 us
    pallas_call x1, Pallas kernels, sparse_forward(): pl.pallas_call(sparse_forward_kernel, grid_spec=pltpu.PrefetchScalarGridS...  11.7 us
    unnamed x60, local copies, waits for them, and re-layouts  9.71 us
    pallas_call x8, Pallas kernels, whole_call(): pl.pallas_call(functools.partial(drop, kernel, n_in, len(deps)), in_specs...  8.04 us
    pallas_call x1, Pallas kernels, linear_backward(): pl.pallas_call(linear_backward_kernel, grid=(2, LIN), in_specs=[tile_spec...  7.43 us
  transfers between devices with their start and end apart: 28, of which 14 were waited for; matrix products, arithmetic and copies ran while one was open for 10% of the time, Pallas kernels for 21%

profile of v2, /device:TPU:1, one launch (start us, length us, event | category | flops | bytes accessed | tf_op | source)
XLA Modules:
  0.0 228.1 jit_solution(14666513360599339978)
XLA Ops:
  12.1 1.8 collective-permute-start.1
  13.9 2.2 collective-permute-start.2
  16.1 7.0 %collective-permute-done.1.refs_0_.refs_3_ = bf16[2240,128]{1,0:T(8,128)(2,1)S(1)} collective-permute-done((bf16[2240,128]{1,0:T(8,128)(2,1)S(1)}, bf16[2240,128]{1,0:T(8,128)(2,1)S(1)}, u32[]{:S(2)}, u32[]{:S(2)}) %collective-permute-start.1) | collective-permute-done | bytes 573472 | tf_op jit(solution)/shard_map/ppermute | solution.py:51
  25.4 1.9 collective-permute-start.4
  27.3 3.9 %collective-permute-done.4.refs_5_ = bf16[1024,128]{1,0:T(8,128)(2,1)} collective-permute-done((bf16[1024,128]{1,0:T(8,128)(2,1)}, bf16[1024,128]{1,0:T(8,128)(2,1)}, u32[]{:S(2)}, u32[]{:S(2)}) %collective-permute-start.4) | collective-permute-done | bytes 262176 | tf_op jit(solution)/shard_map/ppermute | solution.py:51
  36.5 1.8 collective-permute-start.6
  38.2 2.5 %collective-permute-start.7 = (bf16[8576,128]{1,0:T(8,128)(2,1)S(1)}, bf16[8576,128]{1,0:T(8,128)(2,1)S(1)}, u32[]{:S(2)}, u32[]{:S(2)}) collective-permute-start(bf16[8576,128]{1,0:T(8,128)(2,1)S(1)} %get-tuple-element.47.rest_0_), channel_id=1, source_target_pairs={{0,4},{4,0},{8,12},{12,8},{16,20},{20,16},{24,28},{28,24},{32,36},... | collective-permute-start | bytes 6586376 | tf_op jit(solution)/shard_map/ppermute | solution.py:55
  40.8 22.3 %collective-permute-done.5.refs_0_.right.rest_1_ = bf16[8576,128]{1,0:T(8,128)(2,1)S(1)} collective-permute-done((bf16[8576,128]{1,0:T(8,128)(2,1)S(1)}, bf16[8576,128]{1,0:T(8,128)(2,1)S(1)}, u32[]{:S(2)}, u32[]{:S(2)}) %collective-permute-start.5) | collective-permute-done | bytes 2195488 | tf_op jit(solution)/shard_map/ppermute | solution.py:51
  63.1 3.4 %copies.3 = (bf16[4480,128]{1,0:T(8,128)(2,1)}, bf16[4096,128]{1,0:T(8,128)(2,1)}) custom-call(bf16[8576,128]{1,0:T(8,128)(2,1)S(1)} %collective-permute-done.5.refs_0_.right.rest_1_, bf16[8576,128]{1,0:T(8,128)(2,1)} %collective-permute-done.6.refs_1_.left.rest_4_, bf16[8576,128]{1,0:T(8,128)(2,1)S(1)} %collective-permute-done.7.refs_2_.rest_5_), custom_call_target="tpu_custom_call" | custom-call | bytes 4390912 | tf_op jit(solution)/shard_map/copies/pallas_call | solution.py:74
  67.5 1.8 collective-permute-start.10
  69.4 3.4 %collective-permute-start.11 = (bf16[8576,128]{1,0:T(8,128)(2,1)S(1)}, bf16[8576,128]{1,0:T(8,128)(2,1)}, u32[]{:S(2)}, u32[]{:S(2)}) collective-permute-start(bf16[8576,128]{1,0:T(8,128)(2,1)S(1)} %collective-permute-done.5.refs_0_.right.rest_1_), channel_id=1, source_target_pairs={{0,4},{4,0},{8,12},{12,8},{16,20},{20,16},{24,28},{28,24},{32,36},... | collective-permute-start | bytes 6586376 | tf_op jit(solution)/shard_map/ppermute | solution.py:55
  73.1 8.7 %collective-permute-done.10.rest_3_ = bf16[4096,128]{1,0:T(8,128)(2,1)} collective-permute-done((bf16[4096,128]{1,0:T(8,128)(2,1)}, bf16[4096,128]{1,0:T(8,128)(2,1)}, u32[]{:S(2)}, u32[]{:S(2)}) %collective-permute-start.10) | collective-permute-done | bytes 1048608 | tf_op jit(solution)/shard_map/ppermute | solution.py:51
  81.8 4.5 %collective-permute-start.13 = (bf16[4096,128]{1,0:T(8,128)(2,1)}, bf16[4096,128]{1,0:T(8,128)(2,1)}, u32[]{:S(2)}, u32[]{:S(2)}) collective-permute-start(bf16[4096,128]{1,0:T(8,128)(2,1)} %collective-permute-done.10.rest_3_), channel_id=1, source_target_pairs={{0,4},{4,0},{8,12},{12,8},{16,20},{20,16},{24,28},{28,24},{32,36},... | collective-permute-start | bytes 3145736 | tf_op jit(solution)/shard_map/ppermute | solution.py:55
  91.4 3.8 %linear_forward.1.base_ref = bf16[1024,512]{1,0:T(8,128)(2,1)S(1)} custom-call(bf16[1024,512]{1,0:T(8,128)(2,1)S(1)} %copy-done.6, bf16[1024,512]{1,0:T(8,128)(2,1)S(1)} %copy-done, bf16[1024,512]{1,0:T(8,128)(2,1)S(1)} %copy-done.2, f32[8,1024]{1,0:T(8,128)S(1)} %broadcast_in_dim.52.c_ref, f32[2,3,128,128]{3,2,1,0:T(8,128)S(1)} %pad_maximum_fusion.s_ref), custom_call_target="tpu_custom_call" | custom-call | flops 2400000000 | bytes 4194304 | tf_op jit(solution)/shard_map/linear_forward/pallas_call | solution.py:166
  95.3 11.7 %sparse_forward.1 = (bf16[1024,512]{1,0:T(8,128)(2,1)S(1)}, bf16[2,5,512,512]{3,2,1,0:T(8,128)(2,1)}, bf16[8,512,128]{2,1,0:T(8,128)(2,1)S(1)}, bf16[8,512,128]{2,1,0:T(8,128)(2,1)S(1)}) custom-call(s32[8,5]{1,0:T(8,128)S(1)} %stack.12.table, bf16[1024,512]{1,0:T(8,128)(2,1)S(1)} %copy-done.6, ...), custom_call_target="tpu_custom_call", output_to_operand_aliasing={{0}: (4, {})} | custom-call | flops 4000000000 | bytes 12582912 | tf_op jit(solution)/shard_map/sparse_forward/pallas_call | solution.py:255
  108.9 9.1 %convolution_convert_fusion = bf16[1024,4096]{1,0:T(8,128)(2,1)} fusion(bf16[1024,512]{1,0:T(8,128)(2,1)S(1)} %get-tuple-element.50.o_ref, bf16[4096,512]{1,0:T(8,128)(2,1)} %param.9), kind=kOutput, calls=%fused_computation | convolution fusion | flops 4299161600 | bytes 13631488 | tf_op jit(solution)/shard_map/dot_general | solution.py:32
  119.6 6.1 %convolution_convert_fusion.1.g_ref = bf16[1024,128]{1,0:T(8,128)(2,1)S(1)} fusion(bf16[1024,4096]{1,0:T(8,128)(2,1)} %all-gather.2.cloned.1.call-done, bf16[4096,512]{1,0:T(8,128)(2,1)} %param.9), kind=kOutput, calls=%fused_computation.4 | convolution fusion | flops 1073872896 | bytes 9699328 | tf_op jit(solution)/shard_map/dot_general | solution.py:32
  125.8 2.5 %copy-done.22 = bf16[2,5,512,512]{3,2,1,0:T(8,128)(2,1)S(1)} copy-done((bf16[2,5,512,512]{3,2,1,0:T(8,128)(2,1)S(1)}, bf16[2,5,512,512]{3,2,1,0:T(8,128)(2,1)}, u32[]{:S(2)}) %copy-start.22) | copy-done | bytes 5242904
  128.3 7.1 %sparse_backward.1 = (bf16[1024,512]{1,0:T(8,128)(2,1)}, f32[1024,512]{1,0:T(8,128)S(1)}, f32[1024,512]{1,0:T(8,128)S(1)}, bf16[8,512,128]{2,1,0:T(8,128)(2,1)S(1)}, bf16[8,512,128]{2,1,0:T(8,128)(2,1)S(1)}) custom-call(s32[1]{0:T(128)} %bitcast.refs_0_.core, bf16[1024,512]{1,0:T(8,128)(2,1)S(1)} %copy-done.7, bf16[1024,512]{1,0:T(8,128)(2,1)S(1)} %copy-done, ...), custom_call_target="tpu_custom_call" | custom-call | flops 8000000000 | bytes 12582912 | tf_op jit(solution)/shard_map/sparse_backward/pallas_call | solution.py:314
  135.5 4.5 %fusion.2.g_ref = bf16[1024,384]{1,0:T(8,128)(2,1)S(1)} fusion(bf16[1024,4096]{1,0:T(8,128)(2,1)S(1)} %copy-done.28, bf16[4096,512]{1,0:T(8,128)(2,1)S(1)} %copy-done.29), kind=kOutput, calls=%fused_computation.3 | convolution fusion | flops 3221618688 | bytes 12320768 | tf_op jit(solution)/shard_map/dot_general | solution.py:32
  140.0 1.8 block_adjoints.1.adj
  147.6 13.6 %collective-permute-done.17.refs_4_ = bf16[2,2240,128]{2,1,0:T(8,128)(2,1)S(1)} collective-permute-done((bf16[2,2240,128]{2,1,0:T(8,128)(2,1)S(1)}, bf16[2,2240,128]{2,1,0:T(8,128)(2,1)S(1)}, u32[]{:S(2)}, u32[]{:S(2)}) %collective-permute-start.17) | collective-permute-done | bytes 1146912 | tf_op jit(solution)/shard_map/ppermute | solution.py:51
  161.2 2.4 %back_near.1 = (bf16[4,2240,128]{2,1,0:T(8,128)(2,1)S(1)}, bf16[4,2240,128]{2,1,0:T(8,128)(2,1)S(1)}) custom-call(s32[3,64]{1,0:T(4,128)S(1)} %pad_add_fusion.refs_0_, bf16[8,512,128]{2,1,0:T(8,128)(2,1)S(1)} %get-tuple-element.60.refs_1_, bf16[8,512,128]{2,1,0:T(8,128)(2,1)S(1)} %collective-permute-done.15.refs_2_, ...), custom_call_target="tpu_custom_call" | custom-call | flops 1000000 | bytes 9076736 | tf_op jit(solution)/shard_map/back_near/pallas_call | solution.py:104
  164.6 1.9 collective-permute-start.20
  166.5 7.4 %linear_backward.1 = (bf16[1024,512]{1,0:T(8,128)(2,1)}, f32[1024,512]{1,0:T(8,128)S(1)}, f32[1024,512]{1,0:T(8,128)S(1)}) custom-call(bf16[1024,512]{1,0:T(8,128)(2,1)S(1)} %copy-done.7, bf16[1024,512]{1,0:T(8,128)(2,1)S(1)} %copy-done, bf16[1024,512]{1,0:T(8,128)(2,1)S(1)} %copy-done.3, ...), custom_call_target="tpu_custom_call", output_to_operand_aliasing={{0}: (6, {}), {1}: (7, {}), {2}: (8, {})} | custom-call | flops 5000000000 | bytes 9437184 | tf_op jit(solution)/shard_map/linear_backward/pallas_call | solution.py:194
  174.0 18.4 %collective-permute-done.19.refs_4_ = bf16[4,2240,128]{2,1,0:T(8,128)(2,1)S(1)} collective-permute-done((bf16[4,2240,128]{2,1,0:T(8,128)(2,1)S(1)}, bf16[4,2240,128]{2,1,0:T(8,128)(2,1)S(1)}, u32[]{:S(2)}, u32[]{:S(2)}) %collective-permute-start.19) | collective-permute-done | bytes 2293792 | tf_op jit(solution)/shard_map/ppermute | solution.py:51
  193.6 2.2 back_turn.1
  198.7 4.1 %collective-permute-done.22.refs_3_ = bf16[1024,128]{1,0:T(8,128)(2,1)S(1)} collective-permute-done((bf16[1024,128]{1,0:T(8,128)(2,1)S(1)}, bf16[1024,128]{1,0:T(8,128)(2,1)S(1)}, u32[]{:S(2)}, u32[]{:S(2)}) %collective-permute-start.22) | collective-permute-done | bytes 262176 | tf_op jit(solution)/shard_map/ppermute | solution.py:51
  204.2 1.9 collective-permute-start.24
  206.2 7.4 %collective-permute-done.23.refs_1_ = bf16[2240,128]{1,0:T(8,128)(2,1)S(1)} collective-permute-done((bf16[2240,128]{1,0:T(8,128)(2,1)S(1)}, bf16[2240,128]{1,0:T(8,128)(2,1)S(1)}, u32[]{:S(2)}, u32[]{:S(2)}) %collective-permute-start.23) | collective-permute-done | bytes 573472 | tf_op jit(solution)/shard_map/ppermute | solution.py:51
  213.8 3.9 %collective-permute-start.25 = (bf16[1216,128]{1,0:T(8,128)(2,1)S(1)}, bf16[1216,128]{1,0:T(8,128)(2,1)S(1)}, u32[]{:S(2)}, u32[]{:S(2)}) collective-permute-start(bf16[1216,128]{1,0:T(8,128)(2,1)S(1)} %get-tuple-element.74), channel_id=1, source_target_pairs={{0,4},{4,0},{8,12},{12,8},{16,20},{20,16},{24,28},{28,24},{32,36},... | collective-permute-start | bytes 933896 | tf_op jit(solution)/shard_map/ppermute | solution.py:55
  218.9 2.3 %finish.1 = (bf16[1024,512]{1,0:T(8,128)(2,1)}, bf16[1024,512]{1,0:T(8,128)(2,1)}) custom-call(s32[1]{0:T(128)} %bitcast.refs_0_.core, bf16[1024,512]{1,0:T(8,128)(2,1)S(1)} %copy-done, bf16[1024,512]{1,0:T(8,128)(2,1)S(1)} %copy-done.3, f32[1024,512]{1,0:T(8,128)S(1)} %get-tuple-element.58.dk, f32[1024,512]{1,0:T(8,128)S(1)} %get-tuple-element.59.dv, ...), custom_call_target="tpu_custom_call" | custom-call | flops 500000000 | bytes 9437184 | tf_op jit(solution)/shard_map/finish/pallas_call | solution.py:505
  (132 shorter events, 36.2 us)
Async XLA Ops:
  7.2 112.4 %all-gather.2.cloned.1.call-start = ((), (), s32[]{:S(2)}) async-start(), calls=%async_computation.2 | async-start | bytes 10485760 | tf_op jit(solution)/shard_map/all_gather | solution.py:601
  7.9 213.3 %reduce-scatter.2.cloned.1.call-start = ((), (), s32[]{:S(2)}) async-start(), calls=%async_computation.1 | async-start | bytes 10485760 | tf_op jit(solution)/shard_map/reduce_scatter | solution.py:641
  9.3 2.8 %collective-permute-start = (bf16[1408,128]{1,0:T(8,128)(2,1)S(1)}, bf16[1408,128]{1,0:T(8,128)(2,1)S(1)}, u32[]{:S(2)}, u32[]{:S(2)}) collective-permute-start(bf16[1408,128]{1,0:T(8,128)(2,1)S(1)} %get-tuple-element.42), channel_id=1, source_target_pairs={{0,4},{4,0},{8,12},{12,8},{16,20},{20,16},{24,28},{28,24},{32,36},... | collective-permute-start | bytes 1081352 | tf_op jit(solution)/shard_map/ppermute | solution.py:55
  12.1 22.9 %copy-start.15 = (bf16[1408,128]{1,0:T(8,128)(2,1)}, bf16[1408,128]{1,0:T(8,128)(2,1)S(1)}, u32[]{:S(2)}) copy-start(bf16[1408,128]{1,0:T(8,128)(2,1)S(1)} %collective-permute-done.refs_2_) | copy-start | bytes 1081348
  12.1 11.0 %collective-permute-start.1 = (bf16[2240,128]{1,0:T(8,128)(2,1)S(1)}, bf16[2240,128]{1,0:T(8,128)(2,1)S(1)}, u32[]{:S(2)}, u32[]{:S(2)}) collective-permute-start(bf16[2240,128]{1,0:T(8,128)(2,1)S(1)} %start.1.refs_2_), channel_id=1, source_target_pairs={{0,8},{4,36},{8,16},{12,44},{16,24},{20,52},{24,0},{28,60},{32,40}... | collective-permute-start | bytes 1720328 | tf_op jit(solution)/shard_map/ppermute | solution.py:51
  13.9 9.2 %collective-permute-start.2 = (bf16[2240,128]{1,0:T(8,128)(2,1)S(1)}, bf16[2240,128]{1,0:T(8,128)(2,1)S(1)}, u32[]{:S(2)}, u32[]{:S(2)}) collective-permute-start(bf16[2240,128]{1,0:T(8,128)(2,1)S(1)} %start.1.refs_2_), channel_id=1, source_target_pairs={{0,24},{4,100},{8,0},{12,108},{16,8},{20,116},{24,16},{28,124},{32... | collective-permute-start | bytes 1720328 | tf_op jit(solution)/shard_map/ppermute | solution.py:51
  24.1 8.0 %collective-permute-start.3 = (bf16[1216,128]{1,0:T(8,128)(2,1)}, bf16[1216,128]{1,0:T(8,128)(2,1)S(1)}, u32[]{:S(2)}, u32[]{:S(2)}) collective-permute-start(bf16[1216,128]{1,0:T(8,128)(2,1)} %get-tuple-element.44), channel_id=1, source_target_pairs={{0,8},{4,36},{8,16},{12,44},{16,24},{20,52},{24,0},{28,60},{32,40}... | collective-permute-start | bytes 933896 | tf_op jit(solution)/shard_map/ppermute | solution.py:51
  25.4 5.8 %collective-permute-start.4 = (bf16[1024,128]{1,0:T(8,128)(2,1)}, bf16[1024,128]{1,0:T(8,128)(2,1)}, u32[]{:S(2)}, u32[]{:S(2)}) collective-permute-start(bf16[1024,128]{1,0:T(8,128)(2,1)} %get-tuple-element.45), channel_id=1, source_target_pairs={{0,24},{4,100},{8,0},{12,108},{16,8},{20,116},{24,16},{28,124},{32... | collective-permute-start | bytes 786440 | tf_op jit(solution)/shard_map/ppermute | solution.py:51
  35.5 31.0 %copy-start.8 = (bf16[8576,128]{1,0:T(8,128)(2,1)}, bf16[8576,128]{1,0:T(8,128)(2,1)S(1)}, u32[]{:S(2)}) copy-start(bf16[8576,128]{1,0:T(8,128)(2,1)S(1)} %get-tuple-element.47.rest_0_) | copy-start | bytes 6586372
  35.6 37.2 %copy-start.27 = (s32[64,4]{0,1:T(4,128)S(1)}, s32[64,4]{0,1:T(4,128)}, u32[]{:S(2)}) copy-start(s32[64,4]{0,1:T(4,128)} %param.11) | copy-start | bytes 3076
  35.6 51.3 %copy-start.21 = (s32[2,4]{1,0:T(2,128)S(1)}, s32[2,4]{1,0:T(2,128)}, u32[]{:S(2)}) copy-start(s32[2,4]{1,0:T(2,128)} %copy-done.20) | copy-start | bytes 100
  35.6 27.5 %collective-permute-start.5 = (bf16[8576,128]{1,0:T(8,128)(2,1)S(1)}, bf16[8576,128]{1,0:T(8,128)(2,1)S(1)}, u32[]{:S(2)}, u32[]{:S(2)}) collective-permute-start(bf16[8576,128]{1,0:T(8,128)(2,1)S(1)} %get-tuple-element.47.rest_0_), channel_id=1, source_target_pairs={{0,32},{4,12},{8,40},{12,20},{16,48},{20,28},{24,56},{28,4},{32,64... | collective-permute-start | bytes 6586376 | tf_op jit(solution)/shard_map/ppermute | solution.py:51
  36.5 26.6 %collective-permute-start.6 = (bf16[8576,128]{1,0:T(8,128)(2,1)S(1)}, bf16[8576,128]{1,0:T(8,128)(2,1)}, u32[]{:S(2)}, u32[]{:S(2)}) collective-permute-start(bf16[8576,128]{1,0:T(8,128)(2,1)S(1)} %get-tuple-element.47.rest_0_), channel_id=1, source_target_pairs={{0,96},{4,28},{8,104},{12,4},{16,112},{20,12},{24,120},{28,20},{32... | collective-permute-start | bytes 6586376 | tf_op jit(solution)/shard_map/ppermute | solution.py:51
  38.2 24.9 %collective-permute-start.7 = (bf16[8576,128]{1,0:T(8,128)(2,1)S(1)}, bf16[8576,128]{1,0:T(8,128)(2,1)S(1)}, u32[]{:S(2)}, u32[]{:S(2)}) collective-permute-start(bf16[8576,128]{1,0:T(8,128)(2,1)S(1)} %get-tuple-element.47.rest_0_), channel_id=1, source_target_pairs={{0,4},{4,0},{8,12},{12,8},{16,20},{20,16},{24,28},{28,24},{32,36},... | collective-permute-start | bytes 6586376 | tf_op jit(solution)/shard_map/ppermute | solution.py:55
  66.5 19.7 %collective-permute-start.8 = (bf16[4480,128]{1,0:T(8,128)(2,1)}, bf16[4480,128]{1,0:T(8,128)(2,1)}, u32[]{:S(2)}, u32[]{:S(2)}) collective-permute-start(bf16[4480,128]{1,0:T(8,128)(2,1)} %get-tuple-element.48), channel_id=1, source_target_pairs={{0,32},{4,12},{8,40},{12,20},{16,48},{20,28},{24,56},{28,4},{32,64... | collective-permute-start | bytes 3440648 | tf_op jit(solution)/shard_map/ppermute | solution.py:51
  67.5 14.3 %collective-permute-start.10 = (bf16[4096,128]{1,0:T(8,128)(2,1)}, bf16[4096,128]{1,0:T(8,128)(2,1)}, u32[]{:S(2)}, u32[]{:S(2)}) collective-permute-start(bf16[4096,128]{1,0:T(8,128)(2,1)} %get-tuple-element.49), channel_id=1, source_target_pairs={{0,96},{4,28},{8,104},{12,4},{16,112},{20,12},{24,120},{28,20},{32... | collective-permute-start | bytes 3145736 | tf_op jit(solution)/shard_map/ppermute | solution.py:51
  69.4 25.8 %collective-permute-start.11 = (bf16[8576,128]{1,0:T(8,128)(2,1)S(1)}, bf16[8576,128]{1,0:T(8,128)(2,1)}, u32[]{:S(2)}, u32[]{:S(2)}) collective-permute-start(bf16[8576,128]{1,0:T(8,128)(2,1)S(1)} %collective-permute-done.5.refs_0_.right.rest_1_), channel_id=1, source_target_pairs={{0,4},{4,0},{8,12},{12,8},{16,20},{20,16},{24,28},{28,24},{32,36},... | collective-permute-start | bytes 6586376 | tf_op jit(solution)/shard_map/ppermute | solution.py:55
  72.7 22.5 %collective-permute-start.14 = (bf16[8576,128]{1,0:T(8,128)(2,1)}, bf16[8576,128]{1,0:T(8,128)(2,1)}, u32[]{:S(2)}, u32[]{:S(2)}) collective-permute-start(bf16[8576,128]{1,0:T(8,128)(2,1)} %collective-permute-done.6.refs_1_.left.rest_4_), channel_id=1, source_target_pairs={{0,4},{4,0},{8,12},{12,8},{16,20},{20,16},{24,28},{28,24},{32,36},... | collective-permute-start | bytes 6586376 | tf_op jit(solution)/shard_map/ppermute | solution.py:55
  81.8 13.4 %collective-permute-start.13 = (bf16[4096,128]{1,0:T(8,128)(2,1)}, bf16[4096,128]{1,0:T(8,128)(2,1)}, u32[]{:S(2)}, u32[]{:S(2)}) collective-permute-start(bf16[4096,128]{1,0:T(8,128)(2,1)} %collective-permute-done.10.rest_3_), channel_id=1, source_target_pairs={{0,4},{4,0},{8,12},{12,8},{16,20},{20,16},{24,28},{28,24},{32,36},... | collective-permute-start | bytes 3145736 | tf_op jit(solution)/shard_map/ppermute | solution.py:55
  86.3 9.0 %collective-permute-start.12 = (bf16[4480,128]{1,0:T(8,128)(2,1)}, bf16[4480,128]{1,0:T(8,128)(2,1)}, u32[]{:S(2)}, u32[]{:S(2)}) collective-permute-start(bf16[4480,128]{1,0:T(8,128)(2,1)} %collective-permute-done.8.far.rest_2_), channel_id=1, source_target_pairs={{0,4},{4,0},{8,12},{12,8},{16,20},{20,16},{24,28},{28,24},{32,36},... | collective-permute-start | bytes 3440648 | tf_op jit(solution)/shard_map/ppermute | solution.py:55
  88.7 1.7 collective-permute-start.9
  135.3 8.0 %collective-permute-start.15 = (bf16[8,512,128]{2,1,0:T(8,128)(2,1)S(1)}, bf16[8,512,128]{2,1,0:T(8,128)(2,1)S(1)}, u32[]{:S(2)}, u32[]{:S(2)}) collective-permute-start(bf16[8,512,128]{2,1,0:T(8,128)(2,1)S(1)} %get-tuple-element.61), channel_id=1, source_target_pairs={{0,4},{4,0},{8,12},{12,8},{16,20},{20,16},{24,28},{28,24},{32,36},... | collective-permute-start | bytes 3145736 | tf_op jit(solution)/shard_map/ppermute | solution.py:55
  141.9 1.4 collective-permute-start.16
  144.7 16.5 %collective-permute-start.17 = (bf16[2,2240,128]{2,1,0:T(8,128)(2,1)S(1)}, bf16[2,2240,128]{2,1,0:T(8,128)(2,1)S(1)}, u32[]{:S(2)}, u32[]{:S(2)}) collective-permute-start(bf16[2,2240,128]{2,1,0:T(8,128)(2,1)S(1)} %get-tuple-element.62), channel_id=1, source_target_pairs={{0,32},{4,12},{8,40},{12,20},{16,48},{20,28},{24,56},{28,4},{32,64... | collective-permute-start | bytes 3440648 | tf_op jit(solution)/shard_map/ppermute | solution.py:51
  145.9 15.3 %collective-permute-start.18 = (bf16[2,2240,128]{2,1,0:T(8,128)(2,1)S(1)}, bf16[2,2240,128]{2,1,0:T(8,128)(2,1)S(1)}, u32[]{:S(2)}, u32[]{:S(2)}) collective-permute-start(bf16[2,2240,128]{2,1,0:T(8,128)(2,1)S(1)} %get-tuple-element.63), channel_id=1, source_target_pairs={{0,96},{4,28},{8,104},{12,4},{16,112},{20,12},{24,120},{28,20},{32... | collective-permute-start | bytes 3440648 | tf_op jit(solution)/shard_map/ppermute | solution.py:51
  163.6 28.8 %collective-permute-start.19 = (bf16[4,2240,128]{2,1,0:T(8,128)(2,1)S(1)}, bf16[4,2240,128]{2,1,0:T(8,128)(2,1)S(1)}, u32[]{:S(2)}, u32[]{:S(2)}) collective-permute-start(bf16[4,2240,128]{2,1,0:T(8,128)(2,1)S(1)} %get-tuple-element.64), channel_id=1, source_target_pairs={{0,32},{4,12},{8,40},{12,20},{16,48},{20,28},{24,56},{28,4},{32,64... | collective-permute-start | bytes 6881288 | tf_op jit(solution)/shard_map/ppermute | solution.py:51
  164.6 27.8 %collective-permute-start.20 = (bf16[4,2240,128]{2,1,0:T(8,128)(2,1)S(1)}, bf16[4,2240,128]{2,1,0:T(8,128)(2,1)S(1)}, u32[]{:S(2)}, u32[]{:S(2)}) collective-permute-start(bf16[4,2240,128]{2,1,0:T(8,128)(2,1)S(1)} %get-tuple-element.65), channel_id=1, source_target_pairs={{0,96},{4,28},{8,104},{12,4},{16,112},{20,12},{24,120},{28,20},{32... | collective-permute-start | bytes 6881288 | tf_op jit(solution)/shard_map/ppermute | solution.py:51
  195.8 7.5 %collective-permute-start.21 = (bf16[1216,128]{1,0:T(8,128)(2,1)S(1)}, bf16[1216,128]{1,0:T(8,128)(2,1)S(1)}, u32[]{:S(2)}, u32[]{:S(2)}) collective-permute-start(bf16[1216,128]{1,0:T(8,128)(2,1)S(1)} %get-tuple-element.69), channel_id=1, source_target_pairs={{0,8},{4,36},{8,16},{12,44},{16,24},{20,52},{24,0},{28,60},{32,40}... | collective-permute-start | bytes 933896 | tf_op jit(solution)/shard_map/ppermute | solution.py:51
  197.3 5.5 %collective-permute-start.22 = (bf16[1024,128]{1,0:T(8,128)(2,1)S(1)}, bf16[1024,128]{1,0:T(8,128)(2,1)S(1)}, u32[]{:S(2)}, u32[]{:S(2)}) collective-permute-start(bf16[1024,128]{1,0:T(8,128)(2,1)S(1)} %get-tuple-element.70), channel_id=1, source_target_pairs={{0,24},{4,100},{8,0},{12,108},{16,8},{20,116},{24,16},{28,124},{32... | collective-permute-start | bytes 786440 | tf_op jit(solution)/shard_map/ppermute | solution.py:51
  203.4 10.1 %collective-permute-start.23 = (bf16[2240,128]{1,0:T(8,128)(2,1)S(1)}, bf16[2240,128]{1,0:T(8,128)(2,1)S(1)}, u32[]{:S(2)}, u32[]{:S(2)}) collective-permute-start(bf16[2240,128]{1,0:T(8,128)(2,1)S(1)} %get-tuple-element.71), channel_id=1, source_target_pairs={{0,8},{4,36},{8,16},{12,44},{16,24},{20,52},{24,0},{28,60},{32,40}... | collective-permute-start | bytes 1720328 | tf_op jit(solution)/shard_map/ppermute | solution.py:51
  204.2 9.3 %collective-permute-start.24 = (bf16[2240,128]{1,0:T(8,128)(2,1)S(1)}, bf16[2240,128]{1,0:T(8,128)(2,1)S(1)}, u32[]{:S(2)}, u32[]{:S(2)}) collective-permute-start(bf16[2240,128]{1,0:T(8,128)(2,1)S(1)} %get-tuple-element.72), channel_id=1, source_target_pairs={{0,24},{4,100},{8,0},{12,108},{16,8},{20,116},{24,16},{28,124},{32... | collective-permute-start | bytes 1720328 | tf_op jit(solution)/shard_map/ppermute | solution.py:51
  213.8 5.1 %collective-permute-start.25 = (bf16[1216,128]{1,0:T(8,128)(2,1)S(1)}, bf16[1216,128]{1,0:T(8,128)(2,1)S(1)}, u32[]{:S(2)}, u32[]{:S(2)}) collective-permute-start(bf16[1216,128]{1,0:T(8,128)(2,1)S(1)} %get-tuple-element.74), channel_id=1, source_target_pairs={{0,4},{4,0},{8,12},{12,8},{16,20},{20,16},{24,28},{28,24},{32,36},... | collective-permute-start | bytes 933896 | tf_op jit(solution)/shard_map/ppermute | solution.py:55
  (26 other events, 121.1 us)
Sparse Core Ops, SparseCore 0:
  9.7 86.3 all-gather.1
  119.2 81.7 reduce-scatter.1

commit v3 on v2

--- a/solution.py
+++ b/solution.py
@@ -23,7 +23,6 @@
 HALF = LIN * HD // CORES
 UNIT = 4 * BLOCK + HALF
 FRONT = 2 * BLOCK + HALF
-LINE = 4 * 4 * BLOCK + 2 * HALF
 MID = 8 * BLOCK
 TILE = (BLOCK, HD)
 
@@ -55,39 +54,6 @@
     return lax.ppermute(value, "ctx", [(i, i ^ 1) for i in range(CTX)])
 
 
-def copies_kernel(moves, n_in, n_deps, *refs):
-    ins, outs, sems = refs[:n_in], refs[n_in + n_deps : -1], refs[-1]
-    copies = [
-        pltpu.make_async_copy(
-            ins[i].at[pl.ds(i0, n)], outs[o].at[pl.ds(o0, n)], sems.at[m]
-        )
-        for m, (i, i0, o, o0, n) in enumerate(moves)
-    ]
-    for copy in copies:
-        copy.start()
-    for copy in copies:
-        copy.wait()
-
-
-def copies(inputs, sizes, moves, deps=()):
-    anywhere = pl.BlockSpec(memory_space=pl.ANY)
-    return pl.pallas_call(
-        functools.partial(copies_kernel, moves, len(inputs), len(deps)),
-        in_specs=[anywhere] * (len(inputs) + len(deps)),
-        out_specs=[pl.BlockSpec(memory_space=pltpu.VMEM)] * len(sizes),
-        out_shape=[jax.ShapeDtypeStruct((n,) + inputs[0].shape[1:], BF) for n in sizes],
-        scratch_shapes=[pltpu.SemaphoreType.DMA((len(moves),))],
-        compiler_params=params(16),
-        cost_estimate=cost(0, sum(m[4] for m in moves) * math.prod(inputs[0].shape[1:]) * 4),
-        name="copies",
-    )(*inputs, *deps)
-
-
-def halves(right, left, n, deps=()):
-    m = left.shape[0] - n
-    return copies([right, left], [n, m], [(0, 0, 0, 0, n), (1, n, 1, 0, m)], deps)
-
-
 def drop(kernel, n_in, n_deps, *refs):
     kernel(*refs[:n_in], *refs[n_in + n_deps :])
 
@@ -154,7 +120,7 @@
     return high, (value - high.astype(F32)).astype(BF)
 
 
-def linear_forward_kernel(q_ref, k_ref, v_ref, c_ref, s_ref, out_ref):
+def linear_forward_kernel(q_ref, k_ref, v_ref, c_ref, s_ref, base_ref, out_ref):
     q, k, v, c = q_ref[...], k_ref[...], v_ref[...], c_ref[0:1, :]
     weights = jnp.where(causal_mask(), dot(k, q, 1, 1) * c, 0.0).astype(BF)
     hi, lo = split(s_ref[0, 0].T)
@@ -162,17 +128,18 @@
     out_ref[...] = out.T.astype(BF)
 
 
-def linear_forward(queries, keys, values, scale, before):
+def linear_forward(queries, keys, values, scale, before, base):
     return pl.pallas_call(
         linear_forward_kernel,
         grid=(2, LIN),
-        in_specs=[tile_spec()] * 3 + [scale_spec(), state_spec()],
+        in_specs=[tile_spec()] * 3 + [scale_spec(), state_spec(), ANY],
         out_specs=tile_spec(),
         out_shape=jax.ShapeDtypeStruct(queries.shape, BF),
-        compiler_params=params(24),
+        input_output_aliases={5: 0},
+        compiler_params=params(12),
         cost_estimate=cost(2.4e9, 4 * MIB),
         name="linear_forward",
-    )(queries, keys, values, scale, before)
+    )(queries, keys, values, scale, before, base)
 
 
 def linear_backward_kernel(
@@ -198,96 +165,105 @@
         out_specs=[tile_spec()] * 3,
         out_shape=[jax.ShapeDtypeStruct(shape, t) for t in (BF, F32, F32)],
         input_output_aliases={6: 0, 7: 1, 8: 2},
-        compiler_params=params(24),
+        compiler_params=params(16),
         cost_estimate=cost(5e9, 9 * MIB),
         name="linear_backward",
     )(queries, keys, values, grads, scale, before, *bases, dep)
 
 
-def sparse_forward_kernel(table, q_ref, k_ref, v_ref, base_ref, dep, *rest):
-    pieces = rest[:10]
-    out_ref, p_ref, kf_ref, vf_ref, s_ref, sems = rest[10:]
+PIECES = 16
+
+
+def sparse_forward_kernel(table, q_ref, k_ref, v_ref, *rest):
+    pieces = rest[:PIECES]
+    out_ref, p_ref, kf_ref, vf_ref, inv_ref, s_ref, sems = rest[PIECES:]
     step = pl.program_id(0)
-    for r in range(LISTED):
-        row = step * LISTED + r
-        for j in range(10):
-
-            @pl.when(table[row, 0] == j)
-            def _():
-                pltpu.make_async_copy(pieces[j].at[pl.ds(pl.multiple_of(table[row, 1] * HD, HD), BLOCK)], kf_ref.at[r], sems.at[0, r]).start()
-
-            @pl.when(table[row, 2] == j)
-            def _():
-                pltpu.make_async_copy(pieces[j].at[pl.ds(pl.multiple_of(table[row, 3] * HD, HD), BLOCK)], vf_ref.at[r], sems.at[1, r]).start()
+
+    @pl.when(step == 0)
+    def _():
+        @pl.loop(0, 2 * LISTED)
+        def _(row):
+            for j in range(PIECES):
+                for n, far in ((0, kf_ref), (1, vf_ref)):
+
+                    @pl.when(table[row, 2 * n] == j)
+                    def _():
+                        at = pl.ds(pl.multiple_of(table[row, 2 * n + 1] * HD, HD), BLOCK)
+                        pltpu.make_async_copy(pieces[j].at[at], far.at[row], sems.at[n, row]).start()
 
     q = q_ref[...]
     s = jnp.where(causal_mask(), dot(k_ref[...], q, 1, 1) * SCALING, -1e30)
     s_ref[0] = s
     peak = jnp.max(s, axis=0, keepdims=True)
     for r in range(LISTED):
-        pltpu.make_async_copy(pieces[0].at[pl.ds(0, BLOCK)], kf_ref.at[r], sems.at[0, r]).wait()
-        bias = jnp.where(table[step * LISTED + r, 4] == 1, 0.0, -1e30).astype(F32)
-        s = dot(kf_ref[r], q, 1, 1) * SCALING + bias
+        row = step * LISTED + r
+        pltpu.make_async_copy(pieces[0].at[pl.ds(0, BLOCK)], kf_ref.at[row], sems.at[0, row]).wait()
+        bias = jnp.where(table[row, 4] == 1, 0.0, -1e30).astype(F32)
+        s = dot(kf_ref[row], q, 1, 1) * SCALING + bias
         s_ref[r + 1] = s
         peak = jnp.maximum(peak, jnp.max(s, axis=0, keepdims=True))
     total = jnp.zeros((1, BLOCK), F32)
+    out = jnp.zeros((HD, BLOCK), F32)
     for r in range(LISTED + 1):
         e = jnp.exp(s_ref[r] - peak)
-        s_ref[r] = e
         total = total + jnp.sum(e, axis=0, keepdims=True)
-    inverse = 1.0 / total
-    out = jnp.zeros((HD, BLOCK), F32)
-    for r in range(LISTED + 1):
-        p = (s_ref[r] * inverse).astype(BF)
+        p = e.astype(BF)
         p_ref[0, r] = p
         if r == 0:
             value = v_ref[...]
         else:
-            pltpu.make_async_copy(pieces[0].at[pl.ds(0, BLOCK)], vf_ref.at[r - 1], sems.at[1, r - 1]).wait()
-            value = vf_ref[r - 1]
+            row = step * LISTED + r - 1
+            pltpu.make_async_copy(pieces[0].at[pl.ds(0, BLOCK)], vf_ref.at[row], sems.at[1, row]).wait()
+            value = vf_ref[row]
         out = out + dot(value, p, 0, 0)
-    out_ref[...] = out.T.astype(BF)
-
-
-def sparse_forward(table, queries, keys, values, base, dep, pieces):
+    inverse = 1.0 / total
+    inv_ref[...] = jnp.broadcast_to(inverse, (8, BLOCK))
+    out_ref[...] = (out * inverse).T.astype(BF)
+
+
+def sparse_forward(table, queries, keys, values, pieces):
     column = pl.BlockSpec(TILE, lambda i, t: (i, LIN))
-    anywhere = pl.BlockSpec(memory_space=pl.ANY)
+    far = (2 * LISTED, BLOCK, HD)
     return pl.pallas_call(
         sparse_forward_kernel,
         grid_spec=pltpu.PrefetchScalarGridSpec(
             num_scalar_prefetch=1,
             grid=(2,),
-            in_specs=[column] * 3 + [anywhere] * 12,
+            in_specs=[column] * 3 + [ANY] * PIECES,
             out_specs=[
                 column,
                 pl.BlockSpec((1, LISTED + 1, BLOCK, BLOCK), lambda i, t: (i, 0, 0, 0)),
-                pl.BlockSpec((LISTED, BLOCK, HD), lambda i, t: (i, 0, 0)),
-                pl.BlockSpec((LISTED, BLOCK, HD), lambda i, t: (i, 0, 0)),
+                pl.BlockSpec(far, lambda i, t: (0, 0, 0)),
+                pl.BlockSpec(far, lambda i, t: (0, 0, 0)),
+                pl.BlockSpec((8, BLOCK), lambda i, t: (0, i)),
             ],
             scratch_shapes=[
                 pltpu.VMEM((LISTED + 1, BLOCK, BLOCK), F32),
-                pltpu.SemaphoreType.DMA((2, LISTED)),
+                pltpu.SemaphoreType.DMA((2, 2 * LISTED)),
             ],
         ),
         out_shape=[
             jax.ShapeDtypeStruct(queries.shape, BF),
             jax.ShapeDtypeStruct((2, LISTED + 1, BLOCK, BLOCK), BF),
-            jax.ShapeDtypeStruct((2 * LISTED, BLOCK, HD), BF),
-            jax.ShapeDtypeStruct((2 * LISTED, BLOCK, HD), BF),
+            jax.ShapeDtypeStruct(far, BF),
+            jax.ShapeDtypeStruct(far, BF),
+            jax.ShapeDtypeStruct((8, queries.shape[0]), F32),
         ],
-        input_output_aliases={4: 0},
-        compiler_params=params(32),
+        compiler_params=params(20),
         cost_estimate=cost(4e9, 12 * MIB),
         name="sparse_forward",
-    )(table, queries, keys, values, base, dep, *pieces)
+    )(table, queries, keys, values, *pieces)
 
 
 def sparse_backward_kernel(
-    core, q_ref, k_ref, v_ref, g_ref, o_ref, p_ref, kf_ref, vf_ref, dep, dq_ref, dk_ref, dv_ref, mine_ref, sent_ref
+    core, q_ref, k_ref, v_ref, g_ref, o_ref, p_ref, kf_ref, vf_ref, inv_ref, dq_ref, dk_ref, dv_ref, mine_ref, sent_ref
 ):
     first = core[0] == 0
     q, g = q_ref[...], g_ref[...]
-    row_dot = jnp.sum((g.astype(F32) * o_ref[...].astype(F32)).T, axis=0, keepdims=True)
+    inverse = inv_ref[0:1, :]
+    turned = g.astype(F32).T * inverse
+    row_dot = jnp.sum(turned * o_ref[...].astype(F32).T, axis=0, keepdims=True)
+    g = turned.T.astype(BF)
     dq = jnp.zeros((HD, BLOCK), F32)
     for r in range(LISTED + 1):
         p = p_ref[0, r]
@@ -307,7 +283,7 @@
     dq_ref[...] = (dq * SCALING).T.astype(BF)
 
 
-def sparse_backward(core, queries, keys, values, grads, outs, probs, far_k, far_v, dep):
+def sparse_backward(core, queries, keys, values, grads, outs, probs, far_k, far_v, inverse):
     column = pl.BlockSpec(TILE, lambda i, c: (i, LIN))
     four = pl.BlockSpec((LISTED, BLOCK, HD), lambda i, c: (i, 0, 0))
     five = pl.BlockSpec((1, LISTED + 1, BLOCK, BLOCK), lambda i, c: (i, 0, 0, 0))
@@ -317,7 +293,8 @@
             num_scalar_prefetch=1,
             grid=(2,),
             in_specs=[column] * 3
-            + [pl.BlockSpec(TILE, lambda i, c: (i, 0)), column, five, four, four, ANY],
+            + [pl.BlockSpec(TILE, lambda i, c: (i, 0)), column, five, four, four]
+            + [pl.BlockSpec((8, BLOCK), lambda i, c: (0, i))],
             out_specs=[column, column, column, four, four],
         ),
         out_shape=[
@@ -327,10 +304,10 @@
             jax.ShapeDtypeStruct((2 * LISTED, BLOCK, HD), BF),
             jax.ShapeDtypeStruct((2 * LISTED, BLOCK, HD), BF),
         ],
-        compiler_params=params(32),
+        compiler_params=params(20),
         cost_estimate=cost(8e9, 12 * MIB),
         name="sparse_backward",
-    )(core, queries, keys, values, grads, outs, probs, far_k, far_v, dep)
+    )(core, queries, keys, values, grads, outs, probs, far_k, far_v, inverse)
 
 
 def begin_kernel(core, k_ref, v_ref, states, mine, sent):
@@ -348,24 +325,21 @@
     sent[0 : 2 * BLOCK] = jnp.where(first, v, k)
 
 
-def start_kernel(core, mine, got, states, out, scratch):
+def start_kernel(core, mine, got, states, out, rest, scratch):
     out[0 : 2 * BLOCK] = mine[...]
-    out[FRONT:] = got[0 : 2 * BLOCK]
+    rest[...] = got[0 : 2 * BLOCK]
     for h in range(LIN):
         other = got[2 * BLOCK + h * HD : 2 * BLOCK + (h + 1) * HD].astype(F32)
         scratch[h * HD : (h + 1) * HD] = states[0, h] + states[1, h] + other
     out[2 * BLOCK : FRONT] = scratch[pl.ds(pl.multiple_of(core[0] * HALF, HALF), HALF)].astype(BF)
 
 
-def line_kernel(core, earlier, start, right, far_a, far_b, left, line, local):
-    for spot, piece in ((0, start), (4 * BLOCK, right), (MID + 2 * HALF + 4 * BLOCK, left)):
-        line[spot : spot + 2 * BLOCK] = piece[0 : 2 * BLOCK]
-        line[spot + 2 * BLOCK : spot + 4 * BLOCK] = piece[FRONT:]
-    spot = MID + 2 * HALF
-    line[spot : spot + 2 * BLOCK] = far_a[0 : 2 * BLOCK]
-    line[spot + 2 * BLOCK : spot + 4 * BLOCK] = far_b[...]
+def line_kernel(core, earlier, sa, sb, ra, rb, fa, fb, la, lb, low, line, local):
+    for n, (one, two) in enumerate(((sa, fa), (sb, fb), (ra, la), (rb, lb))):
+        low[2 * BLOCK * n : 2 * BLOCK * (n + 1)] = one[0 : 2 * BLOCK]
+        line[2 * BLOCK * n : 2 * BLOCK * (n + 1)] = two[0 : 2 * BLOCK]
     first = core[0] == 0
-    s = [p[2 * BLOCK : FRONT].astype(F32) for p in (start, right, far_a, left)]
+    s = [p[2 * BLOCK : FRONT].astype(F32) for p in (sa, ra, fa, la)]
     m = [earlier[0, p].astype(F32) for p in range(SIDE)]
     before = s[1] * m[1] + s[2] * m[2] + s[3] * m[3]
     total = s[0] + s[1] + s[2] + s[3]
@@ -374,7 +348,8 @@
     local[...] = before
 
 
-def prefix_kernel(earlier, local, right, far, left, out, scratch, sems):
+def prefix_kernel(earlier, local, right, far, left, *rest):
+    out, scratch, sems = rest[-3:]
     got = [
         pltpu.make_async_copy(piece.at[pl.ds(MID, 2 * HALF)], scratch.at[n], sems.at[n])
         for n, piece in enumerate((right, far, left))
@@ -390,17 +365,17 @@
     out[...] = total
 
 
-def prefix(earlier, local, right, far, left):
+def prefix(earlier, local, right, far, left, deps):
     return pl.pallas_call(
         prefix_kernel,
-        in_specs=[SM, VM, ANY, ANY, ANY],
+        in_specs=[SM, VM] + [ANY] * (3 + len(deps)),
         out_specs=VM,
         out_shape=jax.ShapeDtypeStruct((HALF, HD), F32),
         scratch_shapes=[pltpu.VMEM((3, 2 * HALF, HD), BF), pltpu.SemaphoreType.DMA((3,))],
         compiler_params=params(4),
         cost_estimate=cost(1e5, MIB // 2),
         name="prefix",
-    )(earlier, local, right, far, left)
+    )(earlier, local, right, far, left, *deps)
 
 
 SPOTS = (0, BLOCK, FRONT, FRONT + BLOCK)
@@ -434,43 +409,44 @@
         fill(table, own, peer, half, 10 + u, far_b, u)
 
 
+def free_kernel(table, own, peer, half, right, left):
+    @pl.loop(0, 2)
+    def _(u):
+        fill(table, own, peer, half, 6 + u, right, u)
+        fill(table, own, peer, half, 12 + u, left, u)
+
+
 def near_kernel(table, own, peer, half, ra, rb, right, left):
     @pl.loop(0, 2)
     def _(u):
         fill(table, own, peer, half, 4 + u, right, u, [ra], u)
-        fill(table, own, peer, half, 6 + u, right, u + 2)
-        fill(table, own, peer, half, 12 + u, left, u)
-        fill(table, own, peer, half, 14 + u, left, u + 2, [rb], u)
-
-
-def turn_kernel(table, own, peer, half, r1, r3, home, right, far_a, far_b, left, unit):
-    @pl.loop(0, SIDE)
+        fill(table, own, peer, half, 14 + u, left, u, [rb], u)
+
+
+def turn_kernel(table, own, peer, half, rl, rh, ll, lh, home, right_a, right_b, far_a, far_b, left_a, left_b, unit):
+    @pl.loop(0, 2)
     def _(u):
-        fill(table, own, peer, half, u, unit, u, [r1, r3], u)
+        fill(table, own, peer, half, u, unit, u, [rl, ll], u)
+        fill(table, own, peer, half, 2 + u, unit, 2 + u, [rh, lh], u)
 
     home[...] = unit[0]
-    right[...] = unit[1]
-    far_a[...] = unit[2, 0:FRONT]
-    far_b[...] = unit[2, FRONT:]
-    left[...] = unit[3]
+    for n, (a, b) in ((1, (right_a, right_b)), (2, (far_a, far_b)), (3, (left_a, left_b))):
+        a[...] = unit[n, 0:FRONT]
+        b[...] = unit[n, FRONT:]
 
 
 def last_kernel(right, left, ra, rb, o_right, o_left):
-    o_right[0:FRONT] = (right[0:FRONT].astype(F32) + ra[...].astype(F32)).astype(BF)
-    o_right[FRONT:] = right[FRONT:]
-    o_left[0:FRONT] = left[0:FRONT]
-    o_left[FRONT:] = (left[FRONT:].astype(F32) + rb[...].astype(F32)).astype(BF)
-
-
-def tail_kernel(home, r1, r3, mine, sent, extra):
-    def total(a, b):
-        return home[a:b].astype(F32) + r1[a:b].astype(F32) + r3[a:b].astype(F32)
-
-    mine[...] = total(0, 2 * BLOCK).astype(BF)
-    more = total(2 * BLOCK, FRONT)
-    extra[...] = more
-    sent[0 : 2 * BLOCK] = total(FRONT, UNIT).astype(BF)
-    sent[2 * BLOCK :] = more.astype(BF)
+    o_right[...] = (right[...].astype(F32) + ra[...].astype(F32)).astype(BF)
+    o_left[...] = (left[...].astype(F32) + rb[...].astype(F32)).astype(BF)
+
+
+def tail_kernel(home, ra, rb, la, lb, mine, sent, extra):
+    front = home[0:FRONT].astype(F32) + ra[...].astype(F32) + la[...].astype(F32)
+    mine[...] = front[0 : 2 * BLOCK].astype(BF)
+    extra[...] = front[2 * BLOCK :]
+    sent[2 * BLOCK :] = front[2 * BLOCK :].astype(BF)
+    back = home[FRONT:].astype(F32) + rb[...].astype(F32) + lb[...].astype(F32)
+    sent[0 : 2 * BLOCK] = back.astype(BF)
 
 
 def finish_kernel(core, k_ref, v_ref, dk, dv, mine_ref, got_ref, tail_ref, extra, adj, peer, kg, vg, scratch):
@@ -543,11 +519,8 @@
 
 def piece_of(blocks, place, stream):
     outer, first, rest = spot_of(blocks, place, stream)
-    late = first >= 2
-    second = (outer == 2) & late
-    piece = jnp.where(outer < 2, outer, jnp.where(outer == 3, 4, jnp.where(second, 3, 2)))
-    index = first * 16 + rest * 4 + jnp.where(late, 3, 0) - jnp.where(second, 35, 0)
-    return piece + 5 * (place % CORES != stream).astype(jnp.int32), index
+    index = first % 2 * 16 + rest * 4
+    return outer * 2 + first // 2 + 8 * (place % CORES != stream).astype(jnp.int32), index
 
 
 def fetch_table(lists, place):
@@ -608,24 +581,25 @@
         "begin",
     )
     got = swap(sent)
-    (start,) = whole_call(
-        start_kernel, [core], [mine, got, states], [((UNIT, HD), BF)], "start",
+    sa, sb = whole_call(
+        start_kernel, [core], [mine, got, states], [((FRONT, HD), BF), ((2 * BLOCK, HD), BF)], "start",
         scratch=[pltpu.VMEM((LIN * HD, HD), F32)],
     )
-    a_right, a_left = ring_move(start, 0, 1), ring_move(start, 0, -1)
-    cut = halves(a_right, a_left, FRONT)
-    a_far = ring_move(cut[0], 0, 1), ring_move(cut[1], 0, -1)
-    line, inside = whole_call(
-        line_kernel, [core, earlier], [start, a_right, *a_far, a_left],
-        [((LINE, HD), BF), ((HALF, HD), F32)], "line",
-    )
-    b_right, b_left = ring_move(line, 1, 1), ring_move(line, 1, -1)
-    line_swapped = swap(line)
-    cut = halves(b_right, b_left, MID + 2 * HALF, [line_swapped])
-    b_far = ring_move(cut[0], 1, 1), ring_move(cut[1], 1, -1)
-    pieces = [line, b_right, *b_far, b_left]
-    pieces = pieces + [line_swapped] + [swap(p) for p in pieces[1:]]
-    part = prefix(earlier, inside, b_right, b_far[0], b_left)
+    ra, lb = ring_move(sa, 0, 1), ring_move(sb, 0, -1)
+    rb, la = ring_move(sb, 0, 1), ring_move(sa, 0, -1)
+    fa, fb = ring_move(ra, 0, 1), ring_move(lb, 0, -1)
+    low, high, inside = whole_call(
+        line_kernel, [core, earlier], [sa, sb, ra, rb, fa, fb, la, lb],
+        [((MID, HD), BF), ((MID + 2 * HALF, HD), BF), ((HALF, HD), F32)], "line",
+    )
+    low_right, low_left = ring_move(low, 1, 1), ring_move(low, 1, -1)
+    high_left, high_right = ring_move(high, 1, -1), ring_move(high, 1, 1)
+    low_far, high_far = ring_move(low_right, 1, 1), ring_move(high_left, 1, -1)
+    pieces = [low, high, low_right, high_right, low_far, high_far, low_left, high_left]
+    swapped = [swap(p) for p in pieces]
+    pieces = pieces + swapped
+    done = [low_far, low_left, *swapped[:4], *swapped[6:]]
+    part = prefix(earlier, inside, high_right, high_far, high_left, done)
     other = swap(part)
     on_keys = place % CORES == 0
     chip = jnp.where(on_keys, jnp.concatenate([part, other]), jnp.concatenate([other, part]))
@@ -633,16 +607,14 @@
     chip = chip.reshape(LIN, HD, HD)
     before = jnp.stack([chip, chip + states[0]])
 
-    attention = linear_forward(queries, keys, values, scale, before)
-    attention, probs, far_k, far_v = sparse_forward(
-        fetch, queries, keys, values, attention, inside, pieces
-    )
+    sparse_out, probs, far_k, far_v, inverse = sparse_forward(fetch, queries, keys, values, pieces)
+    attention = linear_forward(queries, keys, values, scale, before, sparse_out)
     partial_out = dot(attention, out_weight, 1, 1).astype(BF)
     layer_out = lax.psum_scatter(partial_out, "head", scatter_dimension=1, tiled=True)
     sparse_grad = dot(grad_all, out_weight[:, LIN * HD :], 1, 0).astype(BF)
     linear_grad = dot(grad_all, out_weight[:, : LIN * HD], 1, 0).astype(BF)
     query_grad, own_dk, own_dv, pair_mine, pair_sent = sparse_backward(
-        core, queries, keys, values, sparse_grad, attention, probs, far_k, far_v, inside
+        core, queries, keys, values, sparse_grad, attention, probs, far_k, far_v, inverse
     )
 
     adjoints = block_adjoints(queries, linear_grad, scale)
@@ -655,29 +627,28 @@
     far_a, far_b = whole_call(
         far_kernel, [back], base, [((2, UNIT, HD), BF)] * 2, "back_far"
     )
-    r1, r3 = ring_move(far_a, 1, 1), ring_move(far_b, 1, -1)
-    near = whole_call(
-        near_kernel, [back], base + [r1, r3], [((SIDE, UNIT, HD), BF)] * 2, "back_near"
-    )
-    r1, r3 = ring_move(near[0], 1, 1), ring_move(near[1], 1, -1)
-
+    ra, rb = ring_move(far_a, 1, 1), ring_move(far_b, 1, -1)
+    pair = [((2, UNIT, HD), BF)] * 2
+    free = whole_call(free_kernel, [back], base, pair, "back_free", deps=[far_a])
+    rh, ll = ring_move(free[0], 1, 1), ring_move(free[1], 1, -1)
+    near = whole_call(near_kernel, [back], base + [ra, rb], pair, "back_near")
+    rl, lh = ring_move(near[0], 1, 1), ring_move(near[1], 1, -1)
     query_grad, own_dk, own_dv = linear_backward(
         queries, keys, values, linear_grad, scale, before, (query_grad, own_dk, own_dv), inside
     )
 
-    home, right, far_a, far_b, left = whole_call(
-        turn_kernel, [back], base + [r1, r3],
-        [((UNIT, HD), BF), ((UNIT, HD), BF), ((FRONT, HD), BF), ((2 * BLOCK, HD), BF), ((UNIT, HD), BF)],
+    front, rear = ((FRONT, HD), BF), ((2 * BLOCK, HD), BF)
+    home, right_a, right_b, far_a, far_b, left_a, left_b = whole_call(
+        turn_kernel, [back], base + [rl, rh, ll, lh], [((UNIT, HD), BF)] + [front, rear] * 3,
         "back_turn", deps=[query_grad], scratch=[pltpu.VMEM((SIDE, UNIT, HD), BF)],
     )
-    r1, r3 = ring_move(far_a, 0, 1), ring_move(far_b, 0, -1)
-    right, left = whole_call(
-        last_kernel, [], [right, left, r1, r3], [((UNIT, HD), BF)] * 2, "back_last"
-    )
-    r1, r3 = ring_move(right, 0, 1), ring_move(left, 0, -1)
+    ra, rb = ring_move(far_a, 0, 1), ring_move(far_b, 0, -1)
+    to_rb, to_la = ring_move(right_b, 0, 1), ring_move(left_a, 0, -1)
+    right_a, left_b = whole_call(last_kernel, [], [right_a, left_b, ra, rb], [front, rear], "back_last")
+    to_ra, to_lb = ring_move(right_a, 0, 1), ring_move(left_b, 0, -1)
     mine, sent, extra = whole_call(
-        tail_kernel, [], [home, r1, r3],
-        [((2 * BLOCK, HD), BF), ((FRONT, HD), BF), ((HALF, HD), F32)], "back_tail",
+        tail_kernel, [], [home, to_ra, to_rb, to_la, to_lb],
+        [rear, front, ((HALF, HD), F32)], "back_tail",
     )
     key_grad, value_grad = finish(
         core, keys, values, own_dk, own_dv, mine, swap(sent), extra, adjoints, adjoint_peer

time: 229 us -> 217 us (0.948)
  waiting for transfers between devices: 92.4 us -> 67 us
  starting transfers between devices: 41.5 us -> 53.1 us
  local copies, waits for them, and re-layouts: 10.3 us -> 18.3 us
  Pallas kernels: 48.2 us -> 44.5 us
    ppermute x16 -> x24, waiting for transfers between devices: 86.7 us -> 61.6 us  [ring_move(): return lax.ppermute(value, 'ctx', pairs)]
    unnamed x60 -> x66, local copies, waits for them, and re-layouts: 9.71 us -> 17.8 us
    ppermute x16 -> x24, starting transfers between devices: 24.3 us -> 31.5 us  [ring_move(): return lax.ppermute(value, 'ctx', pairs)]
    ppermute x10 -> x13, starting transfers between devices: 17.2 us -> 21.6 us  [swap(): return lax.ppermute(value, 'ctx', [(i, i ^ 1) for i in range(CTX)])]
    pallas_call x3 -> x1, Pallas kernels: 6.08 us -> 1.85 us  [prefix(): pl.pallas_call(prefix_kernel, in_specs=[SM, VM] + [ANY] * (3 + len(deps))...]
    pallas_call x8 -> x9, Pallas kernels: 8.04 us -> 9.52 us  [whole_call(): pl.pallas_call(functools.partial(drop, kernel, n_in, len(deps)), in_specs...]
    ppermute x10 -> x13, waiting for transfers between devices: 4.9 us -> 4.76 us  [swap(): return lax.ppermute(value, 'ctx', [(i, i ^ 1) for i in range(CTX)])]
  transfers between devices with their start and end apart: 28 -> 39, of which waited for: 14 -> 16; matrix products, arithmetic and copies ran while one was open for 10% -> 9% of each run, Pallas kernels for 21% -> 21%
where the time goes in v3:
time: 217 us; the launch traced here: 216 us
  waiting for transfers between devices  67 us (31%)
  starting transfers between devices  53.1 us (24%)
  Pallas kernels  44.5 us (21%)
  local copies, waits for them, and re-layouts  18.3 us (8%)
  matrix products  17.5 us (8%)
  between operations  14.6 us (7%)
    ppermute x24, waiting for transfers between devices, ring_move(): return lax.ppermute(value, 'ctx', pairs)  61.6 us
    ppermute x24, starting transfers between devices, ring_move(): return lax.ppermute(value, 'ctx', pairs)  31.5 us
    ppermute x13, starting transfers between devices, swap(): return lax.ppermute(value, 'ctx', [(i, i ^ 1) for i in range(CTX)])  21.6 us
    unnamed x66, local copies, waits for them, and re-layouts  17.8 us
    dot_general x3, matrix products, dot(): lax.dot_general(a, b, (((ca,), (cb,)), ((), ())), preferred_element_type=...  17.5 us
    pallas_call x1, Pallas kernels, sparse_forward(): pl.pallas_call(sparse_forward_kernel, grid_spec=pltpu.PrefetchScalarGridS...  10.3 us
    pallas_call x9, Pallas kernels, whole_call(): pl.pallas_call(functools.partial(drop, kernel, n_in, len(deps)), in_specs...  9.52 us
    pallas_call x1, Pallas kernels, linear_backward(): pl.pallas_call(linear_backward_kernel, grid=(2, LIN), in_specs=[tile_spec...  7.42 us
  transfers between devices with their start and end apart: 39, of which 16 were waited for; matrix products, arithmetic and copies ran while one was open for 9% of the time, Pallas kernels for 21%

profile of v3, /device:TPU:1, one launch (start us, length us, event | category | flops | bytes accessed | tf_op | source)
XLA Modules:
  0.0 216.4 jit_solution(13431173800715898787)
XLA Ops:
  15.4 2.1 collective-permute-start.4
  18.9 2.8 %collective-permute-done.1.refs_4_ = bf16[1216,128]{1,0:T(8,128)(2,1)S(1)} collective-permute-done((bf16[1216,128]{1,0:T(8,128)(2,1)S(1)}, bf16[1216,128]{1,0:T(8,128)(2,1)S(1)}, u32[]{:S(2)}, u32[]{:S(2)}) %collective-permute-start.1) | collective-permute-done | bytes 311328 | tf_op jit(solution)/shard_map/ppermute | solution.py:50
  24.5 7.4 %collective-permute-done.2.refs_5_ = bf16[1024,128]{1,0:T(8,128)(2,1)} collective-permute-done((bf16[1024,128]{1,0:T(8,128)(2,1)}, bf16[1024,128]{1,0:T(8,128)(2,1)}, u32[]{:S(2)}, u32[]{:S(2)}) %collective-permute-start.2) | collective-permute-done | bytes 262176 | tf_op jit(solution)/shard_map/ppermute | solution.py:50
  37.7 3.1 %collective-permute-start.13 = (bf16[4096,128]{1,0:T(8,128)(2,1)S(1)}, bf16[4096,128]{1,0:T(8,128)(2,1)S(1)}, u32[]{:S(2)}, u32[]{:S(2)}) collective-permute-start(bf16[4096,128]{1,0:T(8,128)(2,1)S(1)} %get-tuple-element.52.rest_0_), channel_id=1, source_target_pairs={{0,4},{4,0},{8,12},{12,8},{16,20},{20,16},{24,28},{28,24},{32,36},... | collective-permute-start | bytes 3145736 | tf_op jit(solution)/shard_map/ppermute | solution.py:54
  41.8 7.0 %collective-permute-done.10.rest_2_ = bf16[4096,128]{1,0:T(8,128)(2,1)} collective-permute-done((bf16[4096,128]{1,0:T(8,128)(2,1)S(1)}, bf16[4096,128]{1,0:T(8,128)(2,1)}, u32[]{:S(2)}, u32[]{:S(2)}) %collective-permute-start.10) | collective-permute-done | bytes 1048608 | tf_op jit(solution)/shard_map/ppermute | solution.py:50
  48.8 2.9 %collective-permute-start.14 = (bf16[4480,128]{1,0:T(8,128)(2,1)S(1)}, bf16[4480,128]{1,0:T(8,128)(2,1)S(1)}, u32[]{:S(2)}, u32[]{:S(2)}) collective-permute-start(bf16[4480,128]{1,0:T(8,128)(2,1)S(1)} %get-tuple-element.51.rest_1_), channel_id=1, source_target_pairs={{0,4},{4,0},{8,12},{12,8},{16,20},{20,16},{24,28},{28,24},{32,36},... | collective-permute-start | bytes 3440648 | tf_op jit(solution)/shard_map/ppermute | solution.py:54
  52.7 8.3 %collective-permute-done.8.left.rest_7_ = bf16[4480,128]{1,0:T(8,128)(2,1)S(1)} collective-permute-done((bf16[4480,128]{1,0:T(8,128)(2,1)S(1)}, bf16[4480,128]{1,0:T(8,128)(2,1)S(1)}, u32[]{:S(2)}, u32[]{:S(2)}) %collective-permute-start.8) | collective-permute-done | bytes 1146912 | tf_op jit(solution)/shard_map/ppermute | solution.py:50
  61.0 2.9 %collective-permute-start.9 = (bf16[4480,128]{1,0:T(8,128)(2,1)S(1)}, bf16[4480,128]{1,0:T(8,128)(2,1)}, u32[]{:S(2)}, u32[]{:S(2)}) collective-permute-start(bf16[4480,128]{1,0:T(8,128)(2,1)S(1)} %collective-permute-done.8.left.rest_7_), channel_id=1, source_target_pairs={{0,96},{4,28},{8,104},{12,4},{16,112},{20,12},{24,120},{28,20},{32... | collective-permute-start | bytes 3440648 | tf_op jit(solution)/shard_map/ppermute | solution.py:50
  64.8 3.3 %collective-permute-start.15 = (bf16[4096,128]{1,0:T(8,128)(2,1)}, bf16[4096,128]{1,0:T(8,128)(2,1)}, u32[]{:S(2)}, u32[]{:S(2)}) collective-permute-start(bf16[4096,128]{1,0:T(8,128)(2,1)} %collective-permute-done.10.rest_2_), channel_id=1, source_target_pairs={{0,4},{4,0},{8,12},{12,8},{16,20},{20,16},{24,28},{28,24},{32,36},... | collective-permute-start | bytes 3145736 | tf_op jit(solution)/shard_map/ppermute | solution.py:54
  69.6 2.7 %collective-permute-done.11.rest_0_.rest_4_ = bf16[4096,128]{1,0:T(8,128)(2,1)} collective-permute-done((bf16[4096,128]{1,0:T(8,128)(2,1)}, bf16[4096,128]{1,0:T(8,128)(2,1)}, u32[]{:S(2)}, u32[]{:S(2)}) %collective-permute-start.11) | collective-permute-done | bytes 1048608 | tf_op jit(solution)/shard_map/ppermute | solution.py:50
  72.3 2.9 %collective-permute-start.17 = (bf16[4096,128]{1,0:T(8,128)(2,1)}, bf16[4096,128]{1,0:T(8,128)(2,1)}, u32[]{:S(2)}, u32[]{:S(2)}) collective-permute-start(bf16[4096,128]{1,0:T(8,128)(2,1)} %collective-permute-done.12.rest_1_.rest_6_), channel_id=1, source_target_pairs={{0,4},{4,0},{8,12},{12,8},{16,20},{20,16},{24,28},{28,24},{32,36},... | collective-permute-start | bytes 3145736 | tf_op jit(solution)/shard_map/ppermute | solution.py:54
  76.6 3.9 %collective-permute-start.21 = (bf16[4480,128]{1,0:T(8,128)(2,1)}, bf16[4480,128]{1,0:T(8,128)(2,1)}, u32[]{:S(2)}, u32[]{:S(2)}) collective-permute-start(bf16[4480,128]{1,0:T(8,128)(2,1)} %collective-permute-done.9.far.rest_5_), channel_id=1, source_target_pairs={{0,4},{4,0},{8,12},{12,8},{16,20},{20,16},{24,28},{28,24},{32,36},... | collective-permute-start | bytes 3440648 | tf_op jit(solution)/shard_map/ppermute | solution.py:54
  87.7 10.3 %sparse_forward.1 = (bf16[1024,512]{1,0:T(8,128)(2,1)S(1)}, bf16[2,5,512,512]{3,2,1,0:T(8,128)(2,1)S(1)}, bf16[8,512,128]{2,1,0:T(8,128)(2,1)S(1)}, bf16[8,512,128]{2,1,0:T(8,128)(2,1)S(1)}, f32[8,1024]{1,0:T(8,128)S(1)}) custom-call(s32[8,5]{1,0:T(8,128)S(1)} %stack.14.table, bf16[1024,512]{1,0:T(8,128)(2,1)S(1)} %copy-done.8, ...), custom_call_target="tpu_custom_call" | custom-call | flops 4000000000 | bytes 12582912 | tf_op jit(solution)/shard_map/sparse_forward/pallas_call | solution.py:227
  98.0 2.3 %copy-done.20 = bf16[2,5,512,512]{3,2,1,0:T(8,128)(2,1)} copy-done((bf16[2,5,512,512]{3,2,1,0:T(8,128)(2,1)}, bf16[2,5,512,512]{3,2,1,0:T(8,128)(2,1)S(1)}, u32[]{:S(2)}) %copy-start.20) | copy-done | bytes 5242904
  102.3 3.8 %linear_forward.1.o_ref = bf16[1024,512]{1,0:T(8,128)(2,1)S(1)} custom-call(bf16[1024,512]{1,0:T(8,128)(2,1)S(1)} %copy-done.8, bf16[1024,512]{1,0:T(8,128)(2,1)S(1)} %copy-done, bf16[1024,512]{1,0:T(8,128)(2,1)S(1)} %copy-done.1, f32[8,1024]{1,0:T(8,128)S(1)} %broadcast_in_dim.32.c_ref, ...), custom_call_target="tpu_custom_call", output_to_operand_aliasing={{}: (5, {})} | custom-call | flops 2400000000 | bytes 4194304 | tf_op jit(solution)/shard_map/linear_forward/pallas_call | solution.py:132
  106.1 6.9 %convolution_convert_fusion = bf16[1024,4096]{1,0:T(8,128)(2,1)} fusion(bf16[1024,512]{1,0:T(8,128)(2,1)S(1)} %linear_forward.1.o_ref, bf16[4096,512]{1,0:T(8,128)(2,1)S(1)} %copy-done.29), kind=kOutput, calls=%fused_computation | convolution fusion | flops 4299161600 | bytes 13631488 | tf_op jit(solution)/shard_map/dot_general | solution.py:31
  114.6 6.1 %convolution_convert_fusion.1.g_ref = bf16[1024,128]{1,0:T(8,128)(2,1)S(1)} fusion(bf16[1024,4096]{1,0:T(8,128)(2,1)} %all-gather.2.cloned.1.call-done, bf16[4096,512]{1,0:T(8,128)(2,1)} %param.9), kind=kOutput, calls=%fused_computation.4 | convolution fusion | flops 1073872896 | bytes 9699328 | tf_op jit(solution)/shard_map/dot_general | solution.py:31
  120.7 3.2 %copy-done.21 = bf16[2,5,512,512]{3,2,1,0:T(8,128)(2,1)S(1)} copy-done((bf16[2,5,512,512]{3,2,1,0:T(8,128)(2,1)S(1)}, bf16[2,5,512,512]{3,2,1,0:T(8,128)(2,1)}, u32[]{:S(2)}) %copy-start.21) | copy-done | bytes 5242904
  124.0 7.3 %sparse_backward.1 = (bf16[1024,512]{1,0:T(8,128)(2,1)}, f32[1024,512]{1,0:T(8,128)S(1)}, f32[1024,512]{1,0:T(8,128)S(1)}, bf16[8,512,128]{2,1,0:T(8,128)(2,1)S(1)}, bf16[8,512,128]{2,1,0:T(8,128)(2,1)S(1)}) custom-call(s32[1]{0:T(128)} %bitcast.refs_0_.core, bf16[1024,512]{1,0:T(8,128)(2,1)S(1)} %copy-done.9, bf16[1024,512]{1,0:T(8,128)(2,1)S(1)} %copy-done, ...), custom_call_target="tpu_custom_call" | custom-call | flops 8000000000 | bytes 12582912 | tf_op jit(solution)/shard_map/sparse_backward/pallas_call | solution.py:290
  131.4 4.5 %fusion.2.g_ref = bf16[1024,384]{1,0:T(8,128)(2,1)S(1)} fusion(bf16[1024,4096]{1,0:T(8,128)(2,1)S(1)} %bitcast.16, bf16[4096,512]{1,0:T(8,128)(2,1)S(1)} %copy-done.30), kind=kOutput, calls=%fused_computation.3 | convolution fusion | flops 3221618688 | bytes 12320768 | tf_op jit(solution)/shard_map/dot_general | solution.py:31
  140.7 2.7 %collective-permute-start.25 = (bf16[2,2240,128]{2,1,0:T(8,128)(2,1)S(1)}, bf16[2,2240,128]{2,1,0:T(8,128)(2,1)S(1)}, u32[]{:S(2)}, u32[]{:S(2)}) collective-permute-start(bf16[2,2240,128]{2,1,0:T(8,128)(2,1)S(1)} %get-tuple-element.67), channel_id=1, source_target_pairs={{0,96},{4,28},{8,104},{12,4},{16,112},{20,12},{24,120},{28,20},{32... | collective-permute-start | bytes 3440648 | tf_op jit(solution)/shard_map/ppermute | solution.py:50
  144.8 2.7 %collective-permute-start.28 = (bf16[2,2240,128]{2,1,0:T(8,128)(2,1)S(1)}, bf16[2,2240,128]{2,1,0:T(8,128)(2,1)S(1)}, u32[]{:S(2)}, u32[]{:S(2)}) collective-permute-start(bf16[2,2240,128]{2,1,0:T(8,128)(2,1)S(1)} %get-tuple-element.70), channel_id=1, source_target_pairs={{0,96},{4,28},{8,104},{12,4},{16,112},{20,12},{24,120},{28,20},{32... | collective-permute-start | bytes 3440648 | tf_op jit(solution)/shard_map/ppermute | solution.py:50
  147.5 9.5 %collective-permute-done.24.refs_4_ = bf16[2,2240,128]{2,1,0:T(8,128)(2,1)S(1)} collective-permute-done((bf16[2,2240,128]{2,1,0:T(8,128)(2,1)S(1)}, bf16[2,2240,128]{2,1,0:T(8,128)(2,1)S(1)}, u32[]{:S(2)}, u32[]{:S(2)}) %collective-permute-start.24) | collective-permute-done | bytes 1146912 | tf_op jit(solution)/shard_map/ppermute | solution.py:50
  158.7 2.7 %collective-permute-start.29 = (bf16[2,2240,128]{2,1,0:T(8,128)(2,1)S(1)}, bf16[2,2240,128]{2,1,0:T(8,128)(2,1)S(1)}, u32[]{:S(2)}, u32[]{:S(2)}) collective-permute-start(bf16[2,2240,128]{2,1,0:T(8,128)(2,1)S(1)} %get-tuple-element.71), channel_id=1, source_target_pairs={{0,96},{4,28},{8,104},{12,4},{16,112},{20,12},{24,120},{28,20},{32... | collective-permute-start | bytes 3440648 | tf_op jit(solution)/shard_map/ppermute | solution.py:50
  161.5 7.4 %linear_backward.1 = (bf16[1024,512]{1,0:T(8,128)(2,1)}, f32[1024,512]{1,0:T(8,128)S(1)}, f32[1024,512]{1,0:T(8,128)S(1)}) custom-call(bf16[1024,512]{1,0:T(8,128)(2,1)S(1)} %copy-done.9, bf16[1024,512]{1,0:T(8,128)(2,1)S(1)} %copy-done, bf16[1024,512]{1,0:T(8,128)(2,1)S(1)} %copy-done.1, ...), custom_call_target="tpu_custom_call", output_to_operand_aliasing={{0}: (6, {}), {1}: (7, {}), {2}: (8, {})} | custom-call | flops 5000000000 | bytes 9437184 | tf_op jit(solution)/shard_map/linear_backward/pallas_call | solution.py:161
  169.3 12.3 %collective-permute-done.26.refs_4_ = bf16[2,2240,128]{2,1,0:T(8,128)(2,1)S(1)} collective-permute-done((bf16[2,2240,128]{2,1,0:T(8,128)(2,1)S(1)}, bf16[2,2240,128]{2,1,0:T(8,128)(2,1)S(1)}, u32[]{:S(2)}, u32[]{:S(2)}) %collective-permute-start.26) | collective-permute-done | bytes 1146912 | tf_op jit(solution)/shard_map/ppermute | solution.py:50
  182.8 2.1 back_turn.1
  185.0 3.3 %collective-permute-start.31 = (bf16[1024,128]{1,0:T(8,128)(2,1)S(1)}, bf16[1024,128]{1,0:T(8,128)(2,1)S(1)}, u32[]{:S(2)}, u32[]{:S(2)}) collective-permute-start(bf16[1024,128]{1,0:T(8,128)(2,1)S(1)} %get-tuple-element.76), channel_id=1, source_target_pairs={{0,24},{4,100},{8,0},{12,108},{16,8},{20,116},{24,16},{28,124},{32... | collective-permute-start | bytes 786440 | tf_op jit(solution)/shard_map/ppermute | solution.py:50
  189.7 1.9 collective-permute-done.31.refs_3_
  196.2 6.9 %collective-permute-done.33.refs_2_ = bf16[1024,128]{1,0:T(8,128)(2,1)S(1)} collective-permute-done((bf16[1024,128]{1,0:T(8,128)(2,1)S(1)}, bf16[1024,128]{1,0:T(8,128)(2,1)S(1)}, u32[]{:S(2)}, u32[]{:S(2)}) %collective-permute-start.33) | collective-permute-done | bytes 262176 | tf_op jit(solution)/shard_map/ppermute | solution.py:50
  203.3 2.6 %collective-permute-start.36 = (bf16[1216,128]{1,0:T(8,128)(2,1)S(1)}, bf16[1216,128]{1,0:T(8,128)(2,1)S(1)}, u32[]{:S(2)}, u32[]{:S(2)}) collective-permute-start(bf16[1216,128]{1,0:T(8,128)(2,1)S(1)} %get-tuple-element.82), channel_id=1, source_target_pairs={{0,4},{4,0},{8,12},{12,8},{16,20},{20,16},{24,28},{28,24},{32,36},... | collective-permute-start | bytes 933896 | tf_op jit(solution)/shard_map/ppermute | solution.py:54
  207.2 2.4 %finish.1 = (bf16[1024,512]{1,0:T(8,128)(2,1)}, bf16[1024,512]{1,0:T(8,128)(2,1)}) custom-call(s32[1]{0:T(128)} %bitcast.refs_0_.core, bf16[1024,512]{1,0:T(8,128)(2,1)S(1)} %copy-done, bf16[1024,512]{1,0:T(8,128)(2,1)S(1)} %copy-done.1, f32[1024,512]{1,0:T(8,128)S(1)} %get-tuple-element.62.dk, f32[1024,512]{1,0:T(8,128)S(1)} %get-tuple-element.63.dv, ...), custom_call_target="tpu_custom_call" | custom-call | flops 500000000 | bytes 9437184 | tf_op jit(solution)/shard_map/finish/pallas_call | solution.py:481
  (161 shorter events, 51.5 us)
Async XLA Ops:
  7.2 107.4 %all-gather.2.cloned.1.call-start = ((), (), s32[]{:S(2)}) async-start(), calls=%async_computation.2 | async-start | bytes 10485760 | tf_op jit(solution)/shard_map/all_gather | solution.py:574
  7.9 201.7 %reduce-scatter.2.cloned.1.call-start = ((), (), s32[]{:S(2)}) async-start(), calls=%async_computation.1 | async-start | bytes 10485760 | tf_op jit(solution)/shard_map/reduce_scatter | solution.py:613
  13.6 8.1 %collective-permute-start.1 = (bf16[1216,128]{1,0:T(8,128)(2,1)S(1)}, bf16[1216,128]{1,0:T(8,128)(2,1)S(1)}, u32[]{:S(2)}, u32[]{:S(2)}) collective-permute-start(bf16[1216,128]{1,0:T(8,128)(2,1)S(1)} %get-tuple-element.48.refs_2_), channel_id=1, source_target_pairs={{0,8},{4,36},{8,16},{12,44},{16,24},{20,52},{24,0},{28,60},{32,40}... | collective-permute-start | bytes 933896 | tf_op jit(solution)/shard_map/ppermute | solution.py:50
  17.5 14.5 %collective-permute-start.6 = (bf16[1216,128]{1,0:T(8,128)(2,1)S(1)}, bf16[1216,128]{1,0:T(8,128)(2,1)S(1)}, u32[]{:S(2)}, u32[]{:S(2)}) collective-permute-start(bf16[1216,128]{1,0:T(8,128)(2,1)S(1)} %get-tuple-element.48.refs_2_), channel_id=1, source_target_pairs={{0,24},{4,100},{8,0},{12,108},{16,8},{20,116},{24,16},{28,124},{32... | collective-permute-start | bytes 933896 | tf_op jit(solution)/shard_map/ppermute | solution.py:50
  21.8 10.2 %collective-permute-start.3 = (bf16[1216,128]{1,0:T(8,128)(2,1)S(1)}, bf16[1216,128]{1,0:T(8,128)(2,1)S(1)}, u32[]{:S(2)}, u32[]{:S(2)}) collective-permute-start(bf16[1216,128]{1,0:T(8,128)(2,1)S(1)} %collective-permute-done.1.refs_4_), channel_id=1, source_target_pairs={{0,8},{4,36},{8,16},{12,44},{16,24},{20,52},{24,0},{28,60},{32,40}... | collective-permute-start | bytes 933896 | tf_op jit(solution)/shard_map/ppermute | solution.py:50
  21.8 10.2 %collective-permute-start.2 = (bf16[1024,128]{1,0:T(8,128)(2,1)}, bf16[1024,128]{1,0:T(8,128)(2,1)}, u32[]{:S(2)}, u32[]{:S(2)}) collective-permute-start(bf16[1024,128]{1,0:T(8,128)(2,1)} %get-tuple-element.49.refs_3_), channel_id=1, source_target_pairs={{0,8},{4,36},{8,16},{12,44},{16,24},{20,52},{24,0},{28,60},{32,40}... | collective-permute-start | bytes 786440 | tf_op jit(solution)/shard_map/ppermute | solution.py:50
  23.2 8.8 %collective-permute-start.5 = (bf16[1024,128]{1,0:T(8,128)(2,1)}, bf16[1024,128]{1,0:T(8,128)(2,1)}, u32[]{:S(2)}, u32[]{:S(2)}) collective-permute-start(bf16[1024,128]{1,0:T(8,128)(2,1)} %collective-permute-done.4.refs_9_), channel_id=1, source_target_pairs={{0,24},{4,100},{8,0},{12,108},{16,8},{20,116},{24,16},{28,124},{32... | collective-permute-start | bytes 786440 | tf_op jit(solution)/shard_map/ppermute | solution.py:50
  33.3 15.4 %collective-permute-start.10 = (bf16[4096,128]{1,0:T(8,128)(2,1)S(1)}, bf16[4096,128]{1,0:T(8,128)(2,1)}, u32[]{:S(2)}, u32[]{:S(2)}) collective-permute-start(bf16[4096,128]{1,0:T(8,128)(2,1)S(1)} %get-tuple-element.52.rest_0_), channel_id=1, source_target_pairs={{0,32},{4,12},{8,40},{12,20},{16,48},{20,28},{24,56},{28,4},{32,64... | collective-permute-start | bytes 3145736 | tf_op jit(solution)/shard_map/ppermute | solution.py:50
  34.6 18.1 %collective-permute-start.12 = (bf16[4096,128]{1,0:T(8,128)(2,1)S(1)}, bf16[4096,128]{1,0:T(8,128)(2,1)}, u32[]{:S(2)}, u32[]{:S(2)}) collective-permute-start(bf16[4096,128]{1,0:T(8,128)(2,1)S(1)} %get-tuple-element.52.rest_0_), channel_id=1, source_target_pairs={{0,96},{4,28},{8,104},{12,4},{16,112},{20,12},{24,120},{28,20},{32... | collective-permute-start | bytes 3145736 | tf_op jit(solution)/shard_map/ppermute | solution.py:50
  36.3 24.7 %collective-permute-start.8 = (bf16[4480,128]{1,0:T(8,128)(2,1)S(1)}, bf16[4480,128]{1,0:T(8,128)(2,1)S(1)}, u32[]{:S(2)}, u32[]{:S(2)}) collective-permute-start(bf16[4480,128]{1,0:T(8,128)(2,1)S(1)} %get-tuple-element.51.rest_1_), channel_id=1, source_target_pairs={{0,96},{4,28},{8,104},{12,4},{16,112},{20,12},{24,120},{28,20},{32... | collective-permute-start | bytes 3440648 | tf_op jit(solution)/shard_map/ppermute | solution.py:50
  37.7 26.2 %collective-permute-start.13 = (bf16[4096,128]{1,0:T(8,128)(2,1)S(1)}, bf16[4096,128]{1,0:T(8,128)(2,1)S(1)}, u32[]{:S(2)}, u32[]{:S(2)}) collective-permute-start(bf16[4096,128]{1,0:T(8,128)(2,1)S(1)} %get-tuple-element.52.rest_0_), channel_id=1, source_target_pairs={{0,4},{4,0},{8,12},{12,8},{16,20},{20,16},{24,28},{28,24},{32,36},... | collective-permute-start | bytes 3145736 | tf_op jit(solution)/shard_map/ppermute | solution.py:54
  41.7 26.4 %collective-permute-start.7 = (bf16[4480,128]{1,0:T(8,128)(2,1)S(1)}, bf16[4480,128]{1,0:T(8,128)(2,1)}, u32[]{:S(2)}, u32[]{:S(2)}) collective-permute-start(bf16[4480,128]{1,0:T(8,128)(2,1)S(1)} %get-tuple-element.51.rest_1_), channel_id=1, source_target_pairs={{0,32},{4,12},{8,40},{12,20},{16,48},{20,28},{24,56},{28,4},{32,64... | collective-permute-start | bytes 3440648 | tf_op jit(solution)/shard_map/ppermute | solution.py:50
  48.8 19.3 %collective-permute-start.14 = (bf16[4480,128]{1,0:T(8,128)(2,1)S(1)}, bf16[4480,128]{1,0:T(8,128)(2,1)S(1)}, u32[]{:S(2)}, u32[]{:S(2)}) collective-permute-start(bf16[4480,128]{1,0:T(8,128)(2,1)S(1)} %get-tuple-element.51.rest_1_), channel_id=1, source_target_pairs={{0,4},{4,0},{8,12},{12,8},{16,20},{20,16},{24,28},{28,24},{32,36},... | collective-permute-start | bytes 3440648 | tf_op jit(solution)/shard_map/ppermute | solution.py:54
  52.7 19.6 %collective-permute-start.11 = (bf16[4096,128]{1,0:T(8,128)(2,1)}, bf16[4096,128]{1,0:T(8,128)(2,1)}, u32[]{:S(2)}, u32[]{:S(2)}) collective-permute-start(bf16[4096,128]{1,0:T(8,128)(2,1)} %collective-permute-done.10.rest_2_), channel_id=1, source_target_pairs={{0,32},{4,12},{8,40},{12,20},{16,48},{20,28},{24,56},{28,4},{32,64... | collective-permute-start | bytes 3145736 | tf_op jit(solution)/shard_map/ppermute | solution.py:50
  61.0 15.7 %collective-permute-start.9 = (bf16[4480,128]{1,0:T(8,128)(2,1)S(1)}, bf16[4480,128]{1,0:T(8,128)(2,1)}, u32[]{:S(2)}, u32[]{:S(2)}) collective-permute-start(bf16[4480,128]{1,0:T(8,128)(2,1)S(1)} %collective-permute-done.8.left.rest_7_), channel_id=1, source_target_pairs={{0,96},{4,28},{8,104},{12,4},{16,112},{20,12},{24,120},{28,20},{32... | collective-permute-start | bytes 3440648 | tf_op jit(solution)/shard_map/ppermute | solution.py:50
  64.8 10.7 %collective-permute-start.15 = (bf16[4096,128]{1,0:T(8,128)(2,1)}, bf16[4096,128]{1,0:T(8,128)(2,1)}, u32[]{:S(2)}, u32[]{:S(2)}) collective-permute-start(bf16[4096,128]{1,0:T(8,128)(2,1)} %collective-permute-done.10.rest_2_), channel_id=1, source_target_pairs={{0,4},{4,0},{8,12},{12,8},{16,20},{20,16},{24,28},{28,24},{32,36},... | collective-permute-start | bytes 3145736 | tf_op jit(solution)/shard_map/ppermute | solution.py:54
  68.1 12.5 %collective-permute-start.16 = (bf16[4480,128]{1,0:T(8,128)(2,1)}, bf16[4480,128]{1,0:T(8,128)(2,1)}, u32[]{:S(2)}, u32[]{:S(2)}) collective-permute-start(bf16[4480,128]{1,0:T(8,128)(2,1)} %collective-permute-done.7.right.rest_3_), channel_id=1, source_target_pairs={{0,4},{4,0},{8,12},{12,8},{16,20},{20,16},{24,28},{28,24},{32,36},... | collective-permute-start | bytes 3440648 | tf_op jit(solution)/shard_map/ppermute | solution.py:54
  69.1 11.5 %collective-permute-start.18 = (bf16[4480,128]{1,0:T(8,128)(2,1)S(1)}, bf16[4480,128]{1,0:T(8,128)(2,1)}, u32[]{:S(2)}, u32[]{:S(2)}) collective-permute-start(bf16[4480,128]{1,0:T(8,128)(2,1)S(1)} %collective-permute-done.8.left.rest_7_), channel_id=1, source_target_pairs={{0,4},{4,0},{8,12},{12,8},{16,20},{20,16},{24,28},{28,24},{32,36},... | collective-permute-start | bytes 3440648 | tf_op jit(solution)/shard_map/ppermute | solution.py:54
  72.3 8.3 %collective-permute-start.17 = (bf16[4096,128]{1,0:T(8,128)(2,1)}, bf16[4096,128]{1,0:T(8,128)(2,1)}, u32[]{:S(2)}, u32[]{:S(2)}) collective-permute-start(bf16[4096,128]{1,0:T(8,128)(2,1)} %collective-permute-done.12.rest_1_.rest_6_), channel_id=1, source_target_pairs={{0,4},{4,0},{8,12},{12,8},{16,20},{20,16},{24,28},{28,24},{32,36},... | collective-permute-start | bytes 3145736 | tf_op jit(solution)/shard_map/ppermute | solution.py:54
  75.5 12.1 %collective-permute-start.20 = (bf16[4096,128]{1,0:T(8,128)(2,1)}, bf16[4096,128]{1,0:T(8,128)(2,1)}, u32[]{:S(2)}, u32[]{:S(2)}) collective-permute-start(bf16[4096,128]{1,0:T(8,128)(2,1)} %collective-permute-done.11.rest_0_.rest_4_), channel_id=1, source_target_pairs={{0,4},{4,0},{8,12},{12,8},{16,20},{20,16},{24,28},{28,24},{32,36},... | collective-permute-start | bytes 3145736 | tf_op jit(solution)/shard_map/ppermute | solution.py:54
  76.6 11.0 %collective-permute-start.21 = (bf16[4480,128]{1,0:T(8,128)(2,1)}, bf16[4480,128]{1,0:T(8,128)(2,1)}, u32[]{:S(2)}, u32[]{:S(2)}) collective-permute-start(bf16[4480,128]{1,0:T(8,128)(2,1)} %collective-permute-done.9.far.rest_5_), channel_id=1, source_target_pairs={{0,4},{4,0},{8,12},{12,8},{16,20},{20,16},{24,28},{28,24},{32,36},... | collective-permute-start | bytes 3440648 | tf_op jit(solution)/shard_map/ppermute | solution.py:54
  140.6 16.4 %collective-permute-start.24 = (bf16[2,2240,128]{2,1,0:T(8,128)(2,1)S(1)}, bf16[2,2240,128]{2,1,0:T(8,128)(2,1)S(1)}, u32[]{:S(2)}, u32[]{:S(2)}) collective-permute-start(bf16[2,2240,128]{2,1,0:T(8,128)(2,1)S(1)} %get-tuple-element.66.refs_4_), channel_id=1, source_target_pairs={{0,32},{4,12},{8,40},{12,20},{16,48},{20,28},{24,56},{28,4},{32,64... | collective-permute-start | bytes 3440648 | tf_op jit(solution)/shard_map/ppermute | solution.py:50
  140.7 16.3 %collective-permute-start.25 = (bf16[2,2240,128]{2,1,0:T(8,128)(2,1)S(1)}, bf16[2,2240,128]{2,1,0:T(8,128)(2,1)S(1)}, u32[]{:S(2)}, u32[]{:S(2)}) collective-permute-start(bf16[2,2240,128]{2,1,0:T(8,128)(2,1)S(1)} %get-tuple-element.67), channel_id=1, source_target_pairs={{0,96},{4,28},{8,104},{12,4},{16,112},{20,12},{24,120},{28,20},{32... | collective-permute-start | bytes 3440648 | tf_op jit(solution)/shard_map/ppermute | solution.py:50
  144.7 24.6 %collective-permute-start.27 = (bf16[2,2240,128]{2,1,0:T(8,128)(2,1)S(1)}, bf16[2,2240,128]{2,1,0:T(8,128)(2,1)S(1)}, u32[]{:S(2)}, u32[]{:S(2)}) collective-permute-start(bf16[2,2240,128]{2,1,0:T(8,128)(2,1)S(1)} %get-tuple-element.69), channel_id=1, source_target_pairs={{0,32},{4,12},{8,40},{12,20},{16,48},{20,28},{24,56},{28,4},{32,64... | collective-permute-start | bytes 3440648 | tf_op jit(solution)/shard_map/ppermute | solution.py:50
  144.8 24.5 %collective-permute-start.28 = (bf16[2,2240,128]{2,1,0:T(8,128)(2,1)S(1)}, bf16[2,2240,128]{2,1,0:T(8,128)(2,1)S(1)}, u32[]{:S(2)}, u32[]{:S(2)}) collective-permute-start(bf16[2,2240,128]{2,1,0:T(8,128)(2,1)S(1)} %get-tuple-element.70), channel_id=1, source_target_pairs={{0,96},{4,28},{8,104},{12,4},{16,112},{20,12},{24,120},{28,20},{32... | collective-permute-start | bytes 3440648 | tf_op jit(solution)/shard_map/ppermute | solution.py:50
  158.7 22.9 %collective-permute-start.26 = (bf16[2,2240,128]{2,1,0:T(8,128)(2,1)S(1)}, bf16[2,2240,128]{2,1,0:T(8,128)(2,1)S(1)}, u32[]{:S(2)}, u32[]{:S(2)}) collective-permute-start(bf16[2,2240,128]{2,1,0:T(8,128)(2,1)S(1)} %get-tuple-element.68), channel_id=1, source_target_pairs={{0,32},{4,12},{8,40},{12,20},{16,48},{20,28},{24,56},{28,4},{32,64... | collective-permute-start | bytes 3440648 | tf_op jit(solution)/shard_map/ppermute | solution.py:50
  158.7 22.8 %collective-permute-start.29 = (bf16[2,2240,128]{2,1,0:T(8,128)(2,1)S(1)}, bf16[2,2240,128]{2,1,0:T(8,128)(2,1)S(1)}, u32[]{:S(2)}, u32[]{:S(2)}) collective-permute-start(bf16[2,2240,128]{2,1,0:T(8,128)(2,1)S(1)} %get-tuple-element.71), channel_id=1, source_target_pairs={{0,96},{4,28},{8,104},{12,4},{16,112},{20,12},{24,120},{28,20},{32... | collective-permute-start | bytes 3440648 | tf_op jit(solution)/shard_map/ppermute | solution.py:50
  184.9 7.9 %collective-permute-start.30 = (bf16[1216,128]{1,0:T(8,128)(2,1)S(1)}, bf16[1216,128]{1,0:T(8,128)(2,1)S(1)}, u32[]{:S(2)}, u32[]{:S(2)}) collective-permute-start(bf16[1216,128]{1,0:T(8,128)(2,1)S(1)} %get-tuple-element.75), channel_id=1, source_target_pairs={{0,8},{4,36},{8,16},{12,44},{16,24},{20,52},{24,0},{28,60},{32,40}... | collective-permute-start | bytes 933896 | tf_op jit(solution)/shard_map/ppermute | solution.py:50
  188.3 14.8 %collective-permute-start.34 = (bf16[1216,128]{1,0:T(8,128)(2,1)S(1)}, bf16[1216,128]{1,0:T(8,128)(2,1)S(1)}, u32[]{:S(2)}, u32[]{:S(2)}) collective-permute-start(bf16[1216,128]{1,0:T(8,128)(2,1)S(1)} %get-tuple-element.79), channel_id=1, source_target_pairs={{0,24},{4,100},{8,0},{12,108},{16,8},{20,116},{24,16},{28,124},{32... | collective-permute-start | bytes 933896 | tf_op jit(solution)/shard_map/ppermute | solution.py:50
  193.0 10.1 %collective-permute-start.32 = (bf16[1216,128]{1,0:T(8,128)(2,1)S(1)}, bf16[1216,128]{1,0:T(8,128)(2,1)S(1)}, u32[]{:S(2)}, u32[]{:S(2)}) collective-permute-start(bf16[1216,128]{1,0:T(8,128)(2,1)S(1)} %get-tuple-element.77), channel_id=1, source_target_pairs={{0,8},{4,36},{8,16},{12,44},{16,24},{20,52},{24,0},{28,60},{32,40}... | collective-permute-start | bytes 933896 | tf_op jit(solution)/shard_map/ppermute | solution.py:50
  193.5 9.6 %collective-permute-start.33 = (bf16[1024,128]{1,0:T(8,128)(2,1)S(1)}, bf16[1024,128]{1,0:T(8,128)(2,1)S(1)}, u32[]{:S(2)}, u32[]{:S(2)}) collective-permute-start(bf16[1024,128]{1,0:T(8,128)(2,1)S(1)} %get-tuple-element.78), channel_id=1, source_target_pairs={{0,8},{4,36},{8,16},{12,44},{16,24},{20,52},{24,0},{28,60},{32,40}... | collective-permute-start | bytes 786440 | tf_op jit(solution)/shard_map/ppermute | solution.py:50
  194.9 8.2 %collective-permute-start.35 = (bf16[1024,128]{1,0:T(8,128)(2,1)S(1)}, bf16[1024,128]{1,0:T(8,128)(2,1)S(1)}, u32[]{:S(2)}, u32[]{:S(2)}) collective-permute-start(bf16[1024,128]{1,0:T(8,128)(2,1)S(1)} %get-tuple-element.80), channel_id=1, source_target_pairs={{0,24},{4,100},{8,0},{12,108},{16,8},{20,116},{24,16},{28,124},{32... | collective-permute-start | bytes 786440 | tf_op jit(solution)/shard_map/ppermute | solution.py:50
  (40 other events, 234.9 us)
Sparse Core Ops, SparseCore 0:
  9.7 86.3 all-gather.1
  114.1 79.6 reduce-scatter.1

commit v4 on v3

--- a/solution.py
+++ b/solution.py
@@ -176,7 +176,7 @@
 
 def sparse_forward_kernel(table, q_ref, k_ref, v_ref, *rest):
     pieces = rest[:PIECES]
-    out_ref, p_ref, kf_ref, vf_ref, inv_ref, s_ref, sems = rest[PIECES:]
+    out_ref, kf_ref, vf_ref, log_ref, s_ref, sems = rest[PIECES:]
     step = pl.program_id(0)
 
     @pl.when(step == 0)
@@ -208,7 +208,6 @@
         e = jnp.exp(s_ref[r] - peak)
         total = total + jnp.sum(e, axis=0, keepdims=True)
         p = e.astype(BF)
-        p_ref[0, r] = p
         if r == 0:
             value = v_ref[...]
         else:
@@ -216,9 +215,8 @@
             pltpu.make_async_copy(pieces[0].at[pl.ds(0, BLOCK)], vf_ref.at[row], sems.at[1, row]).wait()
             value = vf_ref[row]
         out = out + dot(value, p, 0, 0)
-    inverse = 1.0 / total
-    inv_ref[...] = jnp.broadcast_to(inverse, (8, BLOCK))
-    out_ref[...] = (out * inverse).T.astype(BF)
+    log_ref[...] = jnp.broadcast_to(peak + jnp.log(total), (8, BLOCK))
+    out_ref[...] = (out / total).T.astype(BF)
 
 
 def sparse_forward(table, queries, keys, values, pieces):
@@ -232,7 +230,6 @@
             in_specs=[column] * 3 + [ANY] * PIECES,
             out_specs=[
                 column,
-                pl.BlockSpec((1, LISTED + 1, BLOCK, BLOCK), lambda i, t: (i, 0, 0, 0)),
                 pl.BlockSpec(far, lambda i, t: (0, 0, 0)),
                 pl.BlockSpec(far, lambda i, t: (0, 0, 0)),
                 pl.BlockSpec((8, BLOCK), lambda i, t: (0, i)),
@@ -244,7 +241,6 @@
         ),
         out_shape=[
             jax.ShapeDtypeStruct(queries.shape, BF),
-            jax.ShapeDtypeStruct((2, LISTED + 1, BLOCK, BLOCK), BF),
             jax.ShapeDtypeStruct(far, BF),
             jax.ShapeDtypeStruct(far, BF),
             jax.ShapeDtypeStruct((8, queries.shape[0]), F32),
@@ -256,24 +252,26 @@
 
 
 def sparse_backward_kernel(
-    core, q_ref, k_ref, v_ref, g_ref, o_ref, p_ref, kf_ref, vf_ref, inv_ref, dq_ref, dk_ref, dv_ref, mine_ref, sent_ref
+    core, table, q_ref, k_ref, v_ref, g_ref, o_ref, kf_ref, vf_ref, log_ref, dq_ref, dk_ref, dv_ref, mine_ref, sent_ref
 ):
     first = core[0] == 0
     q, g = q_ref[...], g_ref[...]
-    inverse = inv_ref[0:1, :]
-    turned = g.astype(F32).T * inverse
-    row_dot = jnp.sum(turned * o_ref[...].astype(F32).T, axis=0, keepdims=True)
-    g = turned.T.astype(BF)
+    row_dot = jnp.sum((g.astype(F32) * o_ref[...].astype(F32)).T, axis=0, keepdims=True)
+    logs = log_ref[0:1, :]
     dq = jnp.zeros((HD, BLOCK), F32)
     for r in range(LISTED + 1):
-        p = p_ref[0, r]
         key = k_ref[...] if r == 0 else kf_ref[r - 1]
         value = v_ref[...] if r == 0 else vf_ref[r - 1]
-        dp = dot(value, g, 1, 1)
-        ds = (p.astype(F32) * (dp - row_dot)).astype(BF)
+        s = dot(key, q, 1, 1) * SCALING
+        if r == 0:
+            p = jnp.exp(jnp.where(causal_mask(), s - logs, -1e30))
+        else:
+            used = table[pl.program_id(0) * LISTED + r - 1, 4] == 1
+            p = jnp.exp(s - jnp.where(used, logs, 1e30))
+        ds = (p * (dot(value, g, 1, 1) - row_dot)).astype(BF)
         dq = dq + dot(key, ds, 0, 0)
         dk = dot(ds, q, 1, 0) * SCALING
-        dv = dot(p, g, 1, 0)
+        dv = dot(p.astype(BF), g, 1, 0)
         if r == 0:
             dk_ref[...] = dk
             dv_ref[...] = dv
@@ -283,18 +281,17 @@
     dq_ref[...] = (dq * SCALING).T.astype(BF)
 
 
-def sparse_backward(core, queries, keys, values, grads, outs, probs, far_k, far_v, inverse):
-    column = pl.BlockSpec(TILE, lambda i, c: (i, LIN))
-    four = pl.BlockSpec((LISTED, BLOCK, HD), lambda i, c: (i, 0, 0))
-    five = pl.BlockSpec((1, LISTED + 1, BLOCK, BLOCK), lambda i, c: (i, 0, 0, 0))
+def sparse_backward(core, table, queries, keys, values, grads, outs, far_k, far_v, logs):
+    column = pl.BlockSpec(TILE, lambda i, c, t: (i, LIN))
+    four = pl.BlockSpec((LISTED, BLOCK, HD), lambda i, c, t: (i, 0, 0))
     return pl.pallas_call(
         sparse_backward_kernel,
         grid_spec=pltpu.PrefetchScalarGridSpec(
-            num_scalar_prefetch=1,
+            num_scalar_prefetch=2,
             grid=(2,),
             in_specs=[column] * 3
-            + [pl.BlockSpec(TILE, lambda i, c: (i, 0)), column, five, four, four]
-            + [pl.BlockSpec((8, BLOCK), lambda i, c: (0, i))],
+            + [pl.BlockSpec(TILE, lambda i, c, t: (i, 0)), column, four, four]
+            + [pl.BlockSpec((8, BLOCK), lambda i, c, t: (0, i))],
             out_specs=[column, column, column, four, four],
         ),
         out_shape=[
@@ -305,9 +302,9 @@
             jax.ShapeDtypeStruct((2 * LISTED, BLOCK, HD), BF),
         ],
         compiler_params=params(20),
-        cost_estimate=cost(8e9, 12 * MIB),
+        cost_estimate=cost(8e9, 8 * MIB),
         name="sparse_backward",
-    )(core, queries, keys, values, grads, outs, probs, far_k, far_v, inverse)
+    )(core, table, queries, keys, values, grads, outs, far_k, far_v, logs)
 
 
 def begin_kernel(core, k_ref, v_ref, states, mine, sent):
@@ -607,14 +604,14 @@
     chip = chip.reshape(LIN, HD, HD)
     before = jnp.stack([chip, chip + states[0]])
 
-    sparse_out, probs, far_k, far_v, inverse = sparse_forward(fetch, queries, keys, values, pieces)
+    sparse_out, far_k, far_v, logs = sparse_forward(fetch, queries, keys, values, pieces)
     attention = linear_forward(queries, keys, values, scale, before, sparse_out)
     partial_out = dot(attention, out_weight, 1, 1).astype(BF)
     layer_out = lax.psum_scatter(partial_out, "head", scatter_dimension=1, tiled=True)
     sparse_grad = dot(grad_all, out_weight[:, LIN * HD :], 1, 0).astype(BF)
     linear_grad = dot(grad_all, out_weight[:, : LIN * HD], 1, 0).astype(BF)
     query_grad, own_dk, own_dv, pair_mine, pair_sent = sparse_backward(
-        core, queries, keys, values, sparse_grad, attention, probs, far_k, far_v, inverse
+        core, fetch, queries, keys, values, sparse_grad, attention, far_k, far_v, logs
     )
 
     adjoints = block_adjoints(queries, linear_grad, scale)

time: 217 us -> 213 us (0.982)
  local copies, waits for them, and re-layouts: 18.3 us -> 12.8 us
    unnamed x66 -> x62, local copies, waits for them, and re-layouts: 17.8 us -> 12.2 us
  transfers between devices with their start and end apart: 39 -> 39, of which waited for: 16 -> 16; matrix products, arithmetic and copies ran while one was open for 9% -> 9% of each run, Pallas kernels for 21% -> 22%
where the time goes in v4:
time: 213 us; the launch traced here: 212 us
  waiting for transfers between devices  67.2 us (32%)
  starting transfers between devices  53.1 us (25%)
  Pallas kernels  45.8 us (22%)
  matrix products  17.4 us (8%)
  between operations  14.6 us (7%)
  local copies, waits for them, and re-layouts  12.8 us (6%)
    ppermute x24, waiting for transfers between devices, ring_move(): return lax.ppermute(value, 'ctx', pairs)  61.8 us
    ppermute x24, starting transfers between devices, ring_move(): return lax.ppermute(value, 'ctx', pairs)  31.7 us
    ppermute x13, starting transfers between devices, swap(): return lax.ppermute(value, 'ctx', [(i, i ^ 1) for i in range(CTX)])  21.2 us
    dot_general x3, matrix products, dot(): lax.dot_general(a, b, (((ca,), (cb,)), ((), ())), preferred_element_type=...  17.4 us
    unnamed x62, local copies, waits for them, and re-layouts  12.2 us
    pallas_call x1, Pallas kernels, sparse_forward(): pl.pallas_call(sparse_forward_kernel, grid_spec=pltpu.PrefetchScalarGridS...  9.82 us
    pallas_call x9, Pallas kernels, whole_call(): pl.pallas_call(functools.partial(drop, kernel, n_in, len(deps)), in_specs...  9.52 us
    pallas_call x1, Pallas kernels, sparse_backward(): pl.pallas_call(sparse_backward_kernel, grid_spec=pltpu.PrefetchScalarGrid...  9.18 us
  transfers between devices with their start and end apart: 39, of which 16 were waited for; matrix products, arithmetic and copies ran while one was open for 9% of the time, Pallas kernels for 22%

profile of v4, /device:TPU:1, one launch (start us, length us, event | category | flops | bytes accessed | tf_op | source)
XLA Modules:
  0.0 212.3 jit_solution(8585345753133251271)
XLA Ops:
  15.4 2.1 collective-permute-start.4
  18.9 2.8 %collective-permute-done.1.refs_4_ = bf16[1216,128]{1,0:T(8,128)(2,1)S(1)} collective-permute-done((bf16[1216,128]{1,0:T(8,128)(2,1)S(1)}, bf16[1216,128]{1,0:T(8,128)(2,1)S(1)}, u32[]{:S(2)}, u32[]{:S(2)}) %collective-permute-start.1) | collective-permute-done | bytes 311328 | tf_op jit(solution)/shard_map/ppermute | solution.py:50
  24.5 7.4 %collective-permute-done.2.refs_5_ = bf16[1024,128]{1,0:T(8,128)(2,1)} collective-permute-done((bf16[1024,128]{1,0:T(8,128)(2,1)}, bf16[1024,128]{1,0:T(8,128)(2,1)}, u32[]{:S(2)}, u32[]{:S(2)}) %collective-permute-start.2) | collective-permute-done | bytes 262176 | tf_op jit(solution)/shard_map/ppermute | solution.py:50
  37.7 3.1 %collective-permute-start.13 = (bf16[4096,128]{1,0:T(8,128)(2,1)S(1)}, bf16[4096,128]{1,0:T(8,128)(2,1)S(1)}, u32[]{:S(2)}, u32[]{:S(2)}) collective-permute-start(bf16[4096,128]{1,0:T(8,128)(2,1)S(1)} %get-tuple-element.51.rest_0_), channel_id=1, source_target_pairs={{0,4},{4,0},{8,12},{12,8},{16,20},{20,16},{24,28},{28,24},{32,36},... | collective-permute-start | bytes 3145736 | tf_op jit(solution)/shard_map/ppermute | solution.py:54
  41.8 7.0 %collective-permute-done.10.rest_2_ = bf16[4096,128]{1,0:T(8,128)(2,1)} collective-permute-done((bf16[4096,128]{1,0:T(8,128)(2,1)S(1)}, bf16[4096,128]{1,0:T(8,128)(2,1)}, u32[]{:S(2)}, u32[]{:S(2)}) %collective-permute-start.10) | collective-permute-done | bytes 1048608 | tf_op jit(solution)/shard_map/ppermute | solution.py:50
  48.8 2.9 %collective-permute-start.14 = (bf16[4480,128]{1,0:T(8,128)(2,1)S(1)}, bf16[4480,128]{1,0:T(8,128)(2,1)S(1)}, u32[]{:S(2)}, u32[]{:S(2)}) collective-permute-start(bf16[4480,128]{1,0:T(8,128)(2,1)S(1)} %get-tuple-element.50.rest_1_), channel_id=1, source_target_pairs={{0,4},{4,0},{8,12},{12,8},{16,20},{20,16},{24,28},{28,24},{32,36},... | collective-permute-start | bytes 3440648 | tf_op jit(solution)/shard_map/ppermute | solution.py:54
  52.7 8.3 %collective-permute-done.8.left.rest_7_ = bf16[4480,128]{1,0:T(8,128)(2,1)S(1)} collective-permute-done((bf16[4480,128]{1,0:T(8,128)(2,1)S(1)}, bf16[4480,128]{1,0:T(8,128)(2,1)S(1)}, u32[]{:S(2)}, u32[]{:S(2)}) %collective-permute-start.8) | collective-permute-done | bytes 1146912 | tf_op jit(solution)/shard_map/ppermute | solution.py:50
  61.0 2.9 %collective-permute-start.9 = (bf16[4480,128]{1,0:T(8,128)(2,1)S(1)}, bf16[4480,128]{1,0:T(8,128)(2,1)}, u32[]{:S(2)}, u32[]{:S(2)}) collective-permute-start(bf16[4480,128]{1,0:T(8,128)(2,1)S(1)} %collective-permute-done.8.left.rest_7_), channel_id=1, source_target_pairs={{0,96},{4,28},{8,104},{12,4},{16,112},{20,12},{24,120},{28,20},{32... | collective-permute-start | bytes 3440648 | tf_op jit(solution)/shard_map/ppermute | solution.py:50
  64.8 3.3 %collective-permute-start.15 = (bf16[4096,128]{1,0:T(8,128)(2,1)}, bf16[4096,128]{1,0:T(8,128)(2,1)}, u32[]{:S(2)}, u32[]{:S(2)}) collective-permute-start(bf16[4096,128]{1,0:T(8,128)(2,1)} %collective-permute-done.10.rest_2_), channel_id=1, source_target_pairs={{0,4},{4,0},{8,12},{12,8},{16,20},{20,16},{24,28},{28,24},{32,36},... | collective-permute-start | bytes 3145736 | tf_op jit(solution)/shard_map/ppermute | solution.py:54
  69.6 2.7 %collective-permute-done.11.rest_0_.rest_4_ = bf16[4096,128]{1,0:T(8,128)(2,1)} collective-permute-done((bf16[4096,128]{1,0:T(8,128)(2,1)}, bf16[4096,128]{1,0:T(8,128)(2,1)}, u32[]{:S(2)}, u32[]{:S(2)}) %collective-permute-start.11) | collective-permute-done | bytes 1048608 | tf_op jit(solution)/shard_map/ppermute | solution.py:50
  72.3 2.9 %collective-permute-start.17 = (bf16[4096,128]{1,0:T(8,128)(2,1)}, bf16[4096,128]{1,0:T(8,128)(2,1)}, u32[]{:S(2)}, u32[]{:S(2)}) collective-permute-start(bf16[4096,128]{1,0:T(8,128)(2,1)} %collective-permute-done.12.rest_1_.rest_6_), channel_id=1, source_target_pairs={{0,4},{4,0},{8,12},{12,8},{16,20},{20,16},{24,28},{28,24},{32,36},... | collective-permute-start | bytes 3145736 | tf_op jit(solution)/shard_map/ppermute | solution.py:54
  76.6 3.9 %collective-permute-start.21 = (bf16[4480,128]{1,0:T(8,128)(2,1)}, bf16[4480,128]{1,0:T(8,128)(2,1)}, u32[]{:S(2)}, u32[]{:S(2)}) collective-permute-start(bf16[4480,128]{1,0:T(8,128)(2,1)} %collective-permute-done.9.far.rest_5_), channel_id=1, source_target_pairs={{0,4},{4,0},{8,12},{12,8},{16,20},{20,16},{24,28},{28,24},{32,36},... | collective-permute-start | bytes 3440648 | tf_op jit(solution)/shard_map/ppermute | solution.py:54
  83.2 1.9 prefix.1
  87.7 9.8 %sparse_forward.1 = (bf16[1024,512]{1,0:T(8,128)(2,1)S(1)}, bf16[8,512,128]{2,1,0:T(8,128)(2,1)S(1)}, bf16[8,512,128]{2,1,0:T(8,128)(2,1)S(1)}, f32[8,1024]{1,0:T(8,128)S(1)}) custom-call(s32[8,5]{1,0:T(8,128)S(1)} %stack.14.table, bf16[1024,512]{1,0:T(8,128)(2,1)S(1)} %copy-done.8, bf16[1024,512]{1,0:T(8,128)(2,1)S(1)} %copy-done, ...), custom_call_target="tpu_custom_call" | custom-call | flops 4000000000 | bytes 12582912 | tf_op jit(solution)/shard_map/sparse_forward/pallas_call | solution.py:225
  99.4 3.8 %linear_forward.1.o_ref = bf16[1024,512]{1,0:T(8,128)(2,1)S(1)} custom-call(bf16[1024,512]{1,0:T(8,128)(2,1)S(1)} %copy-done.8, bf16[1024,512]{1,0:T(8,128)(2,1)S(1)} %copy-done, bf16[1024,512]{1,0:T(8,128)(2,1)S(1)} %copy-done.1, f32[8,1024]{1,0:T(8,128)S(1)} %broadcast_in_dim.32.c_ref, ...), custom_call_target="tpu_custom_call", output_to_operand_aliasing={{}: (5, {})} | custom-call | flops 2400000000 | bytes 4194304 | tf_op jit(solution)/shard_map/linear_forward/pallas_call | solution.py:132
  103.2 6.9 %convolution_convert_fusion = bf16[1024,4096]{1,0:T(8,128)(2,1)} fusion(bf16[1024,512]{1,0:T(8,128)(2,1)S(1)} %linear_forward.1.o_ref, bf16[4096,512]{1,0:T(8,128)(2,1)S(1)} %copy-done.27), kind=kOutput, calls=%fused_computation | convolution fusion | flops 4299161600 | bytes 13631488 | tf_op jit(solution)/shard_map/dot_general | solution.py:31
  111.7 6.1 %convolution_convert_fusion.1.g_ref = bf16[1024,128]{1,0:T(8,128)(2,1)S(1)} fusion(bf16[1024,4096]{1,0:T(8,128)(2,1)} %all-gather.2.cloned.1.call-done, bf16[4096,512]{1,0:T(8,128)(2,1)} %param.9), kind=kOutput, calls=%fused_computation.4 | convolution fusion | flops 1073872896 | bytes 9699328 | tf_op jit(solution)/shard_map/dot_general | solution.py:31
  117.8 9.2 %sparse_backward.1 = (bf16[1024,512]{1,0:T(8,128)(2,1)}, f32[1024,512]{1,0:T(8,128)S(1)}, f32[1024,512]{1,0:T(8,128)S(1)}, bf16[8,512,128]{2,1,0:T(8,128)(2,1)S(1)}, bf16[8,512,128]{2,1,0:T(8,128)(2,1)S(1)}) custom-call(s32[1]{0:T(128)} %bitcast.refs_0_.core, s32[8,5]{1,0:T(8,128)S(1)} %stack.14.table, bf16[1024,512]{1,0:T(8,128)(2,1)S(1)} %copy-done.9, ...), custom_call_target="tpu_custom_call" | custom-call | flops 8000000000 | bytes 8388608 | tf_op jit(solution)/shard_map/sparse_backward/pallas_call | solution.py:287
  127.0 4.5 %fusion.2.g_ref = bf16[1024,384]{1,0:T(8,128)(2,1)S(1)} fusion(bf16[1024,4096]{1,0:T(8,128)(2,1)S(1)} %bitcast.16, bf16[4096,512]{1,0:T(8,128)(2,1)S(1)} %copy-done.28), kind=kOutput, calls=%fused_computation.3 | convolution fusion | flops 3221618688 | bytes 12320768 | tf_op jit(solution)/shard_map/dot_general | solution.py:31
  131.5 1.8 block_adjoints.1.adj
  136.4 2.7 %collective-permute-start.25 = (bf16[2,2240,128]{2,1,0:T(8,128)(2,1)S(1)}, bf16[2,2240,128]{2,1,0:T(8,128)(2,1)S(1)}, u32[]{:S(2)}, u32[]{:S(2)}) collective-permute-start(bf16[2,2240,128]{2,1,0:T(8,128)(2,1)S(1)} %get-tuple-element.65), channel_id=1, source_target_pairs={{0,96},{4,28},{8,104},{12,4},{16,112},{20,12},{24,120},{28,20},{32... | collective-permute-start | bytes 3440648 | tf_op jit(solution)/shard_map/ppermute | solution.py:50
  140.5 2.7 %collective-permute-start.28 = (bf16[2,2240,128]{2,1,0:T(8,128)(2,1)S(1)}, bf16[2,2240,128]{2,1,0:T(8,128)(2,1)S(1)}, u32[]{:S(2)}, u32[]{:S(2)}) collective-permute-start(bf16[2,2240,128]{2,1,0:T(8,128)(2,1)S(1)} %get-tuple-element.68), channel_id=1, source_target_pairs={{0,96},{4,28},{8,104},{12,4},{16,112},{20,12},{24,120},{28,20},{32... | collective-permute-start | bytes 3440648 | tf_op jit(solution)/shard_map/ppermute | solution.py:50
  143.2 9.5 %collective-permute-done.24.refs_4_ = bf16[2,2240,128]{2,1,0:T(8,128)(2,1)S(1)} collective-permute-done((bf16[2,2240,128]{2,1,0:T(8,128)(2,1)S(1)}, bf16[2,2240,128]{2,1,0:T(8,128)(2,1)S(1)}, u32[]{:S(2)}, u32[]{:S(2)}) %collective-permute-start.24) | collective-permute-done | bytes 1146912 | tf_op jit(solution)/shard_map/ppermute | solution.py:50
  154.4 2.7 %collective-permute-start.29 = (bf16[2,2240,128]{2,1,0:T(8,128)(2,1)S(1)}, bf16[2,2240,128]{2,1,0:T(8,128)(2,1)S(1)}, u32[]{:S(2)}, u32[]{:S(2)}) collective-permute-start(bf16[2,2240,128]{2,1,0:T(8,128)(2,1)S(1)} %get-tuple-element.69), channel_id=1, source_target_pairs={{0,96},{4,28},{8,104},{12,4},{16,112},{20,12},{24,120},{28,20},{32... | collective-permute-start | bytes 3440648 | tf_op jit(solution)/shard_map/ppermute | solution.py:50
  157.2 7.4 %linear_backward.1 = (bf16[1024,512]{1,0:T(8,128)(2,1)}, f32[1024,512]{1,0:T(8,128)S(1)}, f32[1024,512]{1,0:T(8,128)S(1)}) custom-call(bf16[1024,512]{1,0:T(8,128)(2,1)S(1)} %copy-done.9, bf16[1024,512]{1,0:T(8,128)(2,1)S(1)} %copy-done, bf16[1024,512]{1,0:T(8,128)(2,1)S(1)} %copy-done.1, ...), custom_call_target="tpu_custom_call", output_to_operand_aliasing={{0}: (6, {}), {1}: (7, {}), {2}: (8, {})} | custom-call | flops 5000000000 | bytes 9437184 | tf_op jit(solution)/shard_map/linear_backward/pallas_call | solution.py:161
  165.0 12.3 %collective-permute-done.26.refs_4_ = bf16[2,2240,128]{2,1,0:T(8,128)(2,1)S(1)} collective-permute-done((bf16[2,2240,128]{2,1,0:T(8,128)(2,1)S(1)}, bf16[2,2240,128]{2,1,0:T(8,128)(2,1)S(1)}, u32[]{:S(2)}, u32[]{:S(2)}) %collective-permute-start.26) | collective-permute-done | bytes 1146912 | tf_op jit(solution)/shard_map/ppermute | solution.py:50
  178.5 2.1 back_turn.1
  181.5 2.9 %collective-permute-start.31 = (bf16[1024,128]{1,0:T(8,128)(2,1)S(1)}, bf16[1024,128]{1,0:T(8,128)(2,1)S(1)}, u32[]{:S(2)}, u32[]{:S(2)}) collective-permute-start(bf16[1024,128]{1,0:T(8,128)(2,1)S(1)} %get-tuple-element.74), channel_id=1, source_target_pairs={{0,24},{4,100},{8,0},{12,108},{16,8},{20,116},{24,16},{28,124},{32... | collective-permute-start | bytes 786440 | tf_op jit(solution)/shard_map/ppermute | solution.py:50
  185.8 1.9 collective-permute-done.31.refs_3_
  192.2 7.0 %collective-permute-done.33.refs_2_ = bf16[1024,128]{1,0:T(8,128)(2,1)S(1)} collective-permute-done((bf16[1024,128]{1,0:T(8,128)(2,1)S(1)}, bf16[1024,128]{1,0:T(8,128)(2,1)S(1)}, u32[]{:S(2)}, u32[]{:S(2)}) %collective-permute-start.33) | collective-permute-done | bytes 262176 | tf_op jit(solution)/shard_map/ppermute | solution.py:50
  199.5 2.3 %collective-permute-start.36 = (bf16[1216,128]{1,0:T(8,128)(2,1)S(1)}, bf16[1216,128]{1,0:T(8,128)(2,1)S(1)}, u32[]{:S(2)}, u32[]{:S(2)}) collective-permute-start(bf16[1216,128]{1,0:T(8,128)(2,1)S(1)} %get-tuple-element.80), channel_id=1, source_target_pairs={{0,4},{4,0},{8,12},{12,8},{16,20},{20,16},{24,28},{28,24},{32,36},... | collective-permute-start | bytes 933896 | tf_op jit(solution)/shard_map/ppermute | solution.py:54
  203.1 2.4 %finish.1 = (bf16[1024,512]{1,0:T(8,128)(2,1)}, bf16[1024,512]{1,0:T(8,128)(2,1)}) custom-call(s32[1]{0:T(128)} %bitcast.refs_0_.core, bf16[1024,512]{1,0:T(8,128)(2,1)S(1)} %copy-done, bf16[1024,512]{1,0:T(8,128)(2,1)S(1)} %copy-done.1, f32[1024,512]{1,0:T(8,128)S(1)} %get-tuple-element.60.dk, f32[1024,512]{1,0:T(8,128)S(1)} %get-tuple-element.61.dv, ...), custom_call_target="tpu_custom_call" | custom-call | flops 500000000 | bytes 9437184 | tf_op jit(solution)/shard_map/finish/pallas_call | solution.py:478
  (157 shorter events, 48.6 us)
Async XLA Ops:
  7.2 104.4 %all-gather.2.cloned.1.call-start = ((), (), s32[]{:S(2)}) async-start(), calls=%async_computation.2 | async-start | bytes 10485760 | tf_op jit(solution)/shard_map/all_gather | solution.py:571
  7.9 197.5 %reduce-scatter.2.cloned.1.call-start = ((), (), s32[]{:S(2)}) async-start(), calls=%async_computation.1 | async-start | bytes 10485760 | tf_op jit(solution)/shard_map/reduce_scatter | solution.py:610
  13.6 8.1 %collective-permute-start.1 = (bf16[1216,128]{1,0:T(8,128)(2,1)S(1)}, bf16[1216,128]{1,0:T(8,128)(2,1)S(1)}, u32[]{:S(2)}, u32[]{:S(2)}) collective-permute-start(bf16[1216,128]{1,0:T(8,128)(2,1)S(1)} %get-tuple-element.47.refs_2_), channel_id=1, source_target_pairs={{0,8},{4,36},{8,16},{12,44},{16,24},{20,52},{24,0},{28,60},{32,40}... | collective-permute-start | bytes 933896 | tf_op jit(solution)/shard_map/ppermute | solution.py:50
  17.5 14.5 %collective-permute-start.6 = (bf16[1216,128]{1,0:T(8,128)(2,1)S(1)}, bf16[1216,128]{1,0:T(8,128)(2,1)S(1)}, u32[]{:S(2)}, u32[]{:S(2)}) collective-permute-start(bf16[1216,128]{1,0:T(8,128)(2,1)S(1)} %get-tuple-element.47.refs_2_), channel_id=1, source_target_pairs={{0,24},{4,100},{8,0},{12,108},{16,8},{20,116},{24,16},{28,124},{32... | collective-permute-start | bytes 933896 | tf_op jit(solution)/shard_map/ppermute | solution.py:50
  21.8 10.2 %collective-permute-start.3 = (bf16[1216,128]{1,0:T(8,128)(2,1)S(1)}, bf16[1216,128]{1,0:T(8,128)(2,1)S(1)}, u32[]{:S(2)}, u32[]{:S(2)}) collective-permute-start(bf16[1216,128]{1,0:T(8,128)(2,1)S(1)} %collective-permute-done.1.refs_4_), channel_id=1, source_target_pairs={{0,8},{4,36},{8,16},{12,44},{16,24},{20,52},{24,0},{28,60},{32,40}... | collective-permute-start | bytes 933896 | tf_op jit(solution)/shard_map/ppermute | solution.py:50
  21.8 10.2 %collective-permute-start.2 = (bf16[1024,128]{1,0:T(8,128)(2,1)}, bf16[1024,128]{1,0:T(8,128)(2,1)}, u32[]{:S(2)}, u32[]{:S(2)}) collective-permute-start(bf16[1024,128]{1,0:T(8,128)(2,1)} %get-tuple-element.48.refs_3_), channel_id=1, source_target_pairs={{0,8},{4,36},{8,16},{12,44},{16,24},{20,52},{24,0},{28,60},{32,40}... | collective-permute-start | bytes 786440 | tf_op jit(solution)/shard_map/ppermute | solution.py:50
  23.2 8.8 %collective-permute-start.5 = (bf16[1024,128]{1,0:T(8,128)(2,1)}, bf16[1024,128]{1,0:T(8,128)(2,1)}, u32[]{:S(2)}, u32[]{:S(2)}) collective-permute-start(bf16[1024,128]{1,0:T(8,128)(2,1)} %collective-permute-done.4.refs_9_), channel_id=1, source_target_pairs={{0,24},{4,100},{8,0},{12,108},{16,8},{20,116},{24,16},{28,124},{32... | collective-permute-start | bytes 786440 | tf_op jit(solution)/shard_map/ppermute | solution.py:50
  33.3 15.4 %collective-permute-start.10 = (bf16[4096,128]{1,0:T(8,128)(2,1)S(1)}, bf16[4096,128]{1,0:T(8,128)(2,1)}, u32[]{:S(2)}, u32[]{:S(2)}) collective-permute-start(bf16[4096,128]{1,0:T(8,128)(2,1)S(1)} %get-tuple-element.51.rest_0_), channel_id=1, source_target_pairs={{0,32},{4,12},{8,40},{12,20},{16,48},{20,28},{24,56},{28,4},{32,64... | collective-permute-start | bytes 3145736 | tf_op jit(solution)/shard_map/ppermute | solution.py:50
  34.6 18.1 %collective-permute-start.12 = (bf16[4096,128]{1,0:T(8,128)(2,1)S(1)}, bf16[4096,128]{1,0:T(8,128)(2,1)}, u32[]{:S(2)}, u32[]{:S(2)}) collective-permute-start(bf16[4096,128]{1,0:T(8,128)(2,1)S(1)} %get-tuple-element.51.rest_0_), channel_id=1, source_target_pairs={{0,96},{4,28},{8,104},{12,4},{16,112},{20,12},{24,120},{28,20},{32... | collective-permute-start | bytes 3145736 | tf_op jit(solution)/shard_map/ppermute | solution.py:50
  36.3 24.7 %collective-permute-start.8 = (bf16[4480,128]{1,0:T(8,128)(2,1)S(1)}, bf16[4480,128]{1,0:T(8,128)(2,1)S(1)}, u32[]{:S(2)}, u32[]{:S(2)}) collective-permute-start(bf16[4480,128]{1,0:T(8,128)(2,1)S(1)} %get-tuple-element.50.rest_1_), channel_id=1, source_target_pairs={{0,96},{4,28},{8,104},{12,4},{16,112},{20,12},{24,120},{28,20},{32... | collective-permute-start | bytes 3440648 | tf_op jit(solution)/shard_map/ppermute | solution.py:50
  37.7 26.2 %collective-permute-start.13 = (bf16[4096,128]{1,0:T(8,128)(2,1)S(1)}, bf16[4096,128]{1,0:T(8,128)(2,1)S(1)}, u32[]{:S(2)}, u32[]{:S(2)}) collective-permute-start(bf16[4096,128]{1,0:T(8,128)(2,1)S(1)} %get-tuple-element.51.rest_0_), channel_id=1, source_target_pairs={{0,4},{4,0},{8,12},{12,8},{16,20},{20,16},{24,28},{28,24},{32,36},... | collective-permute-start | bytes 3145736 | tf_op jit(solution)/shard_map/ppermute | solution.py:54
  41.7 26.4 %collective-permute-start.7 = (bf16[4480,128]{1,0:T(8,128)(2,1)S(1)}, bf16[4480,128]{1,0:T(8,128)(2,1)}, u32[]{:S(2)}, u32[]{:S(2)}) collective-permute-start(bf16[4480,128]{1,0:T(8,128)(2,1)S(1)} %get-tuple-element.50.rest_1_), channel_id=1, source_target_pairs={{0,32},{4,12},{8,40},{12,20},{16,48},{20,28},{24,56},{28,4},{32,64... | collective-permute-start | bytes 3440648 | tf_op jit(solution)/shard_map/ppermute | solution.py:50
  48.8 19.3 %collective-permute-start.14 = (bf16[4480,128]{1,0:T(8,128)(2,1)S(1)}, bf16[4480,128]{1,0:T(8,128)(2,1)S(1)}, u32[]{:S(2)}, u32[]{:S(2)}) collective-permute-start(bf16[4480,128]{1,0:T(8,128)(2,1)S(1)} %get-tuple-element.50.rest_1_), channel_id=1, source_target_pairs={{0,4},{4,0},{8,12},{12,8},{16,20},{20,16},{24,28},{28,24},{32,36},... | collective-permute-start | bytes 3440648 | tf_op jit(solution)/shard_map/ppermute | solution.py:54
  52.7 19.6 %collective-permute-start.11 = (bf16[4096,128]{1,0:T(8,128)(2,1)}, bf16[4096,128]{1,0:T(8,128)(2,1)}, u32[]{:S(2)}, u32[]{:S(2)}) collective-permute-start(bf16[4096,128]{1,0:T(8,128)(2,1)} %collective-permute-done.10.rest_2_), channel_id=1, source_target_pairs={{0,32},{4,12},{8,40},{12,20},{16,48},{20,28},{24,56},{28,4},{32,64... | collective-permute-start | bytes 3145736 | tf_op jit(solution)/shard_map/ppermute | solution.py:50
  61.0 15.7 %collective-permute-start.9 = (bf16[4480,128]{1,0:T(8,128)(2,1)S(1)}, bf16[4480,128]{1,0:T(8,128)(2,1)}, u32[]{:S(2)}, u32[]{:S(2)}) collective-permute-start(bf16[4480,128]{1,0:T(8,128)(2,1)S(1)} %collective-permute-done.8.left.rest_7_), channel_id=1, source_target_pairs={{0,96},{4,28},{8,104},{12,4},{16,112},{20,12},{24,120},{28,20},{32... | collective-permute-start | bytes 3440648 | tf_op jit(solution)/shard_map/ppermute | solution.py:50
  64.8 10.7 %collective-permute-start.15 = (bf16[4096,128]{1,0:T(8,128)(2,1)}, bf16[4096,128]{1,0:T(8,128)(2,1)}, u32[]{:S(2)}, u32[]{:S(2)}) collective-permute-start(bf16[4096,128]{1,0:T(8,128)(2,1)} %collective-permute-done.10.rest_2_), channel_id=1, source_target_pairs={{0,4},{4,0},{8,12},{12,8},{16,20},{20,16},{24,28},{28,24},{32,36},... | collective-permute-start | bytes 3145736 | tf_op jit(solution)/shard_map/ppermute | solution.py:54
  68.1 12.5 %collective-permute-start.16 = (bf16[4480,128]{1,0:T(8,128)(2,1)}, bf16[4480,128]{1,0:T(8,128)(2,1)}, u32[]{:S(2)}, u32[]{:S(2)}) collective-permute-start(bf16[4480,128]{1,0:T(8,128)(2,1)} %collective-permute-done.7.right.rest_3_), channel_id=1, source_target_pairs={{0,4},{4,0},{8,12},{12,8},{16,20},{20,16},{24,28},{28,24},{32,36},... | collective-permute-start | bytes 3440648 | tf_op jit(solution)/shard_map/ppermute | solution.py:54
  69.1 11.5 %collective-permute-start.18 = (bf16[4480,128]{1,0:T(8,128)(2,1)S(1)}, bf16[4480,128]{1,0:T(8,128)(2,1)}, u32[]{:S(2)}, u32[]{:S(2)}) collective-permute-start(bf16[4480,128]{1,0:T(8,128)(2,1)S(1)} %collective-permute-done.8.left.rest_7_), channel_id=1, source_target_pairs={{0,4},{4,0},{8,12},{12,8},{16,20},{20,16},{24,28},{28,24},{32,36},... | collective-permute-start | bytes 3440648 | tf_op jit(solution)/shard_map/ppermute | solution.py:54
  72.3 8.3 %collective-permute-start.17 = (bf16[4096,128]{1,0:T(8,128)(2,1)}, bf16[4096,128]{1,0:T(8,128)(2,1)}, u32[]{:S(2)}, u32[]{:S(2)}) collective-permute-start(bf16[4096,128]{1,0:T(8,128)(2,1)} %collective-permute-done.12.rest_1_.rest_6_), channel_id=1, source_target_pairs={{0,4},{4,0},{8,12},{12,8},{16,20},{20,16},{24,28},{28,24},{32,36},... | collective-permute-start | bytes 3145736 | tf_op jit(solution)/shard_map/ppermute | solution.py:54
  75.5 12.1 %collective-permute-start.20 = (bf16[4096,128]{1,0:T(8,128)(2,1)}, bf16[4096,128]{1,0:T(8,128)(2,1)}, u32[]{:S(2)}, u32[]{:S(2)}) collective-permute-start(bf16[4096,128]{1,0:T(8,128)(2,1)} %collective-permute-done.11.rest_0_.rest_4_), channel_id=1, source_target_pairs={{0,4},{4,0},{8,12},{12,8},{16,20},{20,16},{24,28},{28,24},{32,36},... | collective-permute-start | bytes 3145736 | tf_op jit(solution)/shard_map/ppermute | solution.py:54
  76.6 11.0 %collective-permute-start.21 = (bf16[4480,128]{1,0:T(8,128)(2,1)}, bf16[4480,128]{1,0:T(8,128)(2,1)}, u32[]{:S(2)}, u32[]{:S(2)}) collective-permute-start(bf16[4480,128]{1,0:T(8,128)(2,1)} %collective-permute-done.9.far.rest_5_), channel_id=1, source_target_pairs={{0,4},{4,0},{8,12},{12,8},{16,20},{20,16},{24,28},{28,24},{32,36},... | collective-permute-start | bytes 3440648 | tf_op jit(solution)/shard_map/ppermute | solution.py:54
  136.3 16.4 %collective-permute-start.24 = (bf16[2,2240,128]{2,1,0:T(8,128)(2,1)S(1)}, bf16[2,2240,128]{2,1,0:T(8,128)(2,1)S(1)}, u32[]{:S(2)}, u32[]{:S(2)}) collective-permute-start(bf16[2,2240,128]{2,1,0:T(8,128)(2,1)S(1)} %get-tuple-element.64.refs_4_), channel_id=1, source_target_pairs={{0,32},{4,12},{8,40},{12,20},{16,48},{20,28},{24,56},{28,4},{32,64... | collective-permute-start | bytes 3440648 | tf_op jit(solution)/shard_map/ppermute | solution.py:50
  136.4 16.3 %collective-permute-start.25 = (bf16[2,2240,128]{2,1,0:T(8,128)(2,1)S(1)}, bf16[2,2240,128]{2,1,0:T(8,128)(2,1)S(1)}, u32[]{:S(2)}, u32[]{:S(2)}) collective-permute-start(bf16[2,2240,128]{2,1,0:T(8,128)(2,1)S(1)} %get-tuple-element.65), channel_id=1, source_target_pairs={{0,96},{4,28},{8,104},{12,4},{16,112},{20,12},{24,120},{28,20},{32... | collective-permute-start | bytes 3440648 | tf_op jit(solution)/shard_map/ppermute | solution.py:50
  140.4 24.6 %collective-permute-start.27 = (bf16[2,2240,128]{2,1,0:T(8,128)(2,1)S(1)}, bf16[2,2240,128]{2,1,0:T(8,128)(2,1)S(1)}, u32[]{:S(2)}, u32[]{:S(2)}) collective-permute-start(bf16[2,2240,128]{2,1,0:T(8,128)(2,1)S(1)} %get-tuple-element.67), channel_id=1, source_target_pairs={{0,32},{4,12},{8,40},{12,20},{16,48},{20,28},{24,56},{28,4},{32,64... | collective-permute-start | bytes 3440648 | tf_op jit(solution)/shard_map/ppermute | solution.py:50
  140.5 24.5 %collective-permute-start.28 = (bf16[2,2240,128]{2,1,0:T(8,128)(2,1)S(1)}, bf16[2,2240,128]{2,1,0:T(8,128)(2,1)S(1)}, u32[]{:S(2)}, u32[]{:S(2)}) collective-permute-start(bf16[2,2240,128]{2,1,0:T(8,128)(2,1)S(1)} %get-tuple-element.68), channel_id=1, source_target_pairs={{0,96},{4,28},{8,104},{12,4},{16,112},{20,12},{24,120},{28,20},{32... | collective-permute-start | bytes 3440648 | tf_op jit(solution)/shard_map/ppermute | solution.py:50
  154.3 22.9 %collective-permute-start.26 = (bf16[2,2240,128]{2,1,0:T(8,128)(2,1)S(1)}, bf16[2,2240,128]{2,1,0:T(8,128)(2,1)S(1)}, u32[]{:S(2)}, u32[]{:S(2)}) collective-permute-start(bf16[2,2240,128]{2,1,0:T(8,128)(2,1)S(1)} %get-tuple-element.66), channel_id=1, source_target_pairs={{0,32},{4,12},{8,40},{12,20},{16,48},{20,28},{24,56},{28,4},{32,64... | collective-permute-start | bytes 3440648 | tf_op jit(solution)/shard_map/ppermute | solution.py:50
  154.4 22.8 %collective-permute-start.29 = (bf16[2,2240,128]{2,1,0:T(8,128)(2,1)S(1)}, bf16[2,2240,128]{2,1,0:T(8,128)(2,1)S(1)}, u32[]{:S(2)}, u32[]{:S(2)}) collective-permute-start(bf16[2,2240,128]{2,1,0:T(8,128)(2,1)S(1)} %get-tuple-element.69), channel_id=1, source_target_pairs={{0,96},{4,28},{8,104},{12,4},{16,112},{20,12},{24,120},{28,20},{32... | collective-permute-start | bytes 3440648 | tf_op jit(solution)/shard_map/ppermute | solution.py:50
  180.6 8.4 %collective-permute-start.30 = (bf16[1216,128]{1,0:T(8,128)(2,1)S(1)}, bf16[1216,128]{1,0:T(8,128)(2,1)S(1)}, u32[]{:S(2)}, u32[]{:S(2)}) collective-permute-start(bf16[1216,128]{1,0:T(8,128)(2,1)S(1)} %get-tuple-element.73), channel_id=1, source_target_pairs={{0,8},{4,36},{8,16},{12,44},{16,24},{20,52},{24,0},{28,60},{32,40}... | collective-permute-start | bytes 933896 | tf_op jit(solution)/shard_map/ppermute | solution.py:50
  184.4 14.9 %collective-permute-start.34 = (bf16[1216,128]{1,0:T(8,128)(2,1)S(1)}, bf16[1216,128]{1,0:T(8,128)(2,1)S(1)}, u32[]{:S(2)}, u32[]{:S(2)}) collective-permute-start(bf16[1216,128]{1,0:T(8,128)(2,1)S(1)} %get-tuple-element.77), channel_id=1, source_target_pairs={{0,24},{4,100},{8,0},{12,108},{16,8},{20,116},{24,16},{28,124},{32... | collective-permute-start | bytes 933896 | tf_op jit(solution)/shard_map/ppermute | solution.py:50
  189.2 10.1 %collective-permute-start.32 = (bf16[1216,128]{1,0:T(8,128)(2,1)S(1)}, bf16[1216,128]{1,0:T(8,128)(2,1)S(1)}, u32[]{:S(2)}, u32[]{:S(2)}) collective-permute-start(bf16[1216,128]{1,0:T(8,128)(2,1)S(1)} %get-tuple-element.75), channel_id=1, source_target_pairs={{0,8},{4,36},{8,16},{12,44},{16,24},{20,52},{24,0},{28,60},{32,40}... | collective-permute-start | bytes 933896 | tf_op jit(solution)/shard_map/ppermute | solution.py:50
  189.6 9.7 %collective-permute-start.33 = (bf16[1024,128]{1,0:T(8,128)(2,1)S(1)}, bf16[1024,128]{1,0:T(8,128)(2,1)S(1)}, u32[]{:S(2)}, u32[]{:S(2)}) collective-permute-start(bf16[1024,128]{1,0:T(8,128)(2,1)S(1)} %get-tuple-element.76), channel_id=1, source_target_pairs={{0,8},{4,36},{8,16},{12,44},{16,24},{20,52},{24,0},{28,60},{32,40}... | collective-permute-start | bytes 786440 | tf_op jit(solution)/shard_map/ppermute | solution.py:50
  191.0 8.3 %collective-permute-start.35 = (bf16[1024,128]{1,0:T(8,128)(2,1)S(1)}, bf16[1024,128]{1,0:T(8,128)(2,1)S(1)}, u32[]{:S(2)}, u32[]{:S(2)}) collective-permute-start(bf16[1024,128]{1,0:T(8,128)(2,1)S(1)} %get-tuple-element.78), channel_id=1, source_target_pairs={{0,24},{4,100},{8,0},{12,108},{16,8},{20,116},{24,16},{28,124},{32... | collective-permute-start | bytes 786440 | tf_op jit(solution)/shard_map/ppermute | solution.py:50
  (38 other events, 228.0 us)
Sparse Core Ops, SparseCore 0:
  9.7 86.3 all-gather.1
  111.2 80.1 reduce-scatter.1

commit v5 on v4

--- a/solution.py
+++ b/solution.py
@@ -241,8 +241,8 @@
         ),
         out_shape=[
             jax.ShapeDtypeStruct(queries.shape, BF),
-            jax.ShapeDtypeStruct(far, BF),
-            jax.ShapeDtypeStruct(far, BF),
+            pltpu.HBM(far, BF),
+            pltpu.HBM(far, BF),
             jax.ShapeDtypeStruct((8, queries.shape[0]), F32),
         ],
         compiler_params=params(20),

time: 213 us -> 212 us (level)
    unnamed x62 -> x58, local copies, waits for them, and re-layouts: 12.2 us -> 10.2 us
where the time goes in v5:
time: 212 us; the launch traced here: 211 us
  waiting for transfers between devices  67.5 us (32%)
  starting transfers between devices  53.1 us (25%)
  Pallas kernels  46.3 us (22%)
  matrix products  17.4 us (8%)
  between operations  14.6 us (7%)
  local copies, waits for them, and re-layouts  10.8 us (5%)
    ppermute x24, waiting for transfers between devices, ring_move(): return lax.ppermute(value, 'ctx', pairs)  61.7 us
    ppermute x24, starting transfers between devices, ring_move(): return lax.ppermute(value, 'ctx', pairs)  31.5 us
    ppermute x13, starting transfers between devices, swap(): return lax.ppermute(value, 'ctx', [(i, i ^ 1) for i in range(CTX)])  21.6 us
    dot_general x3, matrix products, dot(): lax.dot_general(a, b, (((ca,), (cb,)), ((), ())), preferred_element_type=...  17.4 us
    pallas_call x1, Pallas kernels, sparse_forward(): pl.pallas_call(sparse_forward_kernel, grid_spec=pltpu.PrefetchScalarGridS...  10.3 us
    unnamed x58, local copies, waits for them, and re-layouts  10.2 us
    pallas_call x9, Pallas kernels, whole_call(): pl.pallas_call(functools.partial(drop, kernel, n_in, len(deps)), in_specs...  9.52 us
    pallas_call x1, Pallas kernels, sparse_backward(): pl.pallas_call(sparse_backward_kernel, grid_spec=pltpu.PrefetchScalarGrid...  9.17 us
  transfers between devices with their start and end apart: 39, of which 16 were waited for; matrix products, arithmetic and copies ran while one was open for 9% of the time, Pallas kernels for 22%

profile of v5, /device:TPU:1, one launch (start us, length us, event | category | flops | bytes accessed | tf_op | source)
XLA Modules:
  0.0 211.2 jit_solution(14714667919401796112)
XLA Ops:
  15.4 2.1 %collective-permute-start.4 = (bf16[1024,128]{1,0:T(8,128)(2,1)}, bf16[1024,128]{1,0:T(8,128)(2,1)}, u32[]{:S(2)}, u32[]{:S(2)}) collective-permute-start(bf16[1024,128]{1,0:T(8,128)(2,1)} %get-tuple-element.48.refs_3_), channel_id=1, source_target_pairs={{0,24},{4,100},{8,0},{12,108},{16,8},{20,116},{24,16},{28,124},{32... | collective-permute-start | bytes 786440 | tf_op jit(solution)/shard_map/ppermute | solution.py:50
  18.9 2.8 %collective-permute-done.1.refs_4_ = bf16[1216,128]{1,0:T(8,128)(2,1)S(1)} collective-permute-done((bf16[1216,128]{1,0:T(8,128)(2,1)S(1)}, bf16[1216,128]{1,0:T(8,128)(2,1)S(1)}, u32[]{:S(2)}, u32[]{:S(2)}) %collective-permute-start.1) | collective-permute-done | bytes 311328 | tf_op jit(solution)/shard_map/ppermute | solution.py:50
  24.5 7.4 %collective-permute-done.2.refs_5_ = bf16[1024,128]{1,0:T(8,128)(2,1)} collective-permute-done((bf16[1024,128]{1,0:T(8,128)(2,1)}, bf16[1024,128]{1,0:T(8,128)(2,1)}, u32[]{:S(2)}, u32[]{:S(2)}) %collective-permute-start.2) | collective-permute-done | bytes 262176 | tf_op jit(solution)/shard_map/ppermute | solution.py:50
  37.7 3.1 %collective-permute-start.13 = (bf16[4096,128]{1,0:T(8,128)(2,1)S(1)}, bf16[4096,128]{1,0:T(8,128)(2,1)S(1)}, u32[]{:S(2)}, u32[]{:S(2)}) collective-permute-start(bf16[4096,128]{1,0:T(8,128)(2,1)S(1)} %get-tuple-element.51.rest_0_), channel_id=1, source_target_pairs={{0,4},{4,0},{8,12},{12,8},{16,20},{20,16},{24,28},{28,24},{32,36},... | collective-permute-start | bytes 3145736 | tf_op jit(solution)/shard_map/ppermute | solution.py:54
  41.8 7.0 %collective-permute-done.10.rest_2_ = bf16[4096,128]{1,0:T(8,128)(2,1)} collective-permute-done((bf16[4096,128]{1,0:T(8,128)(2,1)S(1)}, bf16[4096,128]{1,0:T(8,128)(2,1)}, u32[]{:S(2)}, u32[]{:S(2)}) %collective-permute-start.10) | collective-permute-done | bytes 1048608 | tf_op jit(solution)/shard_map/ppermute | solution.py:50
  48.8 2.9 %collective-permute-start.14 = (bf16[4480,128]{1,0:T(8,128)(2,1)S(1)}, bf16[4480,128]{1,0:T(8,128)(2,1)S(1)}, u32[]{:S(2)}, u32[]{:S(2)}) collective-permute-start(bf16[4480,128]{1,0:T(8,128)(2,1)S(1)} %get-tuple-element.50.rest_1_), channel_id=1, source_target_pairs={{0,4},{4,0},{8,12},{12,8},{16,20},{20,16},{24,28},{28,24},{32,36},... | collective-permute-start | bytes 3440648 | tf_op jit(solution)/shard_map/ppermute | solution.py:54
  52.7 8.3 %collective-permute-done.8.left.rest_7_ = bf16[4480,128]{1,0:T(8,128)(2,1)S(1)} collective-permute-done((bf16[4480,128]{1,0:T(8,128)(2,1)S(1)}, bf16[4480,128]{1,0:T(8,128)(2,1)S(1)}, u32[]{:S(2)}, u32[]{:S(2)}) %collective-permute-start.8) | collective-permute-done | bytes 1146912 | tf_op jit(solution)/shard_map/ppermute | solution.py:50
  61.0 2.9 %collective-permute-start.9 = (bf16[4480,128]{1,0:T(8,128)(2,1)S(1)}, bf16[4480,128]{1,0:T(8,128)(2,1)}, u32[]{:S(2)}, u32[]{:S(2)}) collective-permute-start(bf16[4480,128]{1,0:T(8,128)(2,1)S(1)} %collective-permute-done.8.left.rest_7_), channel_id=1, source_target_pairs={{0,96},{4,28},{8,104},{12,4},{16,112},{20,12},{24,120},{28,20},{32... | collective-permute-start | bytes 3440648 | tf_op jit(solution)/shard_map/ppermute | solution.py:50
  64.8 3.3 %collective-permute-start.15 = (bf16[4096,128]{1,0:T(8,128)(2,1)}, bf16[4096,128]{1,0:T(8,128)(2,1)}, u32[]{:S(2)}, u32[]{:S(2)}) collective-permute-start(bf16[4096,128]{1,0:T(8,128)(2,1)} %collective-permute-done.10.rest_2_), channel_id=1, source_target_pairs={{0,4},{4,0},{8,12},{12,8},{16,20},{20,16},{24,28},{28,24},{32,36},... | collective-permute-start | bytes 3145736 | tf_op jit(solution)/shard_map/ppermute | solution.py:54
  69.6 2.7 %collective-permute-done.11.rest_0_.rest_4_ = bf16[4096,128]{1,0:T(8,128)(2,1)} collective-permute-done((bf16[4096,128]{1,0:T(8,128)(2,1)}, bf16[4096,128]{1,0:T(8,128)(2,1)}, u32[]{:S(2)}, u32[]{:S(2)}) %collective-permute-start.11) | collective-permute-done | bytes 1048608 | tf_op jit(solution)/shard_map/ppermute | solution.py:50
  72.3 2.9 %collective-permute-start.17 = (bf16[4096,128]{1,0:T(8,128)(2,1)}, bf16[4096,128]{1,0:T(8,128)(2,1)}, u32[]{:S(2)}, u32[]{:S(2)}) collective-permute-start(bf16[4096,128]{1,0:T(8,128)(2,1)} %collective-permute-done.12.rest_1_.rest_6_), channel_id=1, source_target_pairs={{0,4},{4,0},{8,12},{12,8},{16,20},{20,16},{24,28},{28,24},{32,36},... | collective-permute-start | bytes 3145736 | tf_op jit(solution)/shard_map/ppermute | solution.py:54
  76.6 3.9 %collective-permute-start.21 = (bf16[4480,128]{1,0:T(8,128)(2,1)}, bf16[4480,128]{1,0:T(8,128)(2,1)}, u32[]{:S(2)}, u32[]{:S(2)}) collective-permute-start(bf16[4480,128]{1,0:T(8,128)(2,1)} %collective-permute-done.9.far.rest_5_), channel_id=1, source_target_pairs={{0,4},{4,0},{8,12},{12,8},{16,20},{20,16},{24,28},{28,24},{32,36},... | collective-permute-start | bytes 3440648 | tf_op jit(solution)/shard_map/ppermute | solution.py:54
  83.2 1.9 prefix.1
  87.7 10.3 %sparse_forward.1 = (bf16[1024,512]{1,0:T(8,128)(2,1)S(1)}, bf16[8,512,128]{2,1,0:T(8,128)(2,1)}, bf16[8,512,128]{2,1,0:T(8,128)(2,1)}, f32[8,1024]{1,0:T(8,128)S(1)}) custom-call(s32[8,5]{1,0:T(8,128)S(1)} %stack.14.table, bf16[1024,512]{1,0:T(8,128)(2,1)S(1)} %copy-done.8, bf16[1024,512]{1,0:T(8,128)(2,1)S(1)} %copy-done, bf16[1024,512]{1,0:T(8,128)(2,1)S(1)} %copy-done.1, ...), custom_call_target="tpu_custom_call" | custom-call | flops 4000000000 | bytes 12582912 | tf_op jit(solution)/shard_map/sparse_forward/pallas_call | solution.py:225
  98.1 3.8 %linear_forward.1.o_ref = bf16[1024,512]{1,0:T(8,128)(2,1)S(1)} custom-call(bf16[1024,512]{1,0:T(8,128)(2,1)S(1)} %copy-done.8, bf16[1024,512]{1,0:T(8,128)(2,1)S(1)} %copy-done, bf16[1024,512]{1,0:T(8,128)(2,1)S(1)} %copy-done.1, f32[8,1024]{1,0:T(8,128)S(1)} %broadcast_in_dim.32.c_ref, ...), custom_call_target="tpu_custom_call", output_to_operand_aliasing={{}: (5, {})} | custom-call | flops 2400000000 | bytes 4194304 | tf_op jit(solution)/shard_map/linear_forward/pallas_call | solution.py:132
  101.9 6.9 %convolution_convert_fusion = bf16[1024,4096]{1,0:T(8,128)(2,1)} fusion(bf16[1024,512]{1,0:T(8,128)(2,1)S(1)} %linear_forward.1.o_ref, bf16[4096,512]{1,0:T(8,128)(2,1)S(1)} %copy-done.25), kind=kOutput, calls=%fused_computation | convolution fusion | flops 4299161600 | bytes 13631488 | tf_op jit(solution)/shard_map/dot_general | solution.py:31
  110.3 6.1 %convolution_convert_fusion.1.g_ref = bf16[1024,128]{1,0:T(8,128)(2,1)S(1)} fusion(bf16[1024,4096]{1,0:T(8,128)(2,1)} %all-gather.2.cloned.1.call-done, bf16[4096,512]{1,0:T(8,128)(2,1)} %param.9), kind=kOutput, calls=%fused_computation.4 | convolution fusion | flops 1073872896 | bytes 9699328 | tf_op jit(solution)/shard_map/dot_general | solution.py:31
  116.5 9.2 %sparse_backward.1 = (bf16[1024,512]{1,0:T(8,128)(2,1)}, f32[1024,512]{1,0:T(8,128)S(1)}, f32[1024,512]{1,0:T(8,128)S(1)}, bf16[8,512,128]{2,1,0:T(8,128)(2,1)S(1)}, bf16[8,512,128]{2,1,0:T(8,128)(2,1)S(1)}) custom-call(s32[1]{0:T(128)} %bitcast.refs_0_.core, s32[8,5]{1,0:T(8,128)S(1)} %stack.14.table, bf16[1024,512]{1,0:T(8,128)(2,1)S(1)} %copy-done.9, ...), custom_call_target="tpu_custom_call" | custom-call | flops 8000000000 | bytes 8388608 | tf_op jit(solution)/shard_map/sparse_backward/pallas_call | solution.py:287
  126.2 4.5 %fusion.2.g_ref = bf16[1024,384]{1,0:T(8,128)(2,1)S(1)} fusion(bf16[1024,4096]{1,0:T(8,128)(2,1)S(1)} %bitcast.16, bf16[4096,512]{1,0:T(8,128)(2,1)S(1)} %copy-done.26), kind=kOutput, calls=%fused_computation.3 | convolution fusion | flops 3221618688 | bytes 12320768 | tf_op jit(solution)/shard_map/dot_general | solution.py:31
  130.7 1.8 block_adjoints.1.adj
  135.4 2.7 %collective-permute-start.25 = (bf16[2,2240,128]{2,1,0:T(8,128)(2,1)S(1)}, bf16[2,2240,128]{2,1,0:T(8,128)(2,1)S(1)}, u32[]{:S(2)}, u32[]{:S(2)}) collective-permute-start(bf16[2,2240,128]{2,1,0:T(8,128)(2,1)S(1)} %get-tuple-element.65), channel_id=1, source_target_pairs={{0,96},{4,28},{8,104},{12,4},{16,112},{20,12},{24,120},{28,20},{32... | collective-permute-start | bytes 3440648 | tf_op jit(solution)/shard_map/ppermute | solution.py:50
  139.6 2.7 %collective-permute-start.28 = (bf16[2,2240,128]{2,1,0:T(8,128)(2,1)S(1)}, bf16[2,2240,128]{2,1,0:T(8,128)(2,1)S(1)}, u32[]{:S(2)}, u32[]{:S(2)}) collective-permute-start(bf16[2,2240,128]{2,1,0:T(8,128)(2,1)S(1)} %get-tuple-element.68), channel_id=1, source_target_pairs={{0,96},{4,28},{8,104},{12,4},{16,112},{20,12},{24,120},{28,20},{32... | collective-permute-start | bytes 3440648 | tf_op jit(solution)/shard_map/ppermute | solution.py:50
  142.2 9.5 %collective-permute-done.24.refs_4_ = bf16[2,2240,128]{2,1,0:T(8,128)(2,1)S(1)} collective-permute-done((bf16[2,2240,128]{2,1,0:T(8,128)(2,1)S(1)}, bf16[2,2240,128]{2,1,0:T(8,128)(2,1)S(1)}, u32[]{:S(2)}, u32[]{:S(2)}) %collective-permute-start.24) | collective-permute-done | bytes 1146912 | tf_op jit(solution)/shard_map/ppermute | solution.py:50
  153.5 2.7 %collective-permute-start.29 = (bf16[2,2240,128]{2,1,0:T(8,128)(2,1)S(1)}, bf16[2,2240,128]{2,1,0:T(8,128)(2,1)S(1)}, u32[]{:S(2)}, u32[]{:S(2)}) collective-permute-start(bf16[2,2240,128]{2,1,0:T(8,128)(2,1)S(1)} %get-tuple-element.69), channel_id=1, source_target_pairs={{0,96},{4,28},{8,104},{12,4},{16,112},{20,12},{24,120},{28,20},{32... | collective-permute-start | bytes 3440648 | tf_op jit(solution)/shard_map/ppermute | solution.py:50
  156.2 7.4 %linear_backward.1 = (bf16[1024,512]{1,0:T(8,128)(2,1)}, f32[1024,512]{1,0:T(8,128)S(1)}, f32[1024,512]{1,0:T(8,128)S(1)}) custom-call(bf16[1024,512]{1,0:T(8,128)(2,1)S(1)} %copy-done.9, bf16[1024,512]{1,0:T(8,128)(2,1)S(1)} %copy-done, bf16[1024,512]{1,0:T(8,128)(2,1)S(1)} %copy-done.1, ...), custom_call_target="tpu_custom_call", output_to_operand_aliasing={{0}: (6, {}), {1}: (7, {}), {2}: (8, {})} | custom-call | flops 5000000000 | bytes 9437184 | tf_op jit(solution)/shard_map/linear_backward/pallas_call | solution.py:161
  164.0 12.3 %collective-permute-done.26.refs_4_ = bf16[2,2240,128]{2,1,0:T(8,128)(2,1)S(1)} collective-permute-done((bf16[2,2240,128]{2,1,0:T(8,128)(2,1)S(1)}, bf16[2,2240,128]{2,1,0:T(8,128)(2,1)S(1)}, u32[]{:S(2)}, u32[]{:S(2)}) %collective-permute-start.26) | collective-permute-done | bytes 1146912 | tf_op jit(solution)/shard_map/ppermute | solution.py:50
  177.5 2.1 back_turn.1
  180.7 2.4 %collective-permute-start.31 = (bf16[1024,128]{1,0:T(8,128)(2,1)S(1)}, bf16[1024,128]{1,0:T(8,128)(2,1)S(1)}, u32[]{:S(2)}, u32[]{:S(2)}) collective-permute-start(bf16[1024,128]{1,0:T(8,128)(2,1)S(1)} %get-tuple-element.74), channel_id=1, source_target_pairs={{0,24},{4,100},{8,0},{12,108},{16,8},{20,116},{24,16},{28,124},{32... | collective-permute-start | bytes 786440 | tf_op jit(solution)/shard_map/ppermute | solution.py:50
  184.5 2.2 %collective-permute-done.31.refs_3_ = bf16[1024,128]{1,0:T(8,128)(2,1)S(1)} collective-permute-done((bf16[1024,128]{1,0:T(8,128)(2,1)S(1)}, bf16[1024,128]{1,0:T(8,128)(2,1)S(1)}, u32[]{:S(2)}, u32[]{:S(2)}) %collective-permute-start.31) | collective-permute-done | bytes 262176 | tf_op jit(solution)/shard_map/ppermute | solution.py:50
  191.0 6.9 %collective-permute-done.33.refs_2_ = bf16[1024,128]{1,0:T(8,128)(2,1)S(1)} collective-permute-done((bf16[1024,128]{1,0:T(8,128)(2,1)S(1)}, bf16[1024,128]{1,0:T(8,128)(2,1)S(1)}, u32[]{:S(2)}, u32[]{:S(2)}) %collective-permute-start.33) | collective-permute-done | bytes 262176 | tf_op jit(solution)/shard_map/ppermute | solution.py:50
  198.2 2.5 %collective-permute-start.36 = (bf16[1216,128]{1,0:T(8,128)(2,1)S(1)}, bf16[1216,128]{1,0:T(8,128)(2,1)S(1)}, u32[]{:S(2)}, u32[]{:S(2)}) collective-permute-start(bf16[1216,128]{1,0:T(8,128)(2,1)S(1)} %get-tuple-element.80), channel_id=1, source_target_pairs={{0,4},{4,0},{8,12},{12,8},{16,20},{20,16},{24,28},{28,24},{32,36},... | collective-permute-start | bytes 933896 | tf_op jit(solution)/shard_map/ppermute | solution.py:54
  201.9 2.4 %finish.1 = (bf16[1024,512]{1,0:T(8,128)(2,1)}, bf16[1024,512]{1,0:T(8,128)(2,1)}) custom-call(s32[1]{0:T(128)} %bitcast.refs_0_.core, bf16[1024,512]{1,0:T(8,128)(2,1)S(1)} %copy-done, bf16[1024,512]{1,0:T(8,128)(2,1)S(1)} %copy-done.1, f32[1024,512]{1,0:T(8,128)S(1)} %get-tuple-element.60.dk, f32[1024,512]{1,0:T(8,128)S(1)} %get-tuple-element.61.dv, ...), custom_call_target="tpu_custom_call" | custom-call | flops 500000000 | bytes 9437184 | tf_op jit(solution)/shard_map/finish/pallas_call | solution.py:478
  (153 shorter events, 47.1 us)
Async XLA Ops:
  7.2 103.1 %all-gather.2.cloned.1.call-start = ((), (), s32[]{:S(2)}) async-start(), calls=%async_computation.2 | async-start | bytes 10485760 | tf_op jit(solution)/shard_map/all_gather | solution.py:571
  7.9 196.4 %reduce-scatter.2.cloned.1.call-start = ((), (), s32[]{:S(2)}) async-start(), calls=%async_computation.1 | async-start | bytes 10485760 | tf_op jit(solution)/shard_map/reduce_scatter | solution.py:610
  13.6 8.1 %collective-permute-start.1 = (bf16[1216,128]{1,0:T(8,128)(2,1)S(1)}, bf16[1216,128]{1,0:T(8,128)(2,1)S(1)}, u32[]{:S(2)}, u32[]{:S(2)}) collective-permute-start(bf16[1216,128]{1,0:T(8,128)(2,1)S(1)} %get-tuple-element.47.refs_2_), channel_id=1, source_target_pairs={{0,8},{4,36},{8,16},{12,44},{16,24},{20,52},{24,0},{28,60},{32,40}... | collective-permute-start | bytes 933896 | tf_op jit(solution)/shard_map/ppermute | solution.py:50
  17.5 14.5 %collective-permute-start.6 = (bf16[1216,128]{1,0:T(8,128)(2,1)S(1)}, bf16[1216,128]{1,0:T(8,128)(2,1)S(1)}, u32[]{:S(2)}, u32[]{:S(2)}) collective-permute-start(bf16[1216,128]{1,0:T(8,128)(2,1)S(1)} %get-tuple-element.47.refs_2_), channel_id=1, source_target_pairs={{0,24},{4,100},{8,0},{12,108},{16,8},{20,116},{24,16},{28,124},{32... | collective-permute-start | bytes 933896 | tf_op jit(solution)/shard_map/ppermute | solution.py:50
  21.8 10.2 %collective-permute-start.3 = (bf16[1216,128]{1,0:T(8,128)(2,1)S(1)}, bf16[1216,128]{1,0:T(8,128)(2,1)S(1)}, u32[]{:S(2)}, u32[]{:S(2)}) collective-permute-start(bf16[1216,128]{1,0:T(8,128)(2,1)S(1)} %collective-permute-done.1.refs_4_), channel_id=1, source_target_pairs={{0,8},{4,36},{8,16},{12,44},{16,24},{20,52},{24,0},{28,60},{32,40}... | collective-permute-start | bytes 933896 | tf_op jit(solution)/shard_map/ppermute | solution.py:50
  21.8 10.2 %collective-permute-start.2 = (bf16[1024,128]{1,0:T(8,128)(2,1)}, bf16[1024,128]{1,0:T(8,128)(2,1)}, u32[]{:S(2)}, u32[]{:S(2)}) collective-permute-start(bf16[1024,128]{1,0:T(8,128)(2,1)} %get-tuple-element.48.refs_3_), channel_id=1, source_target_pairs={{0,8},{4,36},{8,16},{12,44},{16,24},{20,52},{24,0},{28,60},{32,40}... | collective-permute-start | bytes 786440 | tf_op jit(solution)/shard_map/ppermute | solution.py:50
  23.2 8.8 %collective-permute-start.5 = (bf16[1024,128]{1,0:T(8,128)(2,1)}, bf16[1024,128]{1,0:T(8,128)(2,1)}, u32[]{:S(2)}, u32[]{:S(2)}) collective-permute-start(bf16[1024,128]{1,0:T(8,128)(2,1)} %collective-permute-done.4.refs_9_), channel_id=1, source_target_pairs={{0,24},{4,100},{8,0},{12,108},{16,8},{20,116},{24,16},{28,124},{32... | collective-permute-start | bytes 786440 | tf_op jit(solution)/shard_map/ppermute | solution.py:50
  33.3 15.4 %collective-permute-start.10 = (bf16[4096,128]{1,0:T(8,128)(2,1)S(1)}, bf16[4096,128]{1,0:T(8,128)(2,1)}, u32[]{:S(2)}, u32[]{:S(2)}) collective-permute-start(bf16[4096,128]{1,0:T(8,128)(2,1)S(1)} %get-tuple-element.51.rest_0_), channel_id=1, source_target_pairs={{0,32},{4,12},{8,40},{12,20},{16,48},{20,28},{24,56},{28,4},{32,64... | collective-permute-start | bytes 3145736 | tf_op jit(solution)/shard_map/ppermute | solution.py:50
  34.6 18.0 %collective-permute-start.12 = (bf16[4096,128]{1,0:T(8,128)(2,1)S(1)}, bf16[4096,128]{1,0:T(8,128)(2,1)}, u32[]{:S(2)}, u32[]{:S(2)}) collective-permute-start(bf16[4096,128]{1,0:T(8,128)(2,1)S(1)} %get-tuple-element.51.rest_0_), channel_id=1, source_target_pairs={{0,96},{4,28},{8,104},{12,4},{16,112},{20,12},{24,120},{28,20},{32... | collective-permute-start | bytes 3145736 | tf_op jit(solution)/shard_map/ppermute | solution.py:50
  36.3 24.7 %collective-permute-start.8 = (bf16[4480,128]{1,0:T(8,128)(2,1)S(1)}, bf16[4480,128]{1,0:T(8,128)(2,1)S(1)}, u32[]{:S(2)}, u32[]{:S(2)}) collective-permute-start(bf16[4480,128]{1,0:T(8,128)(2,1)S(1)} %get-tuple-element.50.rest_1_), channel_id=1, source_target_pairs={{0,96},{4,28},{8,104},{12,4},{16,112},{20,12},{24,120},{28,20},{32... | collective-permute-start | bytes 3440648 | tf_op jit(solution)/shard_map/ppermute | solution.py:50
  37.7 26.2 %collective-permute-start.13 = (bf16[4096,128]{1,0:T(8,128)(2,1)S(1)}, bf16[4096,128]{1,0:T(8,128)(2,1)S(1)}, u32[]{:S(2)}, u32[]{:S(2)}) collective-permute-start(bf16[4096,128]{1,0:T(8,128)(2,1)S(1)} %get-tuple-element.51.rest_0_), channel_id=1, source_target_pairs={{0,4},{4,0},{8,12},{12,8},{16,20},{20,16},{24,28},{28,24},{32,36},... | collective-permute-start | bytes 3145736 | tf_op jit(solution)/shard_map/ppermute | solution.py:54
  41.7 26.4 %collective-permute-start.7 = (bf16[4480,128]{1,0:T(8,128)(2,1)S(1)}, bf16[4480,128]{1,0:T(8,128)(2,1)}, u32[]{:S(2)}, u32[]{:S(2)}) collective-permute-start(bf16[4480,128]{1,0:T(8,128)(2,1)S(1)} %get-tuple-element.50.rest_1_), channel_id=1, source_target_pairs={{0,32},{4,12},{8,40},{12,20},{16,48},{20,28},{24,56},{28,4},{32,64... | collective-permute-start | bytes 3440648 | tf_op jit(solution)/shard_map/ppermute | solution.py:50
  48.8 19.3 %collective-permute-start.14 = (bf16[4480,128]{1,0:T(8,128)(2,1)S(1)}, bf16[4480,128]{1,0:T(8,128)(2,1)S(1)}, u32[]{:S(2)}, u32[]{:S(2)}) collective-permute-start(bf16[4480,128]{1,0:T(8,128)(2,1)S(1)} %get-tuple-element.50.rest_1_), channel_id=1, source_target_pairs={{0,4},{4,0},{8,12},{12,8},{16,20},{20,16},{24,28},{28,24},{32,36},... | collective-permute-start | bytes 3440648 | tf_op jit(solution)/shard_map/ppermute | solution.py:54
  52.7 19.6 %collective-permute-start.11 = (bf16[4096,128]{1,0:T(8,128)(2,1)}, bf16[4096,128]{1,0:T(8,128)(2,1)}, u32[]{:S(2)}, u32[]{:S(2)}) collective-permute-start(bf16[4096,128]{1,0:T(8,128)(2,1)} %collective-permute-done.10.rest_2_), channel_id=1, source_target_pairs={{0,32},{4,12},{8,40},{12,20},{16,48},{20,28},{24,56},{28,4},{32,64... | collective-permute-start | bytes 3145736 | tf_op jit(solution)/shard_map/ppermute | solution.py:50
  61.0 15.7 %collective-permute-start.9 = (bf16[4480,128]{1,0:T(8,128)(2,1)S(1)}, bf16[4480,128]{1,0:T(8,128)(2,1)}, u32[]{:S(2)}, u32[]{:S(2)}) collective-permute-start(bf16[4480,128]{1,0:T(8,128)(2,1)S(1)} %collective-permute-done.8.left.rest_7_), channel_id=1, source_target_pairs={{0,96},{4,28},{8,104},{12,4},{16,112},{20,12},{24,120},{28,20},{32... | collective-permute-start | bytes 3440648 | tf_op jit(solution)/shard_map/ppermute | solution.py:50
  64.8 10.7 %collective-permute-start.15 = (bf16[4096,128]{1,0:T(8,128)(2,1)}, bf16[4096,128]{1,0:T(8,128)(2,1)}, u32[]{:S(2)}, u32[]{:S(2)}) collective-permute-start(bf16[4096,128]{1,0:T(8,128)(2,1)} %collective-permute-done.10.rest_2_), channel_id=1, source_target_pairs={{0,4},{4,0},{8,12},{12,8},{16,20},{20,16},{24,28},{28,24},{32,36},... | collective-permute-start | bytes 3145736 | tf_op jit(solution)/shard_map/ppermute | solution.py:54
  68.1 12.5 %collective-permute-start.16 = (bf16[4480,128]{1,0:T(8,128)(2,1)}, bf16[4480,128]{1,0:T(8,128)(2,1)}, u32[]{:S(2)}, u32[]{:S(2)}) collective-permute-start(bf16[4480,128]{1,0:T(8,128)(2,1)} %collective-permute-done.7.right.rest_3_), channel_id=1, source_target_pairs={{0,4},{4,0},{8,12},{12,8},{16,20},{20,16},{24,28},{28,24},{32,36},... | collective-permute-start | bytes 3440648 | tf_op jit(solution)/shard_map/ppermute | solution.py:54
  69.1 11.5 %collective-permute-start.18 = (bf16[4480,128]{1,0:T(8,128)(2,1)S(1)}, bf16[4480,128]{1,0:T(8,128)(2,1)}, u32[]{:S(2)}, u32[]{:S(2)}) collective-permute-start(bf16[4480,128]{1,0:T(8,128)(2,1)S(1)} %collective-permute-done.8.left.rest_7_), channel_id=1, source_target_pairs={{0,4},{4,0},{8,12},{12,8},{16,20},{20,16},{24,28},{28,24},{32,36},... | collective-permute-start | bytes 3440648 | tf_op jit(solution)/shard_map/ppermute | solution.py:54
  72.3 8.3 %collective-permute-start.17 = (bf16[4096,128]{1,0:T(8,128)(2,1)}, bf16[4096,128]{1,0:T(8,128)(2,1)}, u32[]{:S(2)}, u32[]{:S(2)}) collective-permute-start(bf16[4096,128]{1,0:T(8,128)(2,1)} %collective-permute-done.12.rest_1_.rest_6_), channel_id=1, source_target_pairs={{0,4},{4,0},{8,12},{12,8},{16,20},{20,16},{24,28},{28,24},{32,36},... | collective-permute-start | bytes 3145736 | tf_op jit(solution)/shard_map/ppermute | solution.py:54
  75.5 12.1 %collective-permute-start.20 = (bf16[4096,128]{1,0:T(8,128)(2,1)}, bf16[4096,128]{1,0:T(8,128)(2,1)}, u32[]{:S(2)}, u32[]{:S(2)}) collective-permute-start(bf16[4096,128]{1,0:T(8,128)(2,1)} %collective-permute-done.11.rest_0_.rest_4_), channel_id=1, source_target_pairs={{0,4},{4,0},{8,12},{12,8},{16,20},{20,16},{24,28},{28,24},{32,36},... | collective-permute-start | bytes 3145736 | tf_op jit(solution)/shard_map/ppermute | solution.py:54
  76.6 11.0 %collective-permute-start.21 = (bf16[4480,128]{1,0:T(8,128)(2,1)}, bf16[4480,128]{1,0:T(8,128)(2,1)}, u32[]{:S(2)}, u32[]{:S(2)}) collective-permute-start(bf16[4480,128]{1,0:T(8,128)(2,1)} %collective-permute-done.9.far.rest_5_), channel_id=1, source_target_pairs={{0,4},{4,0},{8,12},{12,8},{16,20},{20,16},{24,28},{28,24},{32,36},... | collective-permute-start | bytes 3440648 | tf_op jit(solution)/shard_map/ppermute | solution.py:54
  125.6 8.4 %collective-permute-start.22 = (bf16[8,512,128]{2,1,0:T(8,128)(2,1)S(1)}, bf16[8,512,128]{2,1,0:T(8,128)(2,1)S(1)}, u32[]{:S(2)}, u32[]{:S(2)}) collective-permute-start(bf16[8,512,128]{2,1,0:T(8,128)(2,1)S(1)} %get-tuple-element.63), channel_id=1, source_target_pairs={{0,4},{4,0},{8,12},{12,8},{16,20},{20,16},{24,28},{28,24},{32,36},... | collective-permute-start | bytes 3145736 | tf_op jit(solution)/shard_map/ppermute | solution.py:54
  135.4 16.4 %collective-permute-start.24 = (bf16[2,2240,128]{2,1,0:T(8,128)(2,1)S(1)}, bf16[2,2240,128]{2,1,0:T(8,128)(2,1)S(1)}, u32[]{:S(2)}, u32[]{:S(2)}) collective-permute-start(bf16[2,2240,128]{2,1,0:T(8,128)(2,1)S(1)} %get-tuple-element.64.refs_4_), channel_id=1, source_target_pairs={{0,32},{4,12},{8,40},{12,20},{16,48},{20,28},{24,56},{28,4},{32,64... | collective-permute-start | bytes 3440648 | tf_op jit(solution)/shard_map/ppermute | solution.py:50
  135.4 16.3 %collective-permute-start.25 = (bf16[2,2240,128]{2,1,0:T(8,128)(2,1)S(1)}, bf16[2,2240,128]{2,1,0:T(8,128)(2,1)S(1)}, u32[]{:S(2)}, u32[]{:S(2)}) collective-permute-start(bf16[2,2240,128]{2,1,0:T(8,128)(2,1)S(1)} %get-tuple-element.65), channel_id=1, source_target_pairs={{0,96},{4,28},{8,104},{12,4},{16,112},{20,12},{24,120},{28,20},{32... | collective-permute-start | bytes 3440648 | tf_op jit(solution)/shard_map/ppermute | solution.py:50
  139.5 24.6 %collective-permute-start.27 = (bf16[2,2240,128]{2,1,0:T(8,128)(2,1)S(1)}, bf16[2,2240,128]{2,1,0:T(8,128)(2,1)S(1)}, u32[]{:S(2)}, u32[]{:S(2)}) collective-permute-start(bf16[2,2240,128]{2,1,0:T(8,128)(2,1)S(1)} %get-tuple-element.67), channel_id=1, source_target_pairs={{0,32},{4,12},{8,40},{12,20},{16,48},{20,28},{24,56},{28,4},{32,64... | collective-permute-start | bytes 3440648 | tf_op jit(solution)/shard_map/ppermute | solution.py:50
  139.6 24.5 %collective-permute-start.28 = (bf16[2,2240,128]{2,1,0:T(8,128)(2,1)S(1)}, bf16[2,2240,128]{2,1,0:T(8,128)(2,1)S(1)}, u32[]{:S(2)}, u32[]{:S(2)}) collective-permute-start(bf16[2,2240,128]{2,1,0:T(8,128)(2,1)S(1)} %get-tuple-element.68), channel_id=1, source_target_pairs={{0,96},{4,28},{8,104},{12,4},{16,112},{20,12},{24,120},{28,20},{32... | collective-permute-start | bytes 3440648 | tf_op jit(solution)/shard_map/ppermute | solution.py:50
  153.4 22.9 %collective-permute-start.26 = (bf16[2,2240,128]{2,1,0:T(8,128)(2,1)S(1)}, bf16[2,2240,128]{2,1,0:T(8,128)(2,1)S(1)}, u32[]{:S(2)}, u32[]{:S(2)}) collective-permute-start(bf16[2,2240,128]{2,1,0:T(8,128)(2,1)S(1)} %get-tuple-element.66), channel_id=1, source_target_pairs={{0,32},{4,12},{8,40},{12,20},{16,48},{20,28},{24,56},{28,4},{32,64... | collective-permute-start | bytes 3440648 | tf_op jit(solution)/shard_map/ppermute | solution.py:50
  153.5 22.8 %collective-permute-start.29 = (bf16[2,2240,128]{2,1,0:T(8,128)(2,1)S(1)}, bf16[2,2240,128]{2,1,0:T(8,128)(2,1)S(1)}, u32[]{:S(2)}, u32[]{:S(2)}) collective-permute-start(bf16[2,2240,128]{2,1,0:T(8,128)(2,1)S(1)} %get-tuple-element.69), channel_id=1, source_target_pairs={{0,96},{4,28},{8,104},{12,4},{16,112},{20,12},{24,120},{28,20},{32... | collective-permute-start | bytes 3440648 | tf_op jit(solution)/shard_map/ppermute | solution.py:50
  183.1 14.9 %collective-permute-start.34 = (bf16[1216,128]{1,0:T(8,128)(2,1)S(1)}, bf16[1216,128]{1,0:T(8,128)(2,1)S(1)}, u32[]{:S(2)}, u32[]{:S(2)}) collective-permute-start(bf16[1216,128]{1,0:T(8,128)(2,1)S(1)} %get-tuple-element.77), channel_id=1, source_target_pairs={{0,24},{4,100},{8,0},{12,108},{16,8},{20,116},{24,16},{28,124},{32... | collective-permute-start | bytes 933896 | tf_op jit(solution)/shard_map/ppermute | solution.py:50
  187.8 10.1 %collective-permute-start.32 = (bf16[1216,128]{1,0:T(8,128)(2,1)S(1)}, bf16[1216,128]{1,0:T(8,128)(2,1)S(1)}, u32[]{:S(2)}, u32[]{:S(2)}) collective-permute-start(bf16[1216,128]{1,0:T(8,128)(2,1)S(1)} %get-tuple-element.75), channel_id=1, source_target_pairs={{0,8},{4,36},{8,16},{12,44},{16,24},{20,52},{24,0},{28,60},{32,40}... | collective-permute-start | bytes 933896 | tf_op jit(solution)/shard_map/ppermute | solution.py:50
  188.3 9.6 %collective-permute-start.33 = (bf16[1024,128]{1,0:T(8,128)(2,1)S(1)}, bf16[1024,128]{1,0:T(8,128)(2,1)S(1)}, u32[]{:S(2)}, u32[]{:S(2)}) collective-permute-start(bf16[1024,128]{1,0:T(8,128)(2,1)S(1)} %get-tuple-element.76), channel_id=1, source_target_pairs={{0,8},{4,36},{8,16},{12,44},{16,24},{20,52},{24,0},{28,60},{32,40}... | collective-permute-start | bytes 786440 | tf_op jit(solution)/shard_map/ppermute | solution.py:50
  189.7 8.3 %collective-permute-start.35 = (bf16[1024,128]{1,0:T(8,128)(2,1)S(1)}, bf16[1024,128]{1,0:T(8,128)(2,1)S(1)}, u32[]{:S(2)}, u32[]{:S(2)}) collective-permute-start(bf16[1024,128]{1,0:T(8,128)(2,1)S(1)} %get-tuple-element.78), channel_id=1, source_target_pairs={{0,24},{4,100},{8,0},{12,108},{16,8},{20,116},{24,16},{28,124},{32... | collective-permute-start | bytes 786440 | tf_op jit(solution)/shard_map/ppermute | solution.py:50
  (36 other events, 226.3 us)
Sparse Core Ops, SparseCore 0:
  9.7 86.3 all-gather.1
  109.8 80.3 reduce-scatter.1
